TPU v7x, 512 devices: a whole 4x8x8 slice. The times are simulated.
512 devices in a mesh: rows: 128 (over y, z, core), grp: 4 (over x).
Axes of the slice: x: 4, y: 8, z: 8, core: 2. Of those that a mesh axis runs over, the one named last changes fastest.
Arguments:
- tiles: float32 [24576, 128, 128], P(('rows', 'grp')), may hold values from 0 to 24
- coords: int32 [24576, 2], P(('rows', 'grp')), may hold values from 0 to 2047, as said below
- live: int32 [512], P(('rows', 'grp')), may hold values from 6 to 48, as said below
- sketch: float32 [262144, 64], P(('rows', 'grp')), may hold values from -6 to 6
Outputs:
- basis: float32 [262144, 64], P(('rows', 'grp'))
Inputs may be any that keep to these rules, and one draw needn't show every extreme that they name: `coords`: slot s of device d (slot d * 48 + s) has the row tile d * 4 + s and the column tile equal to it for s < 4; every other slot of device d has a row tile from d * 4 to d * 4 + 3, and a column tile in row block b - 1, b or b + 1 (modulo 128), where b = d // 4 and row block b is the tiles b * 16 to b * 16 + 15; slot 4 has its column tile in row block b - 1 and slot 5 in row block b + 1. The same coordinate pair may repeat. `live`: every device uses its slots 4 and 5; some device uses all 48.
All inputs are finite; a program needn't handle non-finite values.
Results may differ from a plain program's by a relative error of at most 0.0003.
Values sent between devices are 32-bit elements; how exact they have to be, the bound alone decides.
No kernel may reach another device: no remote copies, remote signals or barrier semaphores. Data moves between devices by JAX's collectives and lax.ppermute only.
A program may use at most 64 MiB of HBM per device.

v0:
```python
import functools

import jax
import jax.numpy as jnp
from jax import lax
from jax.sharding import Mesh
from jax.sharding import PartitionSpec as P

ROWS = ("rows_0", "rows_1", "rows_2")
ROWS_GRP = ("rows_0", "rows_1", "rows_2", "grp")


HIGHEST = lax.Precision.HIGHEST


def from_behind(array, axis, by):
    peers = lax.axis_size(axis)
    return lax.ppermute(array, axis, [(i, (i + by) % peers) for i in range(peers)])


def in_blocks(array, dim, peers):
    before, after = (array.shape[:dim], array.shape[dim + 1 :])
    return jnp.moveaxis(array.reshape(*before, peers, -1, *after), dim, 0)


def sum_at_owner(array, axis, dim):
    parts = in_blocks(array, dim, lax.axis_size(axis))
    arrived = lax.all_to_all(parts, axis, split_axis=0, concat_axis=0, tiled=True)
    return arrived.sum(axis=0)


def laid_out(parts, dim):
    dims = list(parts.shape[1:])
    dims[dim] *= parts.shape[0]
    return jnp.moveaxis(parts, 0, dim).reshape(dims)


def from_everyone(array, axis):
    copies = jnp.broadcast_to(array, (lax.axis_size(axis), *array.shape))
    return lax.all_to_all(copies, axis, split_axis=0, concat_axis=0, tiled=True)


def gathered_copies(array, axis, dim):
    return laid_out(from_everyone(array, axis), dim)


def padded(cells, sides, width):
    for axis, dim in sides:
        count = lax.axis_size(axis)
        head = lax.slice_in_dim(cells, 0, width, axis=dim)
        tail = lax.slice_in_dim(cells, cells.shape[dim] - width, cells.shape[dim], axis=dim)
        cells = jnp.concatenate(
            [
                lax.ppermute(tail, axis, [(i, (i + 1) % count) for i in range(count)]),
                cells,
                lax.ppermute(head, axis, [((i + 1) % count, i) for i in range(count)]),
            ],
            axis=dim,
        )
    return cells


def by_axis(array, axes):
    return functools.reduce(lax.psum, axes, array)


def product_sweep(tile_slab, live_count, source, source_pos, target_pos, targets, transpose):
    target_ids = jnp.arange(targets, dtype=jnp.int32)
    lane_ids = jnp.arange(8, dtype=jnp.int32)
    initial = jnp.zeros((targets, source.shape[1], source.shape[2]), jnp.float32)
    pattern = "sji,sjk->sik" if transpose else "sij,sjk->sik"

    def advance(number, summed):
        offset = number * 8
        stacked = lax.dynamic_slice_in_dim(tile_slab, offset, 8, 0)
        fetched = lax.dynamic_slice_in_dim(source_pos, offset, 8, 0)
        placed = lax.dynamic_slice_in_dim(target_pos, offset, 8, 0)
        product = jnp.einsum(pattern, stacked, source[fetched], precision=HIGHEST)
        active = offset + lane_ids < live_count
        selector = ((placed[None, :] == target_ids[:, None]) & active[None, :]).astype(jnp.float32)
        return summed + jnp.einsum("ns,sik->nik", selector, product, precision=HIGHEST)

    return lax.fori_loop(0, (live_count + 7) // 8, advance, initial)


def local(tiles, coords, live, sketch):
    groups = lax.axis_size("grp")
    cycle_size = lax.axis_size(ROWS)
    row_index = lax.axis_index(ROWS)
    grp_index = lax.axis_index("grp")
    tile_edge = tiles.shape[1]
    columns = sketch.shape[1]
    per_device = sketch.shape[0] // tile_edge
    block_tiles = groups * per_device
    block_base = row_index * block_tiles
    own_base = block_base + grp_index * per_device
    row_pos = coords[:, 0] - own_base
    live_count = live[0]
    col_tiles = coords[:, 1]
    span_pos = (
        col_tiles // block_tiles - row_index + 1 + cycle_size
    ) % cycle_size * block_tiles + col_tiles % block_tiles
    panel = sketch
    for sweep in range(2):
        panel_rows = panel
        source = panel_rows.reshape(-1, tile_edge, columns)
        spread = product_sweep(tiles, live_count, source, row_pos, span_pos, 3 * block_tiles, True)
        spread = spread.reshape(3, block_tiles * tile_edge, columns)
        from_next = from_behind(spread[0], ROWS, -1)
        from_prior = from_behind(spread[2], ROWS, 1)
        summed = spread[1] + from_next + from_prior
        middle_rows = sum_at_owner(summed, "grp", 0)
        whole = gathered_copies(middle_rows, "grp", 0)
        widened = padded(whole, ((ROWS, 0),), whole.shape[0])
        source = widened.reshape(-1, tile_edge, columns)
        image = product_sweep(tiles, live_count, source, span_pos, row_pos, per_device, False)
        image = image.reshape(-1, columns)
        gram = by_axis(
            jnp.dot(image.T, image, precision=HIGHEST, preferred_element_type=jnp.float32), ROWS_GRP
        )
        lower = jnp.linalg.cholesky(gram)
        panel = jax.scipy.linalg.solve_triangular(lower, image.T, lower=True).T
    total_rows = cycle_size * groups * sketch.shape[0]
    return panel * total_rows**0.5


def solution(mesh):
    finer = Mesh(
        mesh.devices.reshape(8, 8, 2, mesh.shape["grp"]), ("rows_0", "rows_1", "rows_2", "grp")
    )
    placed = (P(ROWS_GRP, None, None), P(ROWS_GRP, None), P(ROWS_GRP), P(ROWS_GRP, None))
    return jax.shard_map(
        local, mesh=finer, in_specs=placed, out_specs=P(ROWS_GRP, None), check_vma=False
    )
```

profile of v0, /device:TPU:2, one launch (start us, length us, event | category | flops | bytes accessed | tf_op | source)
XLA Modules:
  0.0 407.4 jit_solution(16212562076796353935)
XLA Ops:
  3.2 9.6 %while.44 = (s32[]{:T(128)}, f32[48,128,64]{1,0,2:T(8,128)S(1)}, s32[]{:T(128)}, s32[48]{0:T(128)S(1)}, s32[]{:T(128)}, /*index=5*/f32[48,128,128]{2,1,0:T(8,128...) while((s32[]{:T(128)}, f32[48,128,64]{1,0,2:T(8,128)S(1)}, ...), condition=%wide.region_1.2_spmd.clone, body=%wide.region_0.1_spmd.clone.sunk | while | flops 138807088 | bytes 4985255 | solution.py:83
  3.9 2.0 fusion.108
  8.7 2.1 fusion.108
  13.2 13.3 %collective-permute-start = (f32[2048,64]{0,1:T(8,128)S(1)}, f32[2048,64]{0,1:T(8,128)S(1)}, u32[]{:S(2)}, u32[]{:S(2)}) collective-permute-start(f32[2048,64]{0,1:T(8,128)S(1)} %bitcast.171), channel_id=1, source_target_pairs={{0,508},{4,0},{8,4},{12,8},{16,12},{20,16},{24,20},{28,24},{32,28}... | collective-permute-start | bytes 1572872 | tf_op jit(solution)/shard_map/ppermute | solution.py:18
  26.7 1.9 collective-permute-start.1
  28.6 4.6 %collective-permute-done = f32[2048,64]{0,1:T(8,128)S(1)} collective-permute-done((f32[2048,64]{0,1:T(8,128)S(1)}, f32[2048,64]{0,1:T(8,128)S(1)}, u32[]{:S(2)}, u32[]{:S(2)}) %collective-permute-start) | collective-permute-done | bytes 524320 | tf_op jit(solution)/shard_map/ppermute | solution.py:18
  33.2 17.4 %collective-permute-done.1 = f32[2048,64]{0,1:T(8,128)S(1)} collective-permute-done((f32[2048,64]{0,1:T(8,128)S(1)}, f32[2048,64]{0,1:T(8,128)S(1)}, u32[]{:S(2)}, u32[]{:S(2)}) %collective-permute-start.1) | collective-permute-done | bytes 524320 | tf_op jit(solution)/shard_map/ppermute | solution.py:18
  50.8 9.7 %all_to_all.22 = f32[4,512,64]{1,2,0:T(8,128)S(1)} all-to-all(f32[4,512,64]{1,2,0:T(8,128)S(1)} %bitcast.153), channel_id=1, replica_groups=mesh['rows_0'=8,'rows_1'=8,'rows_2'=2,'grp'=4] {'grp'}, dimensions={0} | all-to-all | bytes 1048576 | tf_op jit(solution)/shard_map/all_to_all | solution.py:28
  60.7 10.5 %all_to_all.20 = f32[4,512,64]{1,2,0:T(8,128)S(1)} all-to-all(f32[4,512,64]{1,2,0:T(8,128)S(1)} %broadcast_in_dim.21), channel_id=1, replica_groups=mesh['rows_0'=8,'rows_1'=8,'rows_2'=2,'grp'=4] {'grp'}, dimensions={0} | all-to-all | bytes 1048576 | tf_op jit(solution)/shard_map/all_to_all | solution.py:40
  71.2 1.9 collective-permute-start.2
  73.1 7.0 %collective-permute-start.3 = (f32[2048,64]{0,1:T(8,128)S(1)}, f32[2048,64]{0,1:T(8,128)S(1)}, u32[]{:S(2)}, u32[]{:S(2)}) collective-permute-start(f32[2048,64]{0,1:T(8,128)S(1)} %bitcast.158), channel_id=1, source_target_pairs={{4,0},{8,4},{12,8},{16,12},{20,16},{24,20},{28,24},{32,28},{36,32}... | collective-permute-start | bytes 1572872 | tf_op jit(solution)/shard_map/ppermute | solution.py:56
  80.1 4.9 %collective-permute-done.2 = f32[2048,64]{0,1:T(8,128)S(1)} collective-permute-done((f32[2048,64]{0,1:T(8,128)S(1)}, f32[2048,64]{0,1:T(8,128)S(1)}, u32[]{:S(2)}, u32[]{:S(2)}) %collective-permute-start.2) | collective-permute-done | bytes 524320 | tf_op jit(solution)/shard_map/ppermute | solution.py:54
  86.9 2.3 copy.61
  89.2 11.9 %while.45 = (s32[]{:T(128)}, f32[4,128,64]{1,0,2:T(4,128)S(1)}, s32[]{:T(128)}, s32[48]{0:T(128)S(1)}, s32[]{:T(128)}, /*index=5*/f32[48,128,128]{2,1,0:T(8,128)...) while((s32[]{:T(128)}, f32[4,128,64]{1,0,2:T(4,128)S(1)}, ...), condition=%wide.region_4.5_spmd.clone, body=%wide.region_3.4_spmd.clone.sunk | while | flops 103842928 | bytes 2101671 | solution.py:83
  89.3 2.5 gather_fusion.1
  91.7 2.1 fusion.114
  95.2 2.5 gather_fusion.1
  97.7 2.1 fusion.114
  101.4 52.1 %psum.56 = f32[64,64]{0,1:T(8,128)S(1)} all-reduce(f32[64,64]{0,1:T(8,128)S(1)} %convolution_bitcast_fusion.2), channel_id=1, replica_groups=mesh['rows_0'=8,'rows_1'=8,'rows_2'=2,'grp'=4] {'rows_0'}, use_global_device_ids=true, to_apply=%region_5.6 | all-reduce | flops 4096 | bytes 32768 | tf_op jit(solution)/shard_map/psum | solution.py:64
  153.4 27.1 %psum.57 = f32[64,64]{0,1:T(8,128)S(1)} all-reduce(f32[64,64]{0,1:T(8,128)S(1)} %psum.56), channel_id=1, replica_groups=mesh['rows_0'=8,'rows_1'=8,'rows_2'=2,'grp'=4] {'rows_1'}, use_global_device_ids=true, to_apply=%region_6.7 | all-reduce | flops 4096 | bytes 32768 | tf_op jit(solution)/shard_map/psum | solution.py:64
  180.5 3.4 psum.58
  183.9 14.6 %psum.59 = f32[64,64]{0,1:T(8,128)S(1)} all-reduce(f32[64,64]{0,1:T(8,128)S(1)} %psum.58), channel_id=1, replica_groups=mesh['rows_0'=8,'rows_1'=8,'rows_2'=2,'grp'=4] {'grp'}, use_global_device_ids=true, to_apply=%region_8.9 | all-reduce | flops 4096 | bytes 32768 | tf_op jit(solution)/shard_map/psum | solution.py:64
  198.6 5.8 %cholesky.44 = f32[64,64]{1,0:T(8,128)S(1)} custom-call(f32[64,64]{1,0:T(8,128)S(1)} %fusion.68), custom_call_target="Cholesky" | custom-call | tf_op jit(solution)/shard_map/jit(cholesky)/cholesky | solution.py:121
  205.9 4.9 %custom-call.6 = f32[1,64,64]{1,2,0:T(8,128)S(1)} custom-call(f32[1,64,64]{2,1,0:T(8,128)S(1)} %fusion.63), custom_call_target="InvertDiagBlocksLowerTriangular" | custom-call | tf_op jit(solution)/shard_map/jit(_solve_triangular)/triangular_solve | solution.py:122
  211.4 9.6 %while.46 = (s32[]{:T(128)}, f32[48,128,64]{1,0,2:T(8,128)S(1)}, s32[]{:T(128)}, s32[48]{0:T(128)S(1)}, s32[]{:T(128)}, /*index=5*/f32[48,128,128]{2,1,0:T(8,128...) while((s32[]{:T(128)}, f32[48,128,64]{1,0,2:T(8,128)S(1)}, ...), condition=%wide.region_12.15_spmd.clone, body=%wide.region_11.14_spmd.clone.sunk | while | flops 138807088 | bytes 4985255 | solution.py:83
  212.1 2.0 fusion.120
  216.9 2.0 fusion.120
  221.3 1.9 collective-permute-start.4
  223.4 2.6 collective-permute-start.5
  226.0 3.9 collective-permute-done.4
  229.9 17.5 %collective-permute-done.5 = f32[2048,64]{0,1:T(8,128)S(1)} collective-permute-done((f32[2048,64]{0,1:T(8,128)S(1)}, f32[2048,64]{0,1:T(8,128)S(1)}, u32[]{:S(2)}, u32[]{:S(2)}) %collective-permute-start.5) | collective-permute-done | bytes 524320 | tf_op jit(solution)/shard_map/ppermute | solution.py:18
  247.7 10.2 %all_to_all.23 = f32[4,512,64]{1,2,0:T(8,128)S(1)} all-to-all(f32[4,512,64]{1,2,0:T(8,128)S(1)} %bitcast.155), channel_id=1, replica_groups=mesh['rows_0'=8,'rows_1'=8,'rows_2'=2,'grp'=4] {'grp'}, dimensions={0} | all-to-all | bytes 1048576 | tf_op jit(solution)/shard_map/all_to_all | solution.py:28
  258.1 10.5 %all_to_all.21 = f32[4,512,64]{1,2,0:T(8,128)S(1)} all-to-all(f32[4,512,64]{1,2,0:T(8,128)S(1)} %broadcast_in_dim.22), channel_id=1, replica_groups=mesh['rows_0'=8,'rows_1'=8,'rows_2'=2,'grp'=4] {'grp'}, dimensions={0} | all-to-all | bytes 1048576 | tf_op jit(solution)/shard_map/all_to_all | solution.py:40
  268.6 1.9 collective-permute-start.6
  270.5 7.0 %collective-permute-start.7 = (f32[2048,64]{0,1:T(8,128)S(1)}, f32[2048,64]{0,1:T(8,128)S(1)}, u32[]{:S(2)}, u32[]{:S(2)}) collective-permute-start(f32[2048,64]{0,1:T(8,128)S(1)} %bitcast.161), channel_id=1, source_target_pairs={{4,0},{8,4},{12,8},{16,12},{20,16},{24,20},{28,24},{32,28},{36,32}... | collective-permute-start | bytes 1572872 | tf_op jit(solution)/shard_map/ppermute | solution.py:56
  277.5 4.9 %collective-permute-done.6 = f32[2048,64]{0,1:T(8,128)S(1)} collective-permute-done((f32[2048,64]{0,1:T(8,128)S(1)}, f32[2048,64]{0,1:T(8,128)S(1)}, u32[]{:S(2)}, u32[]{:S(2)}) %collective-permute-start.6) | collective-permute-done | bytes 524320 | tf_op jit(solution)/shard_map/ppermute | solution.py:54
  284.3 2.3 copy.64
  286.6 11.9 %while.47 = (s32[]{:T(128)}, f32[4,128,64]{1,0,2:T(4,128)S(1)}, s32[]{:T(128)}, s32[48]{0:T(128)S(1)}, s32[]{:T(128)}, /*index=5*/f32[48,128,128]{2,1,0:T(8,128)...) while((s32[]{:T(128)}, f32[4,128,64]{1,0,2:T(4,128)S(1)}, ...), condition=%wide.region_15.18_spmd.clone, body=%wide.region_14.17_spmd.clone.sunk | while | flops 103842928 | bytes 2101671 | solution.py:83
  286.7 2.5 gather_fusion.3
  289.1 2.1 fusion.126
  292.6 2.5 gather_fusion.3
  295.1 2.1 fusion.126
  298.8 50.4 %psum.60 = f32[64,64]{0,1:T(8,128)S(1)} all-reduce(f32[64,64]{0,1:T(8,128)S(1)} %convolution_bitcast_fusion.1), channel_id=1, replica_groups=mesh['rows_0'=8,'rows_1'=8,'rows_2'=2,'grp'=4] {'rows_0'}, use_global_device_ids=true, to_apply=%region_16.19 | all-reduce | flops 4096 | bytes 32768 | tf_op jit(solution)/shard_map/psum | solution.py:64
  349.2 27.1 %psum.61 = f32[64,64]{0,1:T(8,128)S(1)} all-reduce(f32[64,64]{0,1:T(8,128)S(1)} %psum.60), channel_id=1, replica_groups=mesh['rows_0'=8,'rows_1'=8,'rows_2'=2,'grp'=4] {'rows_1'}, use_global_device_ids=true, to_apply=%region_17.20 | all-reduce | flops 4096 | bytes 32768 | tf_op jit(solution)/shard_map/psum | solution.py:64
  376.3 3.4 psum.62
  379.7 14.6 %psum.63 = f32[64,64]{0,1:T(8,128)S(1)} all-reduce(f32[64,64]{0,1:T(8,128)S(1)} %psum.62), channel_id=1, replica_groups=mesh['rows_0'=8,'rows_1'=8,'rows_2'=2,'grp'=4] {'grp'}, use_global_device_ids=true, to_apply=%region_19.22 | all-reduce | flops 4096 | bytes 32768 | tf_op jit(solution)/shard_map/psum | solution.py:64
  394.3 5.8 %cholesky.55 = f32[64,64]{1,0:T(8,128)S(1)} custom-call(f32[64,64]{1,0:T(8,128)S(1)} %fusion.66), custom_call_target="Cholesky" | custom-call | tf_op jit(solution)/shard_map/jit(cholesky)/cholesky | solution.py:121
  401.5 4.9 %custom-call.7 = f32[1,64,64]{1,2,0:T(8,128)S(1)} custom-call(f32[1,64,64]{2,1,0:T(8,128)S(1)} %fusion.64), custom_call_target="InvertDiagBlocksLowerTriangular" | custom-call | tf_op jit(solution)/shard_map/jit(_solve_triangular)/triangular_solve | solution.py:122
  (86 shorter events, 29.1 us)
Async XLA Ops:
  13.2 20.0 %collective-permute-start = (f32[2048,64]{0,1:T(8,128)S(1)}, f32[2048,64]{0,1:T(8,128)S(1)}, u32[]{:S(2)}, u32[]{:S(2)}) collective-permute-start(f32[2048,64]{0,1:T(8,128)S(1)} %bitcast.171), channel_id=1, source_target_pairs={{0,508},{4,0},{8,4},{12,8},{16,12},{20,16},{24,20},{28,24},{32,28}... | collective-permute-start | bytes 1572872 | tf_op jit(solution)/shard_map/ppermute | solution.py:18
  26.7 23.9 %collective-permute-start.1 = (f32[2048,64]{0,1:T(8,128)S(1)}, f32[2048,64]{0,1:T(8,128)S(1)}, u32[]{:S(2)}, u32[]{:S(2)}) collective-permute-start(f32[2048,64]{0,1:T(8,128)S(1)} %bitcast.173), channel_id=1, source_target_pairs={{0,4},{4,8},{8,12},{12,16},{16,20},{20,24},{24,28},{28,32},{32,36}... | collective-permute-start | bytes 1572872 | tf_op jit(solution)/shard_map/ppermute | solution.py:18
  71.2 13.8 %collective-permute-start.2 = (f32[2048,64]{0,1:T(8,128)S(1)}, f32[2048,64]{0,1:T(8,128)S(1)}, u32[]{:S(2)}, u32[]{:S(2)}) collective-permute-start(f32[2048,64]{0,1:T(8,128)S(1)} %bitcast.157), channel_id=1, source_target_pairs={{0,4},{4,8},{8,12},{12,16},{16,20},{20,24},{24,28},{28,32},{32,36}... | collective-permute-start | bytes 1572872 | tf_op jit(solution)/shard_map/ppermute | solution.py:54
  73.1 13.6 %collective-permute-start.3 = (f32[2048,64]{0,1:T(8,128)S(1)}, f32[2048,64]{0,1:T(8,128)S(1)}, u32[]{:S(2)}, u32[]{:S(2)}) collective-permute-start(f32[2048,64]{0,1:T(8,128)S(1)} %bitcast.158), channel_id=1, source_target_pairs={{4,0},{8,4},{12,8},{16,12},{20,16},{24,20},{28,24},{32,28},{36,32}... | collective-permute-start | bytes 1572872 | tf_op jit(solution)/shard_map/ppermute | solution.py:56
  221.3 8.6 %collective-permute-start.4 = (f32[2048,64]{0,1:T(8,128)S(1)}, f32[2048,64]{0,1:T(8,128)S(1)}, u32[]{:S(2)}, u32[]{:S(2)}) collective-permute-start(f32[2048,64]{0,1:T(8,128)S(1)} %bitcast.172), channel_id=1, source_target_pairs={{0,508},{4,0},{8,4},{12,8},{16,12},{20,16},{24,20},{28,24},{32,28}... | collective-permute-start | bytes 1572872 | tf_op jit(solution)/shard_map/ppermute | solution.py:18
  223.4 24.0 %collective-permute-start.5 = (f32[2048,64]{0,1:T(8,128)S(1)}, f32[2048,64]{0,1:T(8,128)S(1)}, u32[]{:S(2)}, u32[]{:S(2)}) collective-permute-start(f32[2048,64]{0,1:T(8,128)S(1)} %bitcast.174), channel_id=1, source_target_pairs={{0,4},{4,8},{8,12},{12,16},{16,20},{20,24},{24,28},{28,32},{32,36}... | collective-permute-start | bytes 1572872 | tf_op jit(solution)/shard_map/ppermute | solution.py:18
  268.6 13.8 %collective-permute-start.6 = (f32[2048,64]{0,1:T(8,128)S(1)}, f32[2048,64]{0,1:T(8,128)S(1)}, u32[]{:S(2)}, u32[]{:S(2)}) collective-permute-start(f32[2048,64]{0,1:T(8,128)S(1)} %bitcast.160), channel_id=1, source_target_pairs={{0,4},{4,8},{8,12},{12,16},{16,20},{20,24},{24,28},{28,32},{32,36}... | collective-permute-start | bytes 1572872 | tf_op jit(solution)/shard_map/ppermute | solution.py:54
  270.5 13.6 %collective-permute-start.7 = (f32[2048,64]{0,1:T(8,128)S(1)}, f32[2048,64]{0,1:T(8,128)S(1)}, u32[]{:S(2)}, u32[]{:S(2)}) collective-permute-start(f32[2048,64]{0,1:T(8,128)S(1)} %bitcast.161), channel_id=1, source_target_pairs={{4,0},{8,4},{12,8},{16,12},{20,16},{24,20},{28,24},{32,28},{36,32}... | collective-permute-start | bytes 1572872 | tf_op jit(solution)/shard_map/ppermute | solution.py:56
where the time goes:
time: 408 us; the launch traced here: 407 us
  blocking collectives  233 us (57%)
  waiting for transfers between devices  56.8 us (14%)
  starting transfers between devices  37.5 us (9%)
  other arithmetic  32.3 us (8%)
  matrix products  25.8 us (6%)
  local copies, waits for them, and re-layouts  20.1 us (5%)
    psum x8, blocking collectives, by_axis(): return functools.reduce(lax.psum, axes, array)  193 us
    ppermute x4, waiting for transfers between devices, from_behind(): lax.ppermute(array, axis, [(i, (i + by) % peers) for i in range(peers)])  43.4 us
    all_to_all x2, blocking collectives, from_everyone(): return lax.all_to_all(copies, axis, split_axis=0, concat_axis=0, tiled=True)  21 us
    all_to_all x2, blocking collectives, sum_at_owner(): lax.all_to_all(parts, axis, split_axis=0, concat_axis=0, tiled=True)  19.9 us
    ppermute x4, starting transfers between devices, from_behind(): lax.ppermute(array, axis, [(i, (i + by) % peers) for i in range(peers)])  19.7 us
    dot_general x8, matrix products, advance(): product = jnp.einsum(pattern, stacked, source[fetched], precision=HIGHEST)  16.7 us
    ppermute x2, starting transfers between devices, padded(): lax.ppermute(head, axis, [((i + 1) % count, i) for i in range(count)])  13.9 us
    another operation x6, other arithmetic, local(): lower = jnp.linalg.cholesky(gram)  13.1 us
  transfers between devices with their start and end apart: 8, of which 8 were waited for; matrix products, arithmetic and copies ran while one was open for 0% of the time, Pallas kernels for 0%

commit v1 on v0

v1 whole, which is shorter than its diff:
```python
import functools

import jax
import jax.numpy as jnp
from jax import lax
from jax.experimental import pallas as pl
from jax.experimental.pallas import tpu as pltpu
from jax.sharding import Mesh
from jax.sharding import PartitionSpec as P

ROWS = ("y", "z", "c")
ROWS_GRP = ("y", "z", "c", "grp")
HIGHEST = lax.Precision.HIGHEST
F32 = jnp.float32
BF16 = jnp.bfloat16
T = 128
CHUNK = 8


def dot(a, b, contract, precision=None):
    return lax.dot_general(
        a, b, ((contract[:1], contract[1:]), ((), ())), precision=precision, preferred_element_type=F32
    )


def halves(x):
    hi = x.astype(BF16)
    return hi, (x - hi.astype(F32)).astype(BF16)


def fold(q, k):
    return (q[:k, :T] + q[k:, T:]) + (q[k:, :T] + q[:k, T:])


def start_tiles(live, tiles, tbuf, sems, cap):
    for c in range(cap // CHUNK):
        at = pl.ds(c * CHUNK, CHUNK)

        @pl.when(c * CHUNK < live)
        def _():
            pltpu.make_async_copy(tiles.at[at], tbuf.at[at], sems.at[c]).start()


def each_chunk(live, tiles, tbuf, sems, cap, work, wait=True):
    for c in range(cap // CHUNK):
        at = pl.ds(c * CHUNK, CHUNK)

        @pl.when(c * CHUNK < live)
        def _():
            if wait:
                pltpu.make_async_copy(tiles.at[at], tbuf.at[at], sems.at[c]).wait()
            for s in range(c * CHUNK, (c + 1) * CHUNK):
                work(s)


def keep_panel(panel, k, phl):
    for t in range(phl.shape[0]):
        hi, lo = halves(panel(t))
        phl[t, :k, :] = hi
        phl[t, k:, :] = lo


def spread_slot(s, code, hi, lo, phl, acc):
    k = phl.shape[1] // 2
    entry = code[s]
    at = entry & 255
    q = dot(phl[entry >> 8], jnp.concatenate([hi, lo], axis=1), (1, 0))
    acc[at] += fold(q, k)


def put_spread(acc, outs):
    each = outs[0].shape[0]
    for n, out in enumerate(outs):
        out[...] = acc[n * each : (n + 1) * each]


def first_kernel(code, live, tiles, sketch, outer, own, partner, tbuf, phl, acc, sems):
    cap = tiles.shape[0]
    k = sketch.shape[1]
    start_tiles(live[0], tiles, tbuf, sems, cap)
    acc[...] = jnp.zeros_like(acc)
    keep_panel(lambda t: sketch[t * T : (t + 1) * T, :].T, k, phl)

    def work(s):
        hi, lo = halves(tbuf[s])
        spread_slot(s, code, hi, lo, phl, acc)

    each_chunk(live[0], tiles, tbuf, sems, cap, work)
    put_spread(acc, (outer, own, partner))


def keep_spread(parts, shl):
    k = parts[0].shape[1]
    each = parts[0].shape[0]
    for n, part in enumerate(parts):

        def one(i, carry, part=part, n=n):
            hi, lo = halves(part[i])
            shl[n * each + i, :k, :] = hi
            shl[n * each + i, k:, :] = lo
            return carry

        lax.fori_loop(0, each, one, 0, unroll=4)
    shl[3 * each] = jnp.zeros_like(shl[3 * each])


def image_slot(s, code, hi, lo, shl, img):
    k = shl.shape[1] // 2
    entry = code[s]
    q = dot(shl[entry & 255], jnp.concatenate([hi, lo], axis=0), (1, 1))
    img[entry >> 8] += fold(q, k)


def whole_image(img):
    return jnp.concatenate([img[t] for t in range(img.shape[0])], axis=1)


def put_gram(image, out):
    g = dot(image, image, (1, 1), HIGHEST)
    half = g.shape[0] // 2
    out[...] = jnp.concatenate([g[:half], g[half:]], axis=1)


def middle_kernel(
    code, live, tiles, s_outer, s_own, s_partner, outer, own, partner, gram,
    tbuf, thl, shl, img, phl, acc, sems,
):
    cap = tiles.shape[0]
    k = s_own.shape[1]
    start_tiles(live[0], tiles, tbuf, sems, cap)
    keep_spread((s_outer, s_own, s_partner), shl)
    img[...] = jnp.zeros_like(img)
    acc[...] = jnp.zeros_like(acc)

    def forth(s):
        hi, lo = halves(tbuf[s])
        thl[s, :T, :] = hi
        thl[s, T:, :] = lo
        image_slot(s, code, hi, lo, shl, img)

    each_chunk(live[0], tiles, tbuf, sems, cap, forth)
    put_gram(whole_image(img), gram)
    keep_panel(lambda t: img[t], k, phl)

    def back(s):
        spread_slot(s, code, thl[s, :T, :], thl[s, T:, :], phl, acc)

    each_chunk(live[0], tiles, tbuf, sems, cap, back, wait=False)
    put_spread(acc, (outer, own, partner))


def inverse_factor(g):
    k = g.shape[0]
    row_id = lax.broadcasted_iota(jnp.int32, (8, 2 * k), 0)
    eye = (lax.broadcasted_iota(jnp.int32, (k, k), 0) == lax.broadcasted_iota(jnp.int32, (k, k), 1)).astype(F32)
    full = jnp.concatenate([g, eye], axis=1)
    m = [full[8 * j : 8 * j + 8] for j in range(k // 8)]

    def row_of(x, r):
        return jnp.broadcast_to(x[r : r + 1, :], x.shape)

    for j in range(k // 8):
        rows = [row_of(m[j], t) for t in range(8)]
        cols = [
            {i: jnp.broadcast_to(m[i][:, 8 * j + t : 8 * j + t + 1], (8, 2 * k)) for i in range(j, k // 8)}
            for t in range(8)
        ]
        scale = jnp.zeros((8, 2 * k), F32)
        for t in range(8):
            pivot = row_of(cols[t][j], t)
            scale = jnp.where(row_id == t, lax.rsqrt(pivot), scale)
            inv = 1.0 / pivot
            q = rows[t] * inv
            cols[t][j] = jnp.where(row_id > t, cols[t][j], 0.0)
            for u in range(t + 1, 8):
                part = row_of(cols[t][j], u)
                f = part * inv
                rows[u] = rows[u] - part * q
                for i in range(j, k // 8):
                    cols[u][i] = cols[u][i] - cols[t][i] * f
            for i in range(j, k // 8):
                m[i] = m[i] - cols[t][i] * q
        m[j] = m[j] * scale
    return jnp.concatenate([x[:, k:] for x in m], axis=0)


def summed_gram(parts):
    g = parts[0]
    for n in range(1, parts.shape[0]):
        g = g + parts[n]
    half = g.shape[1] // 2
    return jnp.concatenate([g[:, :half], g[:, half:]], axis=0)


def factor_kernel(parts, linv):
    linv[...] = inverse_factor(summed_gram(parts))


def last_kernel(code, live, tiles, s_outer, s_own, s_partner, linv, image, gram, tbuf, shl, img, sems):
    cap = tiles.shape[0]
    start_tiles(live[0], tiles, tbuf, sems, cap)
    keep_spread((s_outer, s_own, s_partner), shl)
    img[...] = jnp.zeros_like(img)

    def forth(s):
        hi, lo = halves(tbuf[s])
        image_slot(s, code, hi, lo, shl, img)

    each_chunk(live[0], tiles, tbuf, sems, cap, forth)
    x = dot(linv[...], whole_image(img), (1, 0), HIGHEST)
    image[...] = x
    put_gram(x, gram)


def basis_kernel(parts, image, basis, *, scale):
    linv = inverse_factor(summed_gram(parts))
    basis[...] = dot(linv, image[...], (1, 0), HIGHEST).T * scale


def to_everyone(x, axes):
    peers = lax.axis_size(axes)
    copies = jnp.broadcast_to(x, (peers, *x.shape))
    return lax.all_to_all(copies, axes, split_axis=0, concat_axis=0, tiled=True)


VMEM = pl.BlockSpec(memory_space=pltpu.VMEM)
ANY = pl.BlockSpec(memory_space=pl.ANY)


def local(tiles, coords, live, sketch):
    rows = lax.axis_size(ROWS)
    groups = lax.axis_size("grp")
    cap = tiles.shape[0]
    k = sketch.shape[1]
    mine = sketch.shape[0] // T
    block = groups * mine
    row = lax.axis_index(ROWS)
    odd = lax.axis_index("c")

    step = (coords[:, 1] // block - row + 1 + rows) % rows
    step = jnp.where(odd == 1, 2 - step, step)
    place = step * block + coords[:, 1] % block
    place = jnp.where(jnp.arange(cap, dtype=jnp.int32) < live[0], place, 3 * block)
    code = place + 256 * (coords[:, 0] % mine)

    outer = [(r, (r - 1) % rows if r % 2 == 0 else (r + 1) % rows) for r in range(rows)]
    partner = [(r, r ^ 1) for r in range(rows)]

    block_shape = jax.ShapeDtypeStruct((block, k, T), F32)
    gram_shape = jax.ShapeDtypeStruct((k // 2, 2 * k), F32)
    square = jax.ShapeDtypeStruct((k, k), F32)
    tbuf = pltpu.VMEM((cap, T, T), F32)
    thl = pltpu.VMEM((cap, 2 * T, T), BF16)
    phl = pltpu.VMEM((mine, 2 * k, T), BF16)
    shl = pltpu.VMEM((3 * block + 1, 2 * k, T), BF16)
    acc = pltpu.VMEM((3 * block + 1, k, T), F32)
    img = pltpu.VMEM((mine, k, T), F32)
    sems = pltpu.SemaphoreType.DMA((cap // CHUNK,))

    def call(kernel, ins, outs, scratch, prefetch=0, name=None):
        return pl.pallas_call(
            kernel,
            grid_spec=pltpu.PrefetchScalarGridSpec(
                num_scalar_prefetch=prefetch, grid=(), in_specs=ins, out_specs=[VMEM] * len(outs), scratch_shapes=scratch
            ),
            out_shape=outs,
            name=name,
            compiler_params=pltpu.CompilerParams(vmem_limit_bytes=48 * 1024 * 1024),
        )

    def exchange(parts, extra=None):
        p_outer, p_own, p_partner = parts
        got_outer = lax.ppermute(p_outer, ROWS, outer)
        got_partner = lax.ppermute(p_partner, ROWS, partner)
        total = p_own + got_outer + got_partner
        pieces = total.reshape(groups, mine, k, T)
        arrived = lax.all_to_all(pieces, "grp", split_axis=0, concat_axis=0, tiled=True)
        whole = to_everyone(arrived.sum(axis=0), "grp").reshape(block, k, T)
        return lax.ppermute(whole, ROWS, outer), whole, lax.ppermute(whole, ROWS, partner)

    def gram_parts(gram):
        gram = to_everyone(gram, ("c", "grp")).sum(axis=0)
        gram = to_everyone(gram, "z").sum(axis=0)
        return to_everyone(gram, "y")

    parts = call(first_kernel, [ANY, VMEM], [block_shape] * 3, [tbuf, phl, acc, sems], 2, "first")(
        code, live, tiles, sketch
    )
    whole = exchange(parts)
    *parts, gram = call(
        middle_kernel, [ANY] + [VMEM] * 3, [block_shape] * 3 + [gram_shape], [tbuf, thl, shl, img, phl, acc, sems], 2, "middle"
    )(code, live, tiles, *whole)
    linv = call(factor_kernel, [VMEM], [square], [], 0, "factor")(gram_parts(gram))[0]
    whole = exchange(parts)
    image, gram = call(
        last_kernel, [ANY] + [VMEM] * 4, [jax.ShapeDtypeStruct((k, mine * T), F32), gram_shape], [tbuf, shl, img, sems], 2, "last"
    )(code, live, tiles, *whole, linv)
    scale = float(rows * groups * sketch.shape[0]) ** 0.5
    return call(
        functools.partial(basis_kernel, scale=scale), [VMEM] * 2, [jax.ShapeDtypeStruct(sketch.shape, F32)], [], 0, "basis"
    )(gram_parts(gram), image)[0]


def solution(mesh):
    finer = Mesh(mesh.devices.reshape(8, 8, 2, mesh.shape["grp"]), ROWS_GRP)
    placed = (P(ROWS_GRP, None, None), P(ROWS_GRP, None), P(ROWS_GRP), P(ROWS_GRP, None))
    return jax.shard_map(local, mesh=finer, in_specs=placed, out_specs=P(ROWS_GRP, None), check_vma=False)
```

time: 408 us -> 190 us (0.47)
  blocking collectives: 233 us -> 105 us
  waiting for transfers between devices: 56.8 us -> 16.7 us
  other arithmetic: 32.3 us -> 2.14 us
  matrix products: 25.8 us -> 0 us
  local copies, waits for them, and re-layouts: 20.1 us -> 5.54 us
  Pallas kernels: 0 us -> 12.3 us
  starting transfers between devices: 37.5 us -> 46.5 us
    psum x8 -> x0, blocking collectives: 193 us -> none  [by_axis(): return functools.reduce(lax.psum, axes, array)]
    all_to_all x4 -> x9, blocking collectives: 40.9 us -> 105 us  [the longest x7 82.7 us: to_everyone(): return lax.all_to_all(copies, axes, split_axis=0, concat_axis=0, tiled=True)]
    ppermute x8, waiting for transfers between devices: 56.8 us -> 16.7 us  [the longest x2 9.84 us: exchange(): got_outer = lax.ppermute(p_outer, ROWS, outer)]
    dot_general x18 -> x0, matrix products: 24.5 us -> none  [the longest x8 16.7 us: advance(): product = jnp.einsum(pattern, stacked, source[fetched], precision=HIGHEST)]
    another operation x10 -> x0, other arithmetic: 24.3 us -> none  [the longest x6 13.1 us: local(): lower = jnp.linalg.cholesky(gram)]
    pallas_call x0 -> x5, Pallas kernels: none -> 12.3 us  [the longest x1 3.38 us: local(): call(last_kernel, [ANY] + [VMEM] * 4, [jax.ShapeDtypeStruct((k, mine * T)...]
    gather x8 -> x0, local copies, waits for them, and re-layouts: 12.2 us -> none  [advance(): product = jnp.einsum(pattern, stacked, source[fetched], precision=HIGHEST)]
    lt x8 -> x0, other arithmetic: 5.2 us -> none  [advance(): active = offset + lane_ids < live_count]
  transfers between devices with their start and end apart: 8 -> 9, of which waited for: 8 -> 3; matrix products, arithmetic and copies ran while one was open for 0% -> 0% of each run, Pallas kernels for 0% -> 1%
where the time goes in v1:
time: 190 us; the launch traced here: 189 us
  blocking collectives  105 us (55%)
  starting transfers between devices  46.5 us (24%)
  waiting for transfers between devices  16.7 us (9%)
  Pallas kernels  12.3 us (6%)
  local copies, waits for them, and re-layouts  5.54 us (3%)
  other arithmetic  2.14 us (1%)
    all_to_all x7, blocking collectives, to_everyone(): return lax.all_to_all(copies, axes, split_axis=0, concat_axis=0, tiled=True)  82.7 us
    all_to_all x2, blocking collectives, exchange(): lax.all_to_all(pieces, 'grp', split_axis=0, concat_axis=0, tiled=True)  22.5 us
    ppermute x2, starting transfers between devices, exchange(): got_outer = lax.ppermute(p_outer, ROWS, outer)  20.3 us
    ppermute x2, starting transfers between devices, exchange(): lax.ppermute(whole, ROWS, outer)  13.7 us
    ppermute x2, waiting for transfers between devices, exchange(): got_outer = lax.ppermute(p_outer, ROWS, outer)  9.84 us
    ppermute x2, waiting for transfers between devices, exchange(): lax.ppermute(whole, ROWS, outer)  6.84 us
    all_to_all x1, starting transfers between devices, to_everyone(): return lax.all_to_all(copies, axes, split_axis=0, concat_axis=0, tiled=True)  4.73 us
    unnamed x7, local copies, waits for them, and re-layouts  3.96 us
  transfers between devices with their start and end apart: 9, of which 3 were waited for; matrix products, arithmetic and copies ran while one was open for 0% of the time, Pallas kernels for 1%

profile of v1, /device:TPU:2, one launch (start us, length us, event | category | flops | bytes accessed | tf_op | source)
XLA Modules:
  0.0 189.4 jit_solution(12925760137533336951)
XLA Ops:
  0.7 1.0 copy.7.sketch
  1.7 0.8 fusion.2.code
  2.5 0.0 copy-start
  2.5 1.9 copy-done
  4.4 1.5 first.1
  5.9 13.3 %collective-permute-start = (f32[16,64,128]{2,1,0:T(8,128)S(1)}, f32[16,64,128]{2,1,0:T(8,128)S(1)}, u32[]{:S(2)}, u32[]{:S(2)}) collective-permute-start(f32[16,64,128]{2,1,0:T(8,128)S(1)} %get-tuple-element.15), channel_id=1, source_target_pairs={{0,508},{4,8},{8,4},{12,16},{16,12},{20,24},{24,20},{28,32},{32,28... | collective-permute-start | bytes 1572872 | tf_op jit(solution)/shard_map/ppermute | solution.py:273
  19.2 1.9 %collective-permute-start.1 = (f32[16,64,128]{2,1,0:T(8,128)S(1)}, f32[16,64,128]{2,1,0:T(8,128)S(1)}, u32[]{:S(2)}, u32[]{:S(2)}) collective-permute-start(f32[16,64,128]{2,1,0:T(8,128)S(1)} %get-tuple-element.16), channel_id=1, source_target_pairs={{0,4},{4,0},{8,12},{12,8},{16,20},{20,16},{24,28},{28,24},{32,36},... | collective-permute-start | bytes 1572872 | tf_op jit(solution)/shard_map/ppermute | solution.py:274
  21.1 4.9 %collective-permute-done = f32[16,64,128]{2,1,0:T(8,128)S(1)} collective-permute-done((f32[16,64,128]{2,1,0:T(8,128)S(1)}, f32[16,64,128]{2,1,0:T(8,128)S(1)}, u32[]{:S(2)}, u32[]{:S(2)}) %collective-permute-start) | collective-permute-done | bytes 524320 | tf_op jit(solution)/shard_map/ppermute | solution.py:273
  26.1 0.0 collective-permute-done.1
  26.1 0.1 add_add_fusion.1
  26.2 11.0 %all_to_all.50 = f32[4,4,64,128]{3,2,1,0:T(8,128)S(1)} all-to-all(f32[4,4,64,128]{3,2,1,0:T(8,128)S(1)} %bitcast.29), channel_id=1, replica_groups=mesh['y'=8,'z'=8,'c'=2,'grp'=4] {'grp'}, dimensions={0} | all-to-all | bytes 1048576 | tf_op jit(solution)/shard_map/all_to_all | solution.py:277
  37.2 10.5 %all_to_all.51 = f32[4,4,64,128]{3,2,1,0:T(8,128)S(1)} all-to-all(f32[4,4,64,128]{3,2,1,0:T(8,128)S(1)} %broadcast_in_dim.29), channel_id=1, replica_groups=mesh['y'=8,'z'=8,'c'=2,'grp'=4] {'grp'}, dimensions={0} | all-to-all | bytes 1048576 | tf_op jit(solution)/shard_map/all_to_all | solution.py:223
  47.7 1.9 %collective-permute-start.3 = (f32[16,64,128]{2,1,0:T(8,128)S(1)}, f32[16,64,128]{2,1,0:T(8,128)S(1)}, u32[]{:S(2)}, u32[]{:S(2)}) collective-permute-start(f32[16,64,128]{2,1,0:T(8,128)S(1)} %bitcast.23), channel_id=1, source_target_pairs={{0,4},{4,0},{8,12},{12,8},{16,20},{20,16},{24,28},{28,24},{32,36},... | collective-permute-start | bytes 1572872 | tf_op jit(solution)/shard_map/ppermute | solution.py:279
  49.6 10.0 %collective-permute-start.2 = (f32[16,64,128]{2,1,0:T(8,128)S(1)}, f32[16,64,128]{2,1,0:T(8,128)S(1)}, u32[]{:S(2)}, u32[]{:S(2)}) collective-permute-start(f32[16,64,128]{2,1,0:T(8,128)S(1)} %bitcast.24), channel_id=1, source_target_pairs={{0,508},{4,8},{8,4},{12,16},{16,12},{20,24},{24,20},{28,32},{32,28... | collective-permute-start | bytes 1572872 | tf_op jit(solution)/shard_map/ppermute | solution.py:279
  59.7 0.0 collective-permute-done.3.s_partner
  59.7 6.8 %collective-permute-done.2.s_outer = f32[16,64,128]{2,1,0:T(8,128)S(1)} collective-permute-done((f32[16,64,128]{2,1,0:T(8,128)S(1)}, f32[16,64,128]{2,1,0:T(8,128)S(1)}, u32[]{:S(2)}, u32[]{:S(2)}) %collective-permute-start.2) | collective-permute-done | bytes 524320 | tf_op jit(solution)/shard_map/ppermute | solution.py:279
  66.5 3.3 %middle.1 = (f32[16,64,128]{2,1,0:T(8,128)S(1)}, f32[16,64,128]{2,1,0:T(8,128)S(1)}, f32[16,64,128]{2,1,0:T(8,128)S(1)}, f32[32,128]{1,0:T(8,128)S(1)}) custom-call(s32[48]{0:T(128)S(1)} %fusion.2.code, s32[1]{0:T(128)} %copy.9.live, f32[48,128,128]{2,1,0:T(8,128)} %tiles.5, f32[16,64,128]{2,1,0:T(8,128)S(1)} %collective-permute-done.2.s_outer, ...), custom_call_target="tpu_custom_call" | custom-call | tf_op jit(solution)/shard_map/middle/pallas_call | solution.py:290
  69.8 7.0 %collective-permute-start.4 = (f32[16,64,128]{2,1,0:T(8,128)S(1)}, f32[16,64,128]{2,1,0:T(8,128)S(1)}, u32[]{:S(2)}, u32[]{:S(2)}) collective-permute-start(f32[16,64,128]{2,1,0:T(8,128)S(1)} %get-tuple-element.18), channel_id=1, source_target_pairs={{0,508},{4,8},{8,4},{12,16},{16,12},{20,24},{24,20},{28,32},{32,28... | collective-permute-start | bytes 1572872 | tf_op jit(solution)/shard_map/ppermute | solution.py:273
  76.8 1.9 %collective-permute-start.5 = (f32[16,64,128]{2,1,0:T(8,128)S(1)}, f32[16,64,128]{2,1,0:T(8,128)S(1)}, u32[]{:S(2)}, u32[]{:S(2)}) collective-permute-start(f32[16,64,128]{2,1,0:T(8,128)S(1)} %get-tuple-element.19), channel_id=1, source_target_pairs={{0,4},{4,0},{8,12},{12,8},{16,20},{20,16},{24,28},{28,24},{32,36},... | collective-permute-start | bytes 1572872 | tf_op jit(solution)/shard_map/ppermute | solution.py:274
  78.7 4.9 %collective-permute-done.4 = f32[16,64,128]{2,1,0:T(8,128)S(1)} collective-permute-done((f32[16,64,128]{2,1,0:T(8,128)S(1)}, f32[16,64,128]{2,1,0:T(8,128)S(1)}, u32[]{:S(2)}, u32[]{:S(2)}) %collective-permute-start.4) | collective-permute-done | bytes 524320 | tf_op jit(solution)/shard_map/ppermute | solution.py:273
  83.7 0.0 collective-permute-done.5
  83.7 0.0 copy-start.1
  83.7 0.1 add_add_fusion
  83.8 11.6 %all_to_all.52 = f32[4,4,64,128]{3,2,1,0:T(8,128)} all-to-all(f32[4,4,64,128]{3,2,1,0:T(8,128)S(1)} %bitcast.30), channel_id=1, replica_groups=mesh['y'=8,'z'=8,'c'=2,'grp'=4] {'grp'}, dimensions={0} | all-to-all | bytes 1048576 | tf_op jit(solution)/shard_map/all_to_all | solution.py:277
  95.3 1.1 reduce_sum.55
  96.5 11.2 %all_to_all.53 = f32[4,4,64,128]{3,2,1,0:T(8,128)} all-to-all(f32[4,4,64,128]{3,2,1,0:T(8,128)S(1)} %broadcast_in_dim.30), channel_id=1, replica_groups=mesh['y'=8,'z'=8,'c'=2,'grp'=4] {'grp'}, dimensions={0} | all-to-all | bytes 1048576 | tf_op jit(solution)/shard_map/all_to_all | solution.py:223
  107.6 0.7 broadcast_in_dim.31
  108.3 4.7 %all-to-all-start.4 = ((f32[8,32,128]{2,1,0:T(8,128)}), f32[8,32,128]{2,1,0:T(8,128)S(1)}, u32[]{:S(2)}, u32[]{:S(2)}) async-start(f32[8,32,128]{2,1,0:T(8,128)} %broadcast_in_dim.31), calls=%async_computation.4 | async-start | bytes 262144 | tf_op jit(solution)/shard_map/all_to_all | solution.py:223
  113.0 2.0 %collective-permute-start.7 = (f32[16,64,128]{2,1,0:T(8,128)}, f32[16,64,128]{2,1,0:T(8,128)}, u32[]{:S(2)}, u32[]{:S(2)}) collective-permute-start(f32[16,64,128]{2,1,0:T(8,128)} %bitcast.26), channel_id=1, source_target_pairs={{0,4},{4,0},{8,12},{12,8},{16,20},{20,16},{24,28},{28,24},{32,36},... | collective-permute-start | bytes 1572872 | tf_op jit(solution)/shard_map/ppermute | solution.py:279
  115.1 3.7 %collective-permute-start.6 = (f32[16,64,128]{2,1,0:T(8,128)}, f32[16,64,128]{2,1,0:T(8,128)}, u32[]{:S(2)}, u32[]{:S(2)}) collective-permute-start(f32[16,64,128]{2,1,0:T(8,128)} %bitcast.27), channel_id=1, source_target_pairs={{0,508},{4,8},{8,4},{12,16},{16,12},{20,24},{24,20},{28,32},{32,28... | collective-permute-start | bytes 1572872 | tf_op jit(solution)/shard_map/ppermute | solution.py:279
  118.7 0.0 all-to-all-done.4
  118.8 13.1 %all_to_all.54 = f32[8,32,128]{2,1,0:T(8,128)S(1)} all-to-all(f32[8,32,128]{2,1,0:T(8,128)S(1)} %broadcast_in_dim.32), channel_id=1, replica_groups=mesh['y'=8,'z'=8,'c'=2,'grp'=4] {'z'}, dimensions={0} | all-to-all | bytes 262144 | tf_op jit(solution)/shard_map/all_to_all | solution.py:223
  131.9 11.9 %all_to_all.55.parts = f32[8,32,128]{2,1,0:T(8,128)S(1)} all-to-all(f32[8,32,128]{2,1,0:T(8,128)S(1)} %broadcast_in_dim.33), channel_id=1, replica_groups=mesh['y'=8,'z'=8,'c'=2,'grp'=4] {'y'}, dimensions={0} | all-to-all | bytes 262144 | tf_op jit(solution)/shard_map/all_to_all | solution.py:223
  143.9 1.9 factor.1.linv
  145.7 0.0 collective-permute-done.7.s_partner
  145.7 0.0 collective-permute-done.6.s_outer
  145.7 0.0 copy-done.1
  145.8 0.0 copy-start.2
  145.8 1.0 copy-done.2
  146.8 3.4 %last.1 = (f32[64,512]{1,0:T(8,128)S(1)}, f32[32,128]{1,0:T(8,128)S(1)}) custom-call(s32[48]{0:T(128)S(1)} %fusion.2.code, s32[1]{0:T(128)} %copy.9.live, f32[48,128,128]{2,1,0:T(8,128)S(1)} %copy-done.1, f32[16,64,128]{2,1,0:T(8,128)} %collective-permute-done.6.s_outer, f32[16,64,128]{2,1,0:T(8,128)S(1)} %bitcast.28, ...), custom_call_target="tpu_custom_call" | custom-call | tf_op jit(solution)/shard_map/last/pallas_call | solution.py:295
  150.2 9.8 %all_to_all.56 = f32[8,32,128]{2,1,0:T(8,128)S(1)} all-to-all(f32[8,32,128]{2,1,0:T(8,128)S(1)} %broadcast_in_dim.34), channel_id=1, replica_groups=mesh['y'=8,'z'=8,'c'=2,'grp'=4] {'c','grp'}, dimensions={0} | all-to-all | bytes 262144 | tf_op jit(solution)/shard_map/all_to_all | solution.py:223
  160.0 14.8 %all_to_all.57 = f32[8,32,128]{2,1,0:T(8,128)S(1)} all-to-all(f32[8,32,128]{2,1,0:T(8,128)S(1)} %broadcast_in_dim.35), channel_id=1, replica_groups=mesh['y'=8,'z'=8,'c'=2,'grp'=4] {'z'}, dimensions={0} | all-to-all | bytes 262144 | tf_op jit(solution)/shard_map/all_to_all | solution.py:223
  174.9 11.5 %all_to_all.58.parts = f32[8,32,128]{2,1,0:T(8,128)S(1)} all-to-all(f32[8,32,128]{2,1,0:T(8,128)S(1)} %broadcast_in_dim.36), channel_id=1, replica_groups=mesh['y'=8,'z'=8,'c'=2,'grp'=4] {'y'}, dimensions={0} | all-to-all | bytes 262144 | tf_op jit(solution)/shard_map/all_to_all | solution.py:223
  186.3 2.3 %basis.1 = f32[512,64]{1,0:T(8,128)S(1)} custom-call(f32[8,32,128]{2,1,0:T(8,128)S(1)} %all_to_all.58.parts, f32[64,512]{1,0:T(8,128)S(1)} %get-tuple-element.22.image), custom_call_target="tpu_custom_call" | custom-call | tf_op jit(solution)/shard_map/basis/pallas_call | solution.py:299
  188.6 0.8 copy.8
  (12 shorter events, 0.2 us)
Async XLA Ops:
  2.5 1.9 copy-start
  5.9 20.2 %collective-permute-start = (f32[16,64,128]{2,1,0:T(8,128)S(1)}, f32[16,64,128]{2,1,0:T(8,128)S(1)}, u32[]{:S(2)}, u32[]{:S(2)}) collective-permute-start(f32[16,64,128]{2,1,0:T(8,128)S(1)} %get-tuple-element.15), channel_id=1, source_target_pairs={{0,508},{4,8},{8,4},{12,16},{16,12},{20,24},{24,20},{28,32},{32,28... | collective-permute-start | bytes 1572872 | tf_op jit(solution)/shard_map/ppermute | solution.py:273
  19.2 6.9 %collective-permute-start.1 = (f32[16,64,128]{2,1,0:T(8,128)S(1)}, f32[16,64,128]{2,1,0:T(8,128)S(1)}, u32[]{:S(2)}, u32[]{:S(2)}) collective-permute-start(f32[16,64,128]{2,1,0:T(8,128)S(1)} %get-tuple-element.16), channel_id=1, source_target_pairs={{0,4},{4,0},{8,12},{12,8},{16,20},{20,16},{24,28},{28,24},{32,36},... | collective-permute-start | bytes 1572872 | tf_op jit(solution)/shard_map/ppermute | solution.py:274
  47.7 12.0 %collective-permute-start.3 = (f32[16,64,128]{2,1,0:T(8,128)S(1)}, f32[16,64,128]{2,1,0:T(8,128)S(1)}, u32[]{:S(2)}, u32[]{:S(2)}) collective-permute-start(f32[16,64,128]{2,1,0:T(8,128)S(1)} %bitcast.23), channel_id=1, source_target_pairs={{0,4},{4,0},{8,12},{12,8},{16,20},{20,16},{24,28},{28,24},{32,36},... | collective-permute-start | bytes 1572872 | tf_op jit(solution)/shard_map/ppermute | solution.py:279
  49.6 16.9 %collective-permute-start.2 = (f32[16,64,128]{2,1,0:T(8,128)S(1)}, f32[16,64,128]{2,1,0:T(8,128)S(1)}, u32[]{:S(2)}, u32[]{:S(2)}) collective-permute-start(f32[16,64,128]{2,1,0:T(8,128)S(1)} %bitcast.24), channel_id=1, source_target_pairs={{0,508},{4,8},{8,4},{12,16},{16,12},{20,24},{24,20},{28,32},{32,28... | collective-permute-start | bytes 1572872 | tf_op jit(solution)/shard_map/ppermute | solution.py:279
  69.8 13.8 %collective-permute-start.4 = (f32[16,64,128]{2,1,0:T(8,128)S(1)}, f32[16,64,128]{2,1,0:T(8,128)S(1)}, u32[]{:S(2)}, u32[]{:S(2)}) collective-permute-start(f32[16,64,128]{2,1,0:T(8,128)S(1)} %get-tuple-element.18), channel_id=1, source_target_pairs={{0,508},{4,8},{8,4},{12,16},{16,12},{20,24},{24,20},{28,32},{32,28... | collective-permute-start | bytes 1572872 | tf_op jit(solution)/shard_map/ppermute | solution.py:273
  76.8 6.9 %collective-permute-start.5 = (f32[16,64,128]{2,1,0:T(8,128)S(1)}, f32[16,64,128]{2,1,0:T(8,128)S(1)}, u32[]{:S(2)}, u32[]{:S(2)}) collective-permute-start(f32[16,64,128]{2,1,0:T(8,128)S(1)} %get-tuple-element.19), channel_id=1, source_target_pairs={{0,4},{4,0},{8,12},{12,8},{16,20},{20,16},{24,28},{28,24},{32,36},... | collective-permute-start | bytes 1572872 | tf_op jit(solution)/shard_map/ppermute | solution.py:274
  83.7 62.1 %copy-start.1 = (f32[48,128,128]{2,1,0:T(8,128)S(1)}, f32[48,128,128]{2,1,0:T(8,128)}, u32[]{:S(2)}) copy-start(f32[48,128,128]{2,1,0:T(8,128)} %tiles.5) | copy-start | bytes 9437188
  108.3 10.5 %all-to-all-start.4 = ((f32[8,32,128]{2,1,0:T(8,128)}), f32[8,32,128]{2,1,0:T(8,128)S(1)}, u32[]{:S(2)}, u32[]{:S(2)}) async-start(f32[8,32,128]{2,1,0:T(8,128)} %broadcast_in_dim.31), calls=%async_computation.4 | async-start | bytes 262144 | tf_op jit(solution)/shard_map/all_to_all | solution.py:223
  113.0 32.7 %collective-permute-start.7 = (f32[16,64,128]{2,1,0:T(8,128)}, f32[16,64,128]{2,1,0:T(8,128)}, u32[]{:S(2)}, u32[]{:S(2)}) collective-permute-start(f32[16,64,128]{2,1,0:T(8,128)} %bitcast.26), channel_id=1, source_target_pairs={{0,4},{4,0},{8,12},{12,8},{16,20},{20,16},{24,28},{28,24},{32,36},... | collective-permute-start | bytes 1572872 | tf_op jit(solution)/shard_map/ppermute | solution.py:279
  115.1 30.7 %collective-permute-start.6 = (f32[16,64,128]{2,1,0:T(8,128)}, f32[16,64,128]{2,1,0:T(8,128)}, u32[]{:S(2)}, u32[]{:S(2)}) collective-permute-start(f32[16,64,128]{2,1,0:T(8,128)} %bitcast.27), channel_id=1, source_target_pairs={{0,508},{4,8},{8,4},{12,16},{16,12},{20,24},{24,20},{28,32},{32,28... | collective-permute-start | bytes 1572872 | tf_op jit(solution)/shard_map/ppermute | solution.py:279
  145.8 1.0 copy-start.2

commit v2 on v1

--- a/solution.py
+++ b/solution.py
@@ -76,10 +76,10 @@
 
 def first_kernel(code, live, tiles, sketch, outer, own, partner, tbuf, phl, acc, sems):
     cap = tiles.shape[0]
-    k = sketch.shape[1]
+    k = sketch.shape[0]
     start_tiles(live[0], tiles, tbuf, sems, cap)
     acc[...] = jnp.zeros_like(acc)
-    keep_panel(lambda t: sketch[t * T : (t + 1) * T, :].T, k, phl)
+    keep_panel(lambda t: sketch[:, t * T : (t + 1) * T], k, phl)
 
     def work(s):
         hi, lo = halves(tbuf[s])
@@ -214,7 +214,7 @@
 
 def basis_kernel(parts, image, basis, *, scale):
     linv = inverse_factor(summed_gram(parts))
-    basis[...] = dot(linv, image[...], (1, 0), HIGHEST).T * scale
+    basis[...] = dot(linv, image[...], (1, 0), HIGHEST) * scale
 
 
 def to_everyone(x, axes):
@@ -268,15 +268,40 @@
             compiler_params=pltpu.CompilerParams(vmem_limit_bytes=48 * 1024 * 1024),
         )
 
-    def exchange(parts, extra=None):
+    def over_grp(x):
+        return lax.all_to_all(x, "grp", split_axis=0, concat_axis=0, tiled=True)
+
+    def over_outer(x):
+        return lax.ppermute(x, ROWS, outer)
+
+    def over_partner(x):
+        return lax.ppermute(x, ROWS, partner)
+
+    def pieces(x):
+        return x.reshape(groups, mine, k, T)
+
+    def exchange(parts):
         p_outer, p_own, p_partner = parts
-        got_outer = lax.ppermute(p_outer, ROWS, outer)
-        got_partner = lax.ppermute(p_partner, ROWS, partner)
-        total = p_own + got_outer + got_partner
-        pieces = total.reshape(groups, mine, k, T)
-        arrived = lax.all_to_all(pieces, "grp", split_axis=0, concat_axis=0, tiled=True)
-        whole = to_everyone(arrived.sum(axis=0), "grp").reshape(block, k, T)
-        return lax.ppermute(whole, ROWS, outer), whole, lax.ppermute(whole, ROWS, partner)
+        got = over_partner(p_partner)
+        at_outer = over_outer(over_grp(pieces(p_outer)).sum(axis=0))
+        middle = over_grp(pieces(p_own + got)).sum(axis=0) + at_outer
+        beside = over_outer(middle)
+        own = to_everyone(middle, "grp").reshape(block, k, T)
+        return to_everyone(beside, "grp").reshape(block, k, T), own, over_partner(own)
+
+    def exchange_with_gram(parts, gram):
+        p_outer, p_own, p_partner = parts
+        got_outer = over_outer(p_outer)
+        got = over_partner(p_partner)
+        gram = to_everyone(gram, ("z", "c")).sum(axis=0)
+        total = (p_own + got_outer + got).reshape(groups, mine * k, T)
+        sides = jnp.broadcast_to(gram, (groups, *gram.shape))
+        arrived = over_grp(jnp.concatenate([total, sides], axis=1)).sum(axis=0)
+        middle, gram = arrived[: mine * k].reshape(mine, k, T), arrived[mine * k :]
+        own = to_everyone(middle, "grp").reshape(block, k, T)
+        own, gram = lax.optimization_barrier((own, gram))
+        gram = to_everyone(gram, "y")
+        return (over_outer(own), own, over_partner(own)), gram
 
     def gram_parts(gram):
         gram = to_everyone(gram, ("c", "grp")).sum(axis=0)
@@ -284,21 +309,21 @@
         return to_everyone(gram, "y")
 
     parts = call(first_kernel, [ANY, VMEM], [block_shape] * 3, [tbuf, phl, acc, sems], 2, "first")(
-        code, live, tiles, sketch
+        code, live, tiles, sketch.T
     )
     whole = exchange(parts)
     *parts, gram = call(
         middle_kernel, [ANY] + [VMEM] * 3, [block_shape] * 3 + [gram_shape], [tbuf, thl, shl, img, phl, acc, sems], 2, "middle"
     )(code, live, tiles, *whole)
-    linv = call(factor_kernel, [VMEM], [square], [], 0, "factor")(gram_parts(gram))[0]
-    whole = exchange(parts)
+    whole, gram = exchange_with_gram(parts, gram)
+    linv = call(factor_kernel, [VMEM], [square], [], 0, "factor")(gram)[0]
     image, gram = call(
         last_kernel, [ANY] + [VMEM] * 4, [jax.ShapeDtypeStruct((k, mine * T), F32), gram_shape], [tbuf, shl, img, sems], 2, "last"
     )(code, live, tiles, *whole, linv)
     scale = float(rows * groups * sketch.shape[0]) ** 0.5
     return call(
-        functools.partial(basis_kernel, scale=scale), [VMEM] * 2, [jax.ShapeDtypeStruct(sketch.shape, F32)], [], 0, "basis"
-    )(gram_parts(gram), image)[0]
+        functools.partial(basis_kernel, scale=scale), [VMEM] * 2, [jax.ShapeDtypeStruct(sketch.shape[::-1], F32)], [], 0, "basis"
+    )(gram_parts(gram), image)[0].T
 
 
 def solution(mesh):

time: 190 us -> 189 us (level)
  blocking collectives: 105 us -> 90 us
  starting transfers between devices: 46.5 us -> 57.6 us
  waiting for transfers between devices: 16.7 us -> 20.7 us
    all_to_all x0 -> x2, starting transfers between devices: none -> 14.4 us  [over_grp(): return lax.all_to_all(x, 'grp', split_axis=0, concat_axis=0, tiled=True)]
    ppermute x8, waiting for transfers between devices: 16.7 us -> 3.1 us  [the longest x4 3.09 us: over_outer(): return lax.ppermute(x, ROWS, outer)]
    all_to_all x1 -> x2, waiting for transfers between devices: 0.01 us -> 8.91 us  [to_everyone(): return lax.all_to_all(copies, axes, split_axis=0, concat_axis=0, tiled=True)]
    ppermute x8, starting transfers between devices: 41.7 us -> 32.9 us  [the longest x4 24.7 us: over_outer(): return lax.ppermute(x, ROWS, outer)]
    all_to_all x0 -> x2, waiting for transfers between devices: none -> 8.67 us  [over_grp(): return lax.all_to_all(x, 'grp', split_axis=0, concat_axis=0, tiled=True)]
    all_to_all x2 -> x1, blocking collectives: 22.5 us -> 14.2 us  [over_grp(): return lax.all_to_all(x, 'grp', split_axis=0, concat_axis=0, tiled=True)]
    all_to_all x7 -> x6, blocking collectives: 82.7 us -> 75.7 us  [to_everyone(): return lax.all_to_all(copies, axes, split_axis=0, concat_axis=0, tiled=True)]
    all_to_all x1 -> x2, starting transfers between devices: 4.73 us -> 10.4 us  [to_everyone(): return lax.all_to_all(copies, axes, split_axis=0, concat_axis=0, tiled=True)]
  transfers between devices with their start and end apart: 9 -> 12, of which waited for: 3 -> 6; matrix products, arithmetic and copies ran while one was open for 0% -> 1% of each run, Pallas kernels for 1% -> 1%
where the time goes in v2:
time: 189 us
  blocking collectives  90 us (48%)
  starting transfers between devices  57.6 us (30%)
  waiting for transfers between devices  20.7 us (11%)
  Pallas kernels  12.2 us (6%)
  local copies, waits for them, and re-layouts  4.63 us (2%)
  other arithmetic  3 us (2%)
    all_to_all x6, blocking collectives, to_everyone(): return lax.all_to_all(copies, axes, split_axis=0, concat_axis=0, tiled=True)  75.7 us
    ppermute x4, starting transfers between devices, over_outer(): return lax.ppermute(x, ROWS, outer)  24.7 us
    all_to_all x2, starting transfers between devices, over_grp(): return lax.all_to_all(x, 'grp', split_axis=0, concat_axis=0, tiled=True)  14.4 us
    all_to_all x1, blocking collectives, over_grp(): return lax.all_to_all(x, 'grp', split_axis=0, concat_axis=0, tiled=True)  14.2 us
    all_to_all x2, starting transfers between devices, to_everyone(): return lax.all_to_all(copies, axes, split_axis=0, concat_axis=0, tiled=True)  10.4 us
    all_to_all x2, waiting for transfers between devices, to_everyone(): return lax.all_to_all(copies, axes, split_axis=0, concat_axis=0, tiled=True)  8.91 us
    all_to_all x2, waiting for transfers between devices, over_grp(): return lax.all_to_all(x, 'grp', split_axis=0, concat_axis=0, tiled=True)  8.67 us
    ppermute x4, starting transfers between devices, over_partner(): return lax.ppermute(x, ROWS, partner)  8.14 us
  transfers between devices with their start and end apart: 12, of which 6 were waited for; matrix products, arithmetic and copies ran while one was open for 1% of the time, Pallas kernels for 1%

profile of v2, /device:TPU:2, one launch (start us, length us, event | category | flops | bytes accessed | tf_op | source)
XLA Modules:
  0.0 189.0 jit_solution(2348454232267462795)
XLA Ops:
  0.7 0.8 fusion.2.code
  1.4 0.0 copy-start
  1.4 1.9 copy-done
  3.3 0.0 copy-start.2
  3.3 0.9 copy-done.2
  4.2 1.9 %first.1 = (f32[16,64,128]{2,1,0:T(8,128)}, f32[16,64,128]{2,1,0:T(8,128)S(1)}, f32[16,64,128]{2,1,0:T(8,128)S(1)}) custom-call(s32[48]{0:T(128)S(1)} %fusion.2.code, s32[1]{0:T(128)} %copy.5.live, f32[48,128,128]{2,1,0:T(8,128)S(1)} %copy-done, f32[64,512]{1,0:T(8,128)S(1)} %bitcast.31), custom_call_target="tpu_custom_call" | custom-call | tf_op jit(solution)/shard_map/first/pallas_call | solution.py:311
  6.2 2.4 %collective-permute-start = (f32[16,64,128]{2,1,0:T(8,128)S(1)}, f32[16,64,128]{2,1,0:T(8,128)S(1)}, u32[]{:S(2)}, u32[]{:S(2)}) collective-permute-start(f32[16,64,128]{2,1,0:T(8,128)S(1)} %get-tuple-element.17), channel_id=1, source_target_pairs={{0,4},{4,0},{8,12},{12,8},{16,20},{20,16},{24,28},{28,24},{32,36},... | collective-permute-start | bytes 1572872 | tf_op jit(solution)/shard_map/ppermute | solution.py:278
  8.6 9.5 %all-to-all-start.1 = ((f32[4,4,64,128]{3,2,1,0:T(8,128)}), f32[4,4,64,128]{3,2,1,0:T(8,128)S(1)}, u32[]{:S(2)}, u32[]{:S(2)}) async-start(f32[4,4,64,128]{3,2,1,0:T(8,128)} %bitcast.5), calls=%async_computation.1 | async-start | bytes 1048576 | tf_op jit(solution)/shard_map/all_to_all | solution.py:272
  18.1 0.0 collective-permute-done
  18.1 0.9 add.58
  18.9 8.1 %all-to-all-done.1 = f32[4,4,64,128]{3,2,1,0:T(8,128)S(1)} async-done(((f32[4,4,64,128]{3,2,1,0:T(8,128)}), f32[4,4,64,128]{3,2,1,0:T(8,128)S(1)}, u32[]{:S(2)}, u32[]{:S(2)}) %all-to-all-start.1) | async-done | bytes 524320 | tf_op jit(solution)/shard_map/all_to_all | solution.py:272
  27.0 4.9 %all-to-all-start = ((f32[4,4,64,128]{3,2,1,0:T(8,128)}), f32[4,4,64,128]{3,2,1,0:T(8,128)S(1)}, u32[]{:S(2)}, u32[]{:S(2)}) async-start(f32[4,4,64,128]{3,2,1,0:T(8,128)} %bitcast.4), calls=%async_computation | async-start | bytes 1048576 | tf_op jit(solution)/shard_map/all_to_all | solution.py:272
  32.0 7.5 %collective-permute-start.1 = (f32[4,64,128]{2,1,0:T(8,128)S(1)}, f32[4,64,128]{2,1,0:T(8,128)S(1)}, u32[]{:S(2)}, u32[]{:S(2)}) collective-permute-start(f32[4,64,128]{2,1,0:T(8,128)S(1)} %reduce_sum.55), channel_id=1, source_target_pairs={{0,508},{4,8},{8,4},{12,16},{16,12},{20,24},{24,20},{28,32},{32,28... | collective-permute-start | bytes 393224 | tf_op jit(solution)/shard_map/ppermute | solution.py:275
  39.5 0.6 all-to-all-done
  40.1 2.0 %collective-permute-done.1 = f32[4,64,128]{2,1,0:T(8,128)S(1)} collective-permute-done((f32[4,64,128]{2,1,0:T(8,128)S(1)}, f32[4,64,128]{2,1,0:T(8,128)S(1)}, u32[]{:S(2)}, u32[]{:S(2)}) %collective-permute-start.1) | collective-permute-done | bytes 131104 | tf_op jit(solution)/shard_map/ppermute | solution.py:275
  42.1 0.9 broadcast_in_dim.33
  43.0 4.8 %all-to-all-start.3 = ((f32[4,4,64,128]{3,2,1,0:T(8,128)}), f32[4,4,64,128]{3,2,1,0:T(8,128)S(1)}, u32[]{:S(2)}, u32[]{:S(2)}) async-start(f32[4,4,64,128]{3,2,1,0:T(8,128)} %broadcast_in_dim.33), calls=%async_computation.3 | async-start | bytes 1048576 | tf_op jit(solution)/shard_map/all_to_all | solution.py:223
  47.8 6.4 %collective-permute-start.2 = (f32[4,64,128]{2,1,0:T(8,128)S(1)}, f32[4,64,128]{2,1,0:T(8,128)S(1)}, u32[]{:S(2)}, u32[]{:S(2)}) collective-permute-start(f32[4,64,128]{2,1,0:T(8,128)S(1)} %add.59), channel_id=1, source_target_pairs={{0,508},{4,8},{8,4},{12,16},{16,12},{20,24},{24,20},{28,32},{32,28... | collective-permute-start | bytes 393224 | tf_op jit(solution)/shard_map/ppermute | solution.py:275
  54.2 0.2 all-to-all-done.3
  54.4 1.9 %collective-permute-start.3 = (f32[16,64,128]{2,1,0:T(8,128)S(1)}, f32[16,64,128]{2,1,0:T(8,128)S(1)}, u32[]{:S(2)}, u32[]{:S(2)}) collective-permute-start(f32[16,64,128]{2,1,0:T(8,128)S(1)} %bitcast.28), channel_id=1, source_target_pairs={{0,4},{4,0},{8,12},{12,8},{16,20},{20,16},{24,28},{28,24},{32,36},... | collective-permute-start | bytes 1572872 | tf_op jit(solution)/shard_map/ppermute | solution.py:278
  56.3 1.1 collective-permute-done.2
  57.4 12.0 %all_to_all.55 = f32[4,4,64,128]{3,2,1,0:T(8,128)S(1)} all-to-all(f32[4,4,64,128]{3,2,1,0:T(8,128)S(1)} %broadcast_in_dim.32), channel_id=1, replica_groups=mesh['y'=8,'z'=8,'c'=2,'grp'=4] {'grp'}, dimensions={0} | all-to-all | bytes 1048576 | tf_op jit(solution)/shard_map/all_to_all | solution.py:223
  69.5 0.0 collective-permute-done.3.s_partner
  69.5 2.7 %middle.1 = (f32[16,64,128]{2,1,0:T(8,128)S(1)}, f32[16,64,128]{2,1,0:T(8,128)S(1)}, f32[16,64,128]{2,1,0:T(8,128)S(1)}, f32[32,128]{1,0:T(8,128)S(1)}) custom-call(s32[48]{0:T(128)S(1)} %fusion.2.code, s32[1]{0:T(128)} %copy.5.live, f32[48,128,128]{2,1,0:T(8,128)} %tiles.5, f32[16,64,128]{2,1,0:T(8,128)S(1)} %bitcast.30, f32[16,64,128]{2,1,0:T(8,128)S(1)} %bitcast.29, ...), custom_call_target="tpu_custom_call" | custom-call | tf_op jit(solution)/shard_map/middle/pallas_call | solution.py:315
  72.2 8.2 %collective-permute-start.4 = (f32[16,64,128]{2,1,0:T(8,128)S(1)}, f32[16,64,128]{2,1,0:T(8,128)S(1)}, u32[]{:S(2)}, u32[]{:S(2)}) collective-permute-start(f32[16,64,128]{2,1,0:T(8,128)S(1)} %get-tuple-element.20), channel_id=1, source_target_pairs={{0,508},{4,8},{8,4},{12,16},{16,12},{20,24},{24,20},{28,32},{32,28... | collective-permute-start | bytes 1572872 | tf_op jit(solution)/shard_map/ppermute | solution.py:275
  80.4 1.9 %collective-permute-start.5 = (f32[16,64,128]{2,1,0:T(8,128)S(1)}, f32[16,64,128]{2,1,0:T(8,128)S(1)}, u32[]{:S(2)}, u32[]{:S(2)}) collective-permute-start(f32[16,64,128]{2,1,0:T(8,128)S(1)} %get-tuple-element.21), channel_id=1, source_target_pairs={{0,4},{4,0},{8,12},{12,8},{16,20},{20,16},{24,28},{28,24},{32,36},... | collective-permute-start | bytes 1572872 | tf_op jit(solution)/shard_map/ppermute | solution.py:278
  82.4 13.6 %all_to_all.56 = f32[16,32,128]{2,1,0:T(8,128)S(1)} all-to-all(f32[16,32,128]{2,1,0:T(8,128)S(1)} %broadcast_in_dim.34), channel_id=1, replica_groups=mesh['y'=8,'z'=8,'c'=2,'grp'=4] {'z','c'}, dimensions={0} | all-to-all | bytes 524288 | tf_op jit(solution)/shard_map/all_to_all | solution.py:223
  96.0 0.0 collective-permute-done.4
  96.0 0.0 collective-permute-done.5
  96.0 0.1 add_add_fusion
  96.1 0.0 copy-start.1
  96.2 14.2 %all_to_all.57 = f32[4,288,128]{2,1,0:T(8,128)} all-to-all(f32[4,288,128]{2,1,0:T(8,128)S(1)} %pad_maximum_fusion), channel_id=1, replica_groups=mesh['y'=8,'z'=8,'c'=2,'grp'=4] {'grp'}, dimensions={0} | all-to-all | bytes 1179648 | tf_op jit(solution)/shard_map/all_to_all | solution.py:272
  110.4 1.1 reduce_sum.57
  111.6 0.8 broadcast_in_dim.36
  112.4 5.6 %all-to-all-start.6 = ((f32[4,4,64,128]{3,2,1,0:T(8,128)}), f32[4,4,64,128]{3,2,1,0:T(8,128)}, u32[]{:S(2)}, u32[]{:S(2)}) async-start(f32[4,4,64,128]{3,2,1,0:T(8,128)} %broadcast_in_dim.36), calls=%async_computation.6 | async-start | bytes 1048576 | tf_op jit(solution)/shard_map/all_to_all | solution.py:223
  118.0 8.7 %all-to-all-done.6 = f32[4,4,64,128]{3,2,1,0:T(8,128)} async-done(((f32[4,4,64,128]{3,2,1,0:T(8,128)}), f32[4,4,64,128]{3,2,1,0:T(8,128)}, u32[]{:S(2)}, u32[]{:S(2)}) %all-to-all-start.6) | async-done | bytes 524320 | tf_op jit(solution)/shard_map/all_to_all | solution.py:223
  126.6 1.9 %collective-permute-start.7 = (f32[16,64,128]{2,1,0:T(8,128)}, f32[16,64,128]{2,1,0:T(8,128)S(1)}, u32[]{:S(2)}, u32[]{:S(2)}) collective-permute-start(f32[16,64,128]{2,1,0:T(8,128)} %bitcast.10.s_own), channel_id=1, source_target_pairs={{0,4},{4,0},{8,12},{12,8},{16,20},{20,16},{24,28},{28,24},{32,36},... | collective-permute-start | bytes 1572872 | tf_op jit(solution)/shard_map/ppermute | solution.py:278
  128.6 2.6 %collective-permute-start.6 = (f32[16,64,128]{2,1,0:T(8,128)}, f32[16,64,128]{2,1,0:T(8,128)S(1)}, u32[]{:S(2)}, u32[]{:S(2)}) collective-permute-start(f32[16,64,128]{2,1,0:T(8,128)} %bitcast.10.s_own), channel_id=1, source_target_pairs={{0,508},{4,8},{8,4},{12,16},{16,12},{20,24},{24,20},{28,32},{32,28... | collective-permute-start | bytes 1572872 | tf_op jit(solution)/shard_map/ppermute | solution.py:275
  131.2 16.1 %all_to_all.58.parts = f32[8,32,128]{2,1,0:T(8,128)S(1)} all-to-all(f32[8,32,128]{2,1,0:T(8,128)S(1)} %broadcast_in_dim.37), channel_id=1, replica_groups=mesh['y'=8,'z'=8,'c'=2,'grp'=4] {'y'}, dimensions={0} | all-to-all | bytes 262144 | tf_op jit(solution)/shard_map/all_to_all | solution.py:223
  147.3 1.9 factor.1.linv
  149.2 0.0 collective-permute-done.7.s_partner
  149.2 0.0 collective-permute-done.6.s_outer
  149.2 0.0 copy-done.1
  149.2 2.9 %last.1 = (f32[64,512]{1,0:T(8,128)S(1)}, f32[32,128]{1,0:T(8,128)S(1)}) custom-call(s32[48]{0:T(128)S(1)} %fusion.2.code, s32[1]{0:T(128)} %copy.5.live, f32[48,128,128]{2,1,0:T(8,128)S(1)} %copy-done.1, f32[16,64,128]{2,1,0:T(8,128)S(1)} %collective-permute-done.6.s_outer, f32[16,64,128]{2,1,0:T(8,128)} %bitcast.10.s_own, ...), custom_call_target="tpu_custom_call" | custom-call | tf_op jit(solution)/shard_map/last/pallas_call | solution.py:320
  152.1 9.0 %all_to_all.59 = f32[8,32,128]{2,1,0:T(8,128)S(1)} all-to-all(f32[8,32,128]{2,1,0:T(8,128)S(1)} %broadcast_in_dim.38), channel_id=1, replica_groups=mesh['y'=8,'z'=8,'c'=2,'grp'=4] {'c','grp'}, dimensions={0} | all-to-all | bytes 262144 | tf_op jit(solution)/shard_map/all_to_all | solution.py:223
  161.1 12.7 %all_to_all.60 = f32[8,32,128]{2,1,0:T(8,128)S(1)} all-to-all(f32[8,32,128]{2,1,0:T(8,128)S(1)} %broadcast_in_dim.39), channel_id=1, replica_groups=mesh['y'=8,'z'=8,'c'=2,'grp'=4] {'z'}, dimensions={0} | all-to-all | bytes 262144 | tf_op jit(solution)/shard_map/all_to_all | solution.py:223
  173.8 12.4 %all_to_all.61.parts = f32[8,32,128]{2,1,0:T(8,128)S(1)} all-to-all(f32[8,32,128]{2,1,0:T(8,128)S(1)} %broadcast_in_dim.40), channel_id=1, replica_groups=mesh['y'=8,'z'=8,'c'=2,'grp'=4] {'y'}, dimensions={0} | all-to-all | bytes 262144 | tf_op jit(solution)/shard_map/all_to_all | solution.py:223
  186.2 2.8 %basis.1 = f32[64,512]{1,0:T(8,128)} custom-call(f32[8,32,128]{2,1,0:T(8,128)S(1)} %all_to_all.61.parts, f32[64,512]{1,0:T(8,128)S(1)} %get-tuple-element.26.image), custom_call_target="tpu_custom_call" | custom-call | tf_op jit(solution)/shard_map/basis/pallas_call | solution.py:324
  (16 shorter events, 0.3 us)
Async XLA Ops:
  1.4 1.9 copy-start
  3.3 0.9 copy-start.2
  6.2 11.9 %collective-permute-start = (f32[16,64,128]{2,1,0:T(8,128)S(1)}, f32[16,64,128]{2,1,0:T(8,128)S(1)}, u32[]{:S(2)}, u32[]{:S(2)}) collective-permute-start(f32[16,64,128]{2,1,0:T(8,128)S(1)} %get-tuple-element.17), channel_id=1, source_target_pairs={{0,4},{4,0},{8,12},{12,8},{16,20},{20,16},{24,28},{28,24},{32,36},... | collective-permute-start | bytes 1572872 | tf_op jit(solution)/shard_map/ppermute | solution.py:278
  8.6 18.5 %all-to-all-start.1 = ((f32[4,4,64,128]{3,2,1,0:T(8,128)}), f32[4,4,64,128]{3,2,1,0:T(8,128)S(1)}, u32[]{:S(2)}, u32[]{:S(2)}) async-start(f32[4,4,64,128]{3,2,1,0:T(8,128)} %bitcast.5), calls=%async_computation.1 | async-start | bytes 1048576 | tf_op jit(solution)/shard_map/all_to_all | solution.py:272
  27.0 13.0 %all-to-all-start = ((f32[4,4,64,128]{3,2,1,0:T(8,128)}), f32[4,4,64,128]{3,2,1,0:T(8,128)S(1)}, u32[]{:S(2)}, u32[]{:S(2)}) async-start(f32[4,4,64,128]{3,2,1,0:T(8,128)} %bitcast.4), calls=%async_computation | async-start | bytes 1048576 | tf_op jit(solution)/shard_map/all_to_all | solution.py:272
  32.0 10.1 %collective-permute-start.1 = (f32[4,64,128]{2,1,0:T(8,128)S(1)}, f32[4,64,128]{2,1,0:T(8,128)S(1)}, u32[]{:S(2)}, u32[]{:S(2)}) collective-permute-start(f32[4,64,128]{2,1,0:T(8,128)S(1)} %reduce_sum.55), channel_id=1, source_target_pairs={{0,508},{4,8},{8,4},{12,16},{16,12},{20,24},{24,20},{28,32},{32,28... | collective-permute-start | bytes 393224 | tf_op jit(solution)/shard_map/ppermute | solution.py:275
  43.0 11.4 %all-to-all-start.3 = ((f32[4,4,64,128]{3,2,1,0:T(8,128)}), f32[4,4,64,128]{3,2,1,0:T(8,128)S(1)}, u32[]{:S(2)}, u32[]{:S(2)}) async-start(f32[4,4,64,128]{3,2,1,0:T(8,128)} %broadcast_in_dim.33), calls=%async_computation.3 | async-start | bytes 1048576 | tf_op jit(solution)/shard_map/all_to_all | solution.py:223
  47.8 9.6 %collective-permute-start.2 = (f32[4,64,128]{2,1,0:T(8,128)S(1)}, f32[4,64,128]{2,1,0:T(8,128)S(1)}, u32[]{:S(2)}, u32[]{:S(2)}) collective-permute-start(f32[4,64,128]{2,1,0:T(8,128)S(1)} %add.59), channel_id=1, source_target_pairs={{0,508},{4,8},{8,4},{12,16},{16,12},{20,24},{24,20},{28,32},{32,28... | collective-permute-start | bytes 393224 | tf_op jit(solution)/shard_map/ppermute | solution.py:275
  54.4 15.1 %collective-permute-start.3 = (f32[16,64,128]{2,1,0:T(8,128)S(1)}, f32[16,64,128]{2,1,0:T(8,128)S(1)}, u32[]{:S(2)}, u32[]{:S(2)}) collective-permute-start(f32[16,64,128]{2,1,0:T(8,128)S(1)} %bitcast.28), channel_id=1, source_target_pairs={{0,4},{4,0},{8,12},{12,8},{16,20},{20,16},{24,28},{28,24},{32,36},... | collective-permute-start | bytes 1572872 | tf_op jit(solution)/shard_map/ppermute | solution.py:278
  72.2 23.8 %collective-permute-start.4 = (f32[16,64,128]{2,1,0:T(8,128)S(1)}, f32[16,64,128]{2,1,0:T(8,128)S(1)}, u32[]{:S(2)}, u32[]{:S(2)}) collective-permute-start(f32[16,64,128]{2,1,0:T(8,128)S(1)} %get-tuple-element.20), channel_id=1, source_target_pairs={{0,508},{4,8},{8,4},{12,16},{16,12},{20,24},{24,20},{28,32},{32,28... | collective-permute-start | bytes 1572872 | tf_op jit(solution)/shard_map/ppermute | solution.py:275
  80.4 15.6 %collective-permute-start.5 = (f32[16,64,128]{2,1,0:T(8,128)S(1)}, f32[16,64,128]{2,1,0:T(8,128)S(1)}, u32[]{:S(2)}, u32[]{:S(2)}) collective-permute-start(f32[16,64,128]{2,1,0:T(8,128)S(1)} %get-tuple-element.21), channel_id=1, source_target_pairs={{0,4},{4,0},{8,12},{12,8},{16,20},{20,16},{24,28},{28,24},{32,36},... | collective-permute-start | bytes 1572872 | tf_op jit(solution)/shard_map/ppermute | solution.py:278
  96.1 53.1 %copy-start.1 = (f32[48,128,128]{2,1,0:T(8,128)S(1)}, f32[48,128,128]{2,1,0:T(8,128)}, u32[]{:S(2)}) copy-start(f32[48,128,128]{2,1,0:T(8,128)} %tiles.5) | copy-start | bytes 9437188
  112.4 14.2 %all-to-all-start.6 = ((f32[4,4,64,128]{3,2,1,0:T(8,128)}), f32[4,4,64,128]{3,2,1,0:T(8,128)}, u32[]{:S(2)}, u32[]{:S(2)}) async-start(f32[4,4,64,128]{3,2,1,0:T(8,128)} %broadcast_in_dim.36), calls=%async_computation.6 | async-start | bytes 1048576 | tf_op jit(solution)/shard_map/all_to_all | solution.py:223
  126.6 22.5 %collective-permute-start.7 = (f32[16,64,128]{2,1,0:T(8,128)}, f32[16,64,128]{2,1,0:T(8,128)S(1)}, u32[]{:S(2)}, u32[]{:S(2)}) collective-permute-start(f32[16,64,128]{2,1,0:T(8,128)} %bitcast.10.s_own), channel_id=1, source_target_pairs={{0,4},{4,0},{8,12},{12,8},{16,20},{20,16},{24,28},{28,24},{32,36},... | collective-permute-start | bytes 1572872 | tf_op jit(solution)/shard_map/ppermute | solution.py:278
  128.6 20.6 %collective-permute-start.6 = (f32[16,64,128]{2,1,0:T(8,128)}, f32[16,64,128]{2,1,0:T(8,128)S(1)}, u32[]{:S(2)}, u32[]{:S(2)}) collective-permute-start(f32[16,64,128]{2,1,0:T(8,128)} %bitcast.10.s_own), channel_id=1, source_target_pairs={{0,508},{4,8},{8,4},{12,16},{16,12},{20,24},{24,20},{28,32},{32,28... | collective-permute-start | bytes 1572872 | tf_op jit(solution)/shard_map/ppermute | solution.py:275

commit v3 on v2

--- a/solution.py
+++ b/solution.py
@@ -8,6 +8,7 @@
 from jax.sharding import Mesh
 from jax.sharding import PartitionSpec as P
 
+
 ROWS = ("y", "z", "c")
 ROWS_GRP = ("y", "z", "c", "grp")
 HIGHEST = lax.Precision.HIGHEST
@@ -15,6 +16,7 @@
 BF16 = jnp.bfloat16
 T = 128
 CHUNK = 8
+VMEM_LIMIT = 48 * 1024 * 1024
 
 
 def dot(a, b, contract, precision=None):
@@ -32,23 +34,13 @@
     return (q[:k, :T] + q[k:, T:]) + (q[k:, :T] + q[:k, T:])
 
 
-def start_tiles(live, tiles, tbuf, sems, cap):
+def each_chunk(live, cap, work, ready=None):
     for c in range(cap // CHUNK):
-        at = pl.ds(c * CHUNK, CHUNK)
 
         @pl.when(c * CHUNK < live)
         def _():
-            pltpu.make_async_copy(tiles.at[at], tbuf.at[at], sems.at[c]).start()
-
-
-def each_chunk(live, tiles, tbuf, sems, cap, work, wait=True):
-    for c in range(cap // CHUNK):
-        at = pl.ds(c * CHUNK, CHUNK)
-
-        @pl.when(c * CHUNK < live)
-        def _():
-            if wait:
-                pltpu.make_async_copy(tiles.at[at], tbuf.at[at], sems.at[c]).wait()
+            if ready is not None:
+                ready(c)
             for s in range(c * CHUNK, (c + 1) * CHUNK):
                 work(s)
 
@@ -60,11 +52,11 @@
         phl[t, k:, :] = lo
 
 
-def spread_slot(s, code, hi, lo, phl, acc):
+def spread_slot(s, code, thl, phl, acc):
     k = phl.shape[1] // 2
     entry = code[s]
     at = entry & 255
-    q = dot(phl[entry >> 8], jnp.concatenate([hi, lo], axis=1), (1, 0))
+    q = dot(phl[entry >> 8], jnp.concatenate([thl[s, :T, :], thl[s, T:, :]], axis=1), (1, 0))
     acc[at] += fold(q, k)
 
 
@@ -74,18 +66,35 @@
         out[...] = acc[n * each : (n + 1) * each]
 
 
-def first_kernel(code, live, tiles, sketch, outer, own, partner, tbuf, phl, acc, sems):
+def first_kernel(
+    code, live, tiles, sketch, outer, own, partner, thl, tbuf, panel, phl, acc, sems, panel_sem
+):
     cap = tiles.shape[0]
     k = sketch.shape[0]
-    start_tiles(live[0], tiles, tbuf, sems, cap)
+
+    def tile_copy(c):
+        at = pl.ds(c * CHUNK, CHUNK)
+        return pltpu.make_async_copy(tiles.at[at], tbuf.at[at], sems.at[c])
+
+    panel_copy = pltpu.make_async_copy(sketch, panel, panel_sem)
+    panel_copy.start()
+    for c in range(cap // CHUNK):
+
+        @pl.when(c * CHUNK < live[0])
+        def _():
+            tile_copy(c).start()
+
     acc[...] = jnp.zeros_like(acc)
-    keep_panel(lambda t: sketch[:, t * T : (t + 1) * T], k, phl)
+    panel_copy.wait()
+    keep_panel(lambda t: panel[:, t * T : (t + 1) * T], k, phl)
 
     def work(s):
         hi, lo = halves(tbuf[s])
-        spread_slot(s, code, hi, lo, phl, acc)
-
-    each_chunk(live[0], tiles, tbuf, sems, cap, work)
+        thl[s, :T, :] = hi
+        thl[s, T:, :] = lo
+        spread_slot(s, code, thl, phl, acc)
+
+    each_chunk(live[0], cap, work, lambda c: tile_copy(c).wait())
     put_spread(acc, (outer, own, partner))
 
 
@@ -104,10 +113,10 @@
     shl[3 * each] = jnp.zeros_like(shl[3 * each])
 
 
-def image_slot(s, code, hi, lo, shl, img):
+def image_slot(s, code, thl, shl, img):
     k = shl.shape[1] // 2
     entry = code[s]
-    q = dot(shl[entry & 255], jnp.concatenate([hi, lo], axis=0), (1, 1))
+    q = dot(shl[entry & 255], thl[s], (1, 1))
     img[entry >> 8] += fold(q, k)
 
 
@@ -122,30 +131,17 @@
 
 
 def middle_kernel(
-    code, live, tiles, s_outer, s_own, s_partner, outer, own, partner, gram,
-    tbuf, thl, shl, img, phl, acc, sems,
+    code, live, thl, s_outer, s_own, s_partner, outer, own, partner, gram, shl, img, phl, acc
 ):
-    cap = tiles.shape[0]
+    cap = thl.shape[0]
     k = s_own.shape[1]
-    start_tiles(live[0], tiles, tbuf, sems, cap)
     keep_spread((s_outer, s_own, s_partner), shl)
     img[...] = jnp.zeros_like(img)
     acc[...] = jnp.zeros_like(acc)
-
-    def forth(s):
-        hi, lo = halves(tbuf[s])
-        thl[s, :T, :] = hi
-        thl[s, T:, :] = lo
-        image_slot(s, code, hi, lo, shl, img)
-
-    each_chunk(live[0], tiles, tbuf, sems, cap, forth)
+    each_chunk(live[0], cap, lambda s: image_slot(s, code, thl, shl, img))
     put_gram(whole_image(img), gram)
     keep_panel(lambda t: img[t], k, phl)
-
-    def back(s):
-        spread_slot(s, code, thl[s, :T, :], thl[s, T:, :], phl, acc)
-
-    each_chunk(live[0], tiles, tbuf, sems, cap, back, wait=False)
+    each_chunk(live[0], cap, lambda s: spread_slot(s, code, thl, phl, acc))
     put_spread(acc, (outer, own, partner))
 
 
@@ -196,17 +192,10 @@
     linv[...] = inverse_factor(summed_gram(parts))
 
 
-def last_kernel(code, live, tiles, s_outer, s_own, s_partner, linv, image, gram, tbuf, shl, img, sems):
-    cap = tiles.shape[0]
-    start_tiles(live[0], tiles, tbuf, sems, cap)
+def last_kernel(code, live, thl, s_outer, s_own, s_partner, linv, image, gram, shl, img):
     keep_spread((s_outer, s_own, s_partner), shl)
     img[...] = jnp.zeros_like(img)
-
-    def forth(s):
-        hi, lo = halves(tbuf[s])
-        image_slot(s, code, hi, lo, shl, img)
-
-    each_chunk(live[0], tiles, tbuf, sems, cap, forth)
+    each_chunk(live[0], thl.shape[0], lambda s: image_slot(s, code, thl, shl, img))
     x = dot(linv[...], whole_image(img), (1, 0), HIGHEST)
     image[...] = x
     put_gram(x, gram)
@@ -224,7 +213,7 @@
 
 
 VMEM = pl.BlockSpec(memory_space=pltpu.VMEM)
-ANY = pl.BlockSpec(memory_space=pl.ANY)
+HBM = pl.BlockSpec(memory_space=pltpu.HBM)
 
 
 def local(tiles, coords, live, sketch):
@@ -250,22 +239,21 @@
     gram_shape = jax.ShapeDtypeStruct((k // 2, 2 * k), F32)
     square = jax.ShapeDtypeStruct((k, k), F32)
     tbuf = pltpu.VMEM((cap, T, T), F32)
-    thl = pltpu.VMEM((cap, 2 * T, T), BF16)
+    panel = pltpu.VMEM((k, mine * T), F32)
     phl = pltpu.VMEM((mine, 2 * k, T), BF16)
     shl = pltpu.VMEM((3 * block + 1, 2 * k, T), BF16)
     acc = pltpu.VMEM((3 * block + 1, k, T), F32)
     img = pltpu.VMEM((mine, k, T), F32)
     sems = pltpu.SemaphoreType.DMA((cap // CHUNK,))
 
-    def call(kernel, ins, outs, scratch, prefetch=0, name=None):
+    def call(kernel, ins, outs, scratch, prefetch=0):
         return pl.pallas_call(
             kernel,
             grid_spec=pltpu.PrefetchScalarGridSpec(
                 num_scalar_prefetch=prefetch, grid=(), in_specs=ins, out_specs=[VMEM] * len(outs), scratch_shapes=scratch
             ),
             out_shape=outs,
-            name=name,
-            compiler_params=pltpu.CompilerParams(vmem_limit_bytes=48 * 1024 * 1024),
+            compiler_params=pltpu.CompilerParams(vmem_limit_bytes=VMEM_LIMIT),
         )
 
     def over_grp(x):
@@ -282,18 +270,16 @@
 
     def exchange(parts):
         p_outer, p_own, p_partner = parts
-        got = over_partner(p_partner)
-        at_outer = over_outer(over_grp(pieces(p_outer)).sum(axis=0))
-        middle = over_grp(pieces(p_own + got)).sum(axis=0) + at_outer
-        beside = over_outer(middle)
-        own = to_everyone(middle, "grp").reshape(block, k, T)
-        return to_everyone(beside, "grp").reshape(block, k, T), own, over_partner(own)
+        total = p_own + over_outer(p_outer) + over_partner(p_partner)
+        own = to_everyone(over_grp(pieces(total)).sum(axis=0), "grp").reshape(block, k, T)
+        return over_outer(own), own, over_partner(own)
 
     def exchange_with_gram(parts, gram):
         p_outer, p_own, p_partner = parts
+        gram = to_everyone(gram, ("z", "c"))
         got_outer = over_outer(p_outer)
         got = over_partner(p_partner)
-        gram = to_everyone(gram, ("z", "c")).sum(axis=0)
+        gram = gram.sum(axis=0)
         total = (p_own + got_outer + got).reshape(groups, mine * k, T)
         sides = jnp.broadcast_to(gram, (groups, *gram.shape))
         arrived = over_grp(jnp.concatenate([total, sides], axis=1)).sum(axis=0)
@@ -301,28 +287,35 @@
         own = to_everyone(middle, "grp").reshape(block, k, T)
         own, gram = lax.optimization_barrier((own, gram))
         gram = to_everyone(gram, "y")
-        return (over_outer(own), own, over_partner(own)), gram
+        at_outer = over_outer(own)
+        at_partner = over_partner(own)
+        return (at_outer, own, at_partner), gram
 
     def gram_parts(gram):
         gram = to_everyone(gram, ("c", "grp")).sum(axis=0)
         gram = to_everyone(gram, "z").sum(axis=0)
         return to_everyone(gram, "y")
 
-    parts = call(first_kernel, [ANY, VMEM], [block_shape] * 3, [tbuf, phl, acc, sems], 2, "first")(
-        code, live, tiles, sketch.T
-    )
+    tile_halves = jax.ShapeDtypeStruct((cap, 2 * T, T), BF16)
+    *parts, thl = call(
+        first_kernel,
+        [HBM, HBM],
+        [block_shape] * 3 + [tile_halves],
+        [tbuf, panel, phl, acc, sems, pltpu.SemaphoreType.DMA],
+        2,
+    )(code, live, tiles, sketch.T)
     whole = exchange(parts)
     *parts, gram = call(
-        middle_kernel, [ANY] + [VMEM] * 3, [block_shape] * 3 + [gram_shape], [tbuf, thl, shl, img, phl, acc, sems], 2, "middle"
-    )(code, live, tiles, *whole)
+        middle_kernel, [VMEM] * 4, [block_shape] * 3 + [gram_shape], [shl, img, phl, acc], 2
+    )(code, live, thl, *whole)
     whole, gram = exchange_with_gram(parts, gram)
-    linv = call(factor_kernel, [VMEM], [square], [], 0, "factor")(gram)[0]
+    linv = call(factor_kernel, [VMEM], [square], [], 0)(gram)[0]
     image, gram = call(
-        last_kernel, [ANY] + [VMEM] * 4, [jax.ShapeDtypeStruct((k, mine * T), F32), gram_shape], [tbuf, shl, img, sems], 2, "last"
-    )(code, live, tiles, *whole, linv)
+        last_kernel, [VMEM] * 5, [jax.ShapeDtypeStruct((k, mine * T), F32), gram_shape], [shl, img], 2
+    )(code, live, thl, *whole, linv)
     scale = float(rows * groups * sketch.shape[0]) ** 0.5
     return call(
-        functools.partial(basis_kernel, scale=scale), [VMEM] * 2, [jax.ShapeDtypeStruct(sketch.shape[::-1], F32)], [], 0, "basis"
+        functools.partial(basis_kernel, scale=scale), [VMEM] * 2, [jax.ShapeDtypeStruct(sketch.shape[::-1], F32)], [], 0
     )(gram_parts(gram), image)[0].T
 
 

time: 189 us -> 185 us (0.979)
  starting transfers between devices: 57.6 us -> 45.5 us
  blocking collectives: 90 us -> 96.9 us
  Pallas kernels: 12.2 us -> 14.7 us
    all_to_all x2 -> x0, starting transfers between devices: 14.4 us -> none  [over_grp(): return lax.all_to_all(x, 'grp', split_axis=0, concat_axis=0, tiled=True)]
    all_to_all x1 -> x2, blocking collectives: 14.2 us -> 26.1 us  [over_grp(): return lax.all_to_all(x, 'grp', split_axis=0, concat_axis=0, tiled=True)]
    ppermute x4, waiting for transfers between devices: 3.09 us -> 11.9 us  [over_outer(): return lax.ppermute(x, ROWS, outer)]
    all_to_all x2 -> x0, waiting for transfers between devices: 8.67 us -> none  [over_grp(): return lax.all_to_all(x, 'grp', split_axis=0, concat_axis=0, tiled=True)]
    ppermute x4, starting transfers between devices: 24.7 us -> 32.3 us  [over_outer(): return lax.ppermute(x, ROWS, outer)]
    all_to_all x6, blocking collectives: 75.7 us -> 70.8 us  [to_everyone(): return lax.all_to_all(copies, axes, split_axis=0, concat_axis=0, tiled=True)]
    all_to_all x2 -> x1, starting transfers between devices: 10.4 us -> 5.55 us  [to_everyone(): return lax.all_to_all(copies, axes, split_axis=0, concat_axis=0, tiled=True)]
    pallas_call x4, Pallas kernels: 9.39 us -> 11.9 us  [the longest x1 4.36 us: local(): call(middle_kernel, [VMEM] * 4, [block_shape] * 3 + [gram_shape], [shl, i...]
  transfers between devices with their start and end apart: 12 -> 9, of which waited for: 6 -> 3; matrix products, arithmetic and copies ran while one was open for 1% -> 0% of each run, Pallas kernels for 1% -> 1%
where the time goes in v3:
time: 185 us; the launch traced here: 184 us
  blocking collectives  96.9 us (52%)
  starting transfers between devices  45.5 us (25%)
  waiting for transfers between devices  20.6 us (11%)
  Pallas kernels  14.7 us (8%)
  local copies, waits for them, and re-layouts  3.55 us (2%)
  other arithmetic  2.19 us (1%)
    all_to_all x6, blocking collectives, to_everyone(): return lax.all_to_all(copies, axes, split_axis=0, concat_axis=0, tiled=True)  70.8 us
    ppermute x4, starting transfers between devices, over_outer(): return lax.ppermute(x, ROWS, outer)  32.3 us
    all_to_all x2, blocking collectives, over_grp(): return lax.all_to_all(x, 'grp', split_axis=0, concat_axis=0, tiled=True)  26.1 us
    ppermute x4, waiting for transfers between devices, over_outer(): return lax.ppermute(x, ROWS, outer)  11.9 us
    all_to_all x1, waiting for transfers between devices, to_everyone(): return lax.all_to_all(copies, axes, split_axis=0, concat_axis=0, tiled=True)  8.69 us
    ppermute x4, starting transfers between devices, over_partner(): return lax.ppermute(x, ROWS, partner)  7.66 us
    all_to_all x1, starting transfers between devices, to_everyone(): return lax.all_to_all(copies, axes, split_axis=0, concat_axis=0, tiled=True)  5.55 us
    pallas_call x1, Pallas kernels, local(): call(middle_kernel, [VMEM] * 4, [block_shape] * 3 + [gram_shape], [shl, i...  4.36 us
  transfers between devices with their start and end apart: 9, of which 3 were waited for; matrix products, arithmetic and copies ran while one was open for 0% of the time, Pallas kernels for 1%

profile of v3, /device:TPU:2, one launch (start us, length us, event | category | flops | bytes accessed | tf_op | source)
XLA Modules:
  0.0 184.4 jit_solution(11142626924929004751)
XLA Ops:
  0.7 0.8 fusion.2.code
  1.4 0.0 copy-start.2
  1.4 0.9 copy-done.2
  2.3 2.6 %shard_map.46 = (f32[16,64,128]{2,1,0:T(8,128)S(1)}, f32[16,64,128]{2,1,0:T(8,128)S(1)}, f32[16,64,128]{2,1,0:T(8,128)S(1)}, bf16[48,256,128]{2,1,0:T(8,128)(2,1)S(1)}) custom-call(s32[48]{0:T(128)S(1)} %fusion.2.code, s32[1]{0:T(128)} %copy.5.live, f32[48,128,128]{2,1,0:T(8,128)} %tiles.1, f32[64,512]{1,0:T(8,128)S(1)} %bitcast.29), custom_call_target="tpu_custom_call" | custom-call | tf_op jit(solution)/shard_map/pallas_call | solution.py:300
  4.9 0.0 copy-start
  5.0 1.6 copy-done
  6.6 14.3 %collective-permute-start = (f32[16,64,128]{2,1,0:T(8,128)S(1)}, f32[16,64,128]{2,1,0:T(8,128)S(1)}, u32[]{:S(2)}, u32[]{:S(2)}) collective-permute-start(f32[16,64,128]{2,1,0:T(8,128)S(1)} %get-tuple-element.19), channel_id=1, source_target_pairs={{0,508},{4,8},{8,4},{12,16},{16,12},{20,24},{24,20},{28,32},{32,28... | collective-permute-start | bytes 1572872 | tf_op jit(solution)/shard_map/ppermute | solution.py:263
  20.9 1.9 %collective-permute-start.1 = (f32[16,64,128]{2,1,0:T(8,128)S(1)}, f32[16,64,128]{2,1,0:T(8,128)S(1)}, u32[]{:S(2)}, u32[]{:S(2)}) collective-permute-start(f32[16,64,128]{2,1,0:T(8,128)S(1)} %get-tuple-element.20), channel_id=1, source_target_pairs={{0,4},{4,0},{8,12},{12,8},{16,20},{20,16},{24,28},{28,24},{32,36},... | collective-permute-start | bytes 1572872 | tf_op jit(solution)/shard_map/ppermute | solution.py:266
  22.8 4.9 %collective-permute-done = f32[16,64,128]{2,1,0:T(8,128)S(1)} collective-permute-done((f32[16,64,128]{2,1,0:T(8,128)S(1)}, f32[16,64,128]{2,1,0:T(8,128)S(1)}, u32[]{:S(2)}, u32[]{:S(2)}) %collective-permute-start) | collective-permute-done | bytes 524320 | tf_op jit(solution)/shard_map/ppermute | solution.py:263
  27.7 0.0 collective-permute-done.1
  27.7 0.1 add_add_fusion.1
  27.8 11.3 %all_to_all.45 = f32[4,4,64,128]{3,2,1,0:T(8,128)S(1)} all-to-all(f32[4,4,64,128]{3,2,1,0:T(8,128)S(1)} %bitcast.31), channel_id=1, replica_groups=mesh['y'=8,'z'=8,'c'=2,'grp'=4] {'grp'}, dimensions={0} | all-to-all | bytes 1048576 | tf_op jit(solution)/shard_map/all_to_all | solution.py:260
  39.2 10.5 %all_to_all.46 = f32[4,4,64,128]{3,2,1,0:T(8,128)S(1)} all-to-all(f32[4,4,64,128]{3,2,1,0:T(8,128)S(1)} %broadcast_in_dim.29), channel_id=1, replica_groups=mesh['y'=8,'z'=8,'c'=2,'grp'=4] {'grp'}, dimensions={0} | all-to-all | bytes 1048576 | tf_op jit(solution)/shard_map/all_to_all | solution.py:212
  49.7 1.9 %collective-permute-start.3 = (f32[16,64,128]{2,1,0:T(8,128)S(1)}, f32[16,64,128]{2,1,0:T(8,128)S(1)}, u32[]{:S(2)}, u32[]{:S(2)}) collective-permute-start(f32[16,64,128]{2,1,0:T(8,128)S(1)} %bitcast.26), channel_id=1, source_target_pairs={{0,4},{4,0},{8,12},{12,8},{16,20},{20,16},{24,28},{28,24},{32,36},... | collective-permute-start | bytes 1572872 | tf_op jit(solution)/shard_map/ppermute | solution.py:266
  51.6 6.8 %collective-permute-start.2 = (f32[16,64,128]{2,1,0:T(8,128)S(1)}, f32[16,64,128]{2,1,0:T(8,128)S(1)}, u32[]{:S(2)}, u32[]{:S(2)}) collective-permute-start(f32[16,64,128]{2,1,0:T(8,128)S(1)} %bitcast.27), channel_id=1, source_target_pairs={{0,508},{4,8},{8,4},{12,16},{16,12},{20,24},{24,20},{28,32},{32,28... | collective-permute-start | bytes 1572872 | tf_op jit(solution)/shard_map/ppermute | solution.py:263
  58.4 0.0 collective-permute-done.3.s_partner
  58.4 7.0 %collective-permute-done.2.s_outer = f32[16,64,128]{2,1,0:T(8,128)S(1)} collective-permute-done((f32[16,64,128]{2,1,0:T(8,128)S(1)}, f32[16,64,128]{2,1,0:T(8,128)S(1)}, u32[]{:S(2)}, u32[]{:S(2)}) %collective-permute-start.2) | collective-permute-done | bytes 524320 | tf_op jit(solution)/shard_map/ppermute | solution.py:263
  65.4 4.4 %shard_map.47 = (f32[16,64,128]{2,1,0:T(8,128)S(1)}, f32[16,64,128]{2,1,0:T(8,128)S(1)}, f32[16,64,128]{2,1,0:T(8,128)S(1)}, f32[32,128]{1,0:T(8,128)S(1)}) custom-call(s32[48]{0:T(128)S(1)} %fusion.2.code, s32[1]{0:T(128)} %copy.5.live, bf16[48,256,128]{2,1,0:T(8,128)(2,1)} %copy-done, f32[16,64,128]{2,1,0:T(8,128)S(1)} %collective-permute-done.2.s_outer, ...), custom_call_target="tpu_custom_call" | custom-call | tf_op jit(solution)/shard_map/pallas_call | solution.py:308
  69.8 8.6 %collective-permute-start.4 = (f32[16,64,128]{2,1,0:T(8,128)S(1)}, f32[16,64,128]{2,1,0:T(8,128)S(1)}, u32[]{:S(2)}, u32[]{:S(2)}) collective-permute-start(f32[16,64,128]{2,1,0:T(8,128)S(1)} %get-tuple-element.22), channel_id=1, source_target_pairs={{0,508},{4,8},{8,4},{12,16},{16,12},{20,24},{24,20},{28,32},{32,28... | collective-permute-start | bytes 1572872 | tf_op jit(solution)/shard_map/ppermute | solution.py:263
  78.4 1.9 %collective-permute-start.5 = (f32[16,64,128]{2,1,0:T(8,128)S(1)}, f32[16,64,128]{2,1,0:T(8,128)S(1)}, u32[]{:S(2)}, u32[]{:S(2)}) collective-permute-start(f32[16,64,128]{2,1,0:T(8,128)S(1)} %get-tuple-element.23), channel_id=1, source_target_pairs={{0,4},{4,0},{8,12},{12,8},{16,20},{20,16},{24,28},{28,24},{32,36},... | collective-permute-start | bytes 1572872 | tf_op jit(solution)/shard_map/ppermute | solution.py:266
  80.3 13.6 %all_to_all.47 = f32[16,32,128]{2,1,0:T(8,128)S(1)} all-to-all(f32[16,32,128]{2,1,0:T(8,128)S(1)} %broadcast_in_dim.30), channel_id=1, replica_groups=mesh['y'=8,'z'=8,'c'=2,'grp'=4] {'z','c'}, dimensions={0} | all-to-all | bytes 524288 | tf_op jit(solution)/shard_map/all_to_all | solution.py:212
  94.0 0.0 collective-permute-done.4
  94.0 0.0 collective-permute-done.5
  94.0 0.1 add_add_fusion
  94.1 0.0 copy-start.1
  94.2 14.8 %all_to_all.48 = f32[4,288,128]{2,1,0:T(8,128)} all-to-all(f32[4,288,128]{2,1,0:T(8,128)S(1)} %pad_maximum_fusion), channel_id=1, replica_groups=mesh['y'=8,'z'=8,'c'=2,'grp'=4] {'grp'}, dimensions={0} | all-to-all | bytes 1179648 | tf_op jit(solution)/shard_map/all_to_all | solution.py:260
  109.0 1.1 reduce_sum.47
  110.1 0.9 broadcast_in_dim.32
  111.0 5.6 %all-to-all-start.4 = ((f32[4,4,64,128]{3,2,1,0:T(8,128)}), f32[4,4,64,128]{3,2,1,0:T(8,128)}, u32[]{:S(2)}, u32[]{:S(2)}) async-start(f32[4,4,64,128]{3,2,1,0:T(8,128)} %broadcast_in_dim.32), calls=%async_computation.4 | async-start | bytes 1048576 | tf_op jit(solution)/shard_map/all_to_all | solution.py:212
  116.5 8.7 %all-to-all-done.4 = f32[4,4,64,128]{3,2,1,0:T(8,128)} async-done(((f32[4,4,64,128]{3,2,1,0:T(8,128)}), f32[4,4,64,128]{3,2,1,0:T(8,128)}, u32[]{:S(2)}, u32[]{:S(2)}) %all-to-all-start.4) | async-done | bytes 524320 | tf_op jit(solution)/shard_map/all_to_all | solution.py:212
  125.2 1.9 %collective-permute-start.7 = (f32[16,64,128]{2,1,0:T(8,128)}, f32[16,64,128]{2,1,0:T(8,128)S(1)}, u32[]{:S(2)}, u32[]{:S(2)}) collective-permute-start(f32[16,64,128]{2,1,0:T(8,128)} %bitcast.8.s_own), channel_id=1, source_target_pairs={{0,4},{4,0},{8,12},{12,8},{16,20},{20,16},{24,28},{28,24},{32,36},... | collective-permute-start | bytes 1572872 | tf_op jit(solution)/shard_map/ppermute | solution.py:266
  127.1 2.6 %collective-permute-start.6 = (f32[16,64,128]{2,1,0:T(8,128)}, f32[16,64,128]{2,1,0:T(8,128)S(1)}, u32[]{:S(2)}, u32[]{:S(2)}) collective-permute-start(f32[16,64,128]{2,1,0:T(8,128)} %bitcast.8.s_own), channel_id=1, source_target_pairs={{0,508},{4,8},{8,4},{12,16},{16,12},{20,24},{24,20},{28,32},{32,28... | collective-permute-start | bytes 1572872 | tf_op jit(solution)/shard_map/ppermute | solution.py:263
  129.8 13.5 %all_to_all.49.parts = f32[8,32,128]{2,1,0:T(8,128)S(1)} all-to-all(f32[8,32,128]{2,1,0:T(8,128)S(1)} %broadcast_in_dim.33), channel_id=1, replica_groups=mesh['y'=8,'z'=8,'c'=2,'grp'=4] {'y'}, dimensions={0} | all-to-all | bytes 262144 | tf_op jit(solution)/shard_map/all_to_all | solution.py:212
  143.3 1.9 %shard_map.48.linv = f32[64,64]{1,0:T(8,128)S(1)} custom-call(f32[8,32,128]{2,1,0:T(8,128)S(1)} %all_to_all.49.parts), custom_call_target="tpu_custom_call" | custom-call | tf_op jit(solution)/shard_map/pallas_call | solution.py:312
  145.1 0.0 collective-permute-done.7.s_partner
  145.1 0.0 collective-permute-done.6.s_outer
  145.1 0.0 copy-done.1
  145.2 3.0 %shard_map.49 = (f32[64,512]{1,0:T(8,128)S(1)}, f32[32,128]{1,0:T(8,128)S(1)}) custom-call(s32[48]{0:T(128)S(1)} %fusion.2.code, s32[1]{0:T(128)} %copy.5.live, bf16[48,256,128]{2,1,0:T(8,128)(2,1)S(1)} %copy-done.1, f32[16,64,128]{2,1,0:T(8,128)S(1)} %collective-permute-done.6.s_outer, f32[16,64,128]{2,1,0:T(8,128)} %bitcast.8.s_own, ...), custom_call_target="tpu_custom_call" | custom-call | tf_op jit(solution)/shard_map/pallas_call | solution.py:313
  148.2 9.2 %all_to_all.50 = f32[8,32,128]{2,1,0:T(8,128)S(1)} all-to-all(f32[8,32,128]{2,1,0:T(8,128)S(1)} %broadcast_in_dim.34), channel_id=1, replica_groups=mesh['y'=8,'z'=8,'c'=2,'grp'=4] {'c','grp'}, dimensions={0} | all-to-all | bytes 262144 | tf_op jit(solution)/shard_map/all_to_all | solution.py:212
  157.5 12.6 %all_to_all.51 = f32[8,32,128]{2,1,0:T(8,128)S(1)} all-to-all(f32[8,32,128]{2,1,0:T(8,128)S(1)} %broadcast_in_dim.35), channel_id=1, replica_groups=mesh['y'=8,'z'=8,'c'=2,'grp'=4] {'z'}, dimensions={0} | all-to-all | bytes 262144 | tf_op jit(solution)/shard_map/all_to_all | solution.py:212
  170.1 11.5 %all_to_all.52.parts = f32[8,32,128]{2,1,0:T(8,128)S(1)} all-to-all(f32[8,32,128]{2,1,0:T(8,128)S(1)} %broadcast_in_dim.36), channel_id=1, replica_groups=mesh['y'=8,'z'=8,'c'=2,'grp'=4] {'y'}, dimensions={0} | all-to-all | bytes 262144 | tf_op jit(solution)/shard_map/all_to_all | solution.py:212
  181.6 2.8 %shard_map.50 = f32[64,512]{1,0:T(8,128)} custom-call(f32[8,32,128]{2,1,0:T(8,128)S(1)} %all_to_all.52.parts, f32[64,512]{1,0:T(8,128)S(1)} %get-tuple-element.28.image), custom_call_target="tpu_custom_call" | custom-call | tf_op jit(solution)/shard_map/pallas_call | solution.py:317
  (14 shorter events, 0.3 us)
Async XLA Ops:
  1.4 0.9 copy-start.2
  4.9 1.7 copy-start
  6.6 21.1 %collective-permute-start = (f32[16,64,128]{2,1,0:T(8,128)S(1)}, f32[16,64,128]{2,1,0:T(8,128)S(1)}, u32[]{:S(2)}, u32[]{:S(2)}) collective-permute-start(f32[16,64,128]{2,1,0:T(8,128)S(1)} %get-tuple-element.19), channel_id=1, source_target_pairs={{0,508},{4,8},{8,4},{12,16},{16,12},{20,24},{24,20},{28,32},{32,28... | collective-permute-start | bytes 1572872 | tf_op jit(solution)/shard_map/ppermute | solution.py:263
  20.9 6.9 %collective-permute-start.1 = (f32[16,64,128]{2,1,0:T(8,128)S(1)}, f32[16,64,128]{2,1,0:T(8,128)S(1)}, u32[]{:S(2)}, u32[]{:S(2)}) collective-permute-start(f32[16,64,128]{2,1,0:T(8,128)S(1)} %get-tuple-element.20), channel_id=1, source_target_pairs={{0,4},{4,0},{8,12},{12,8},{16,20},{20,16},{24,28},{28,24},{32,36},... | collective-permute-start | bytes 1572872 | tf_op jit(solution)/shard_map/ppermute | solution.py:266
  49.7 8.7 %collective-permute-start.3 = (f32[16,64,128]{2,1,0:T(8,128)S(1)}, f32[16,64,128]{2,1,0:T(8,128)S(1)}, u32[]{:S(2)}, u32[]{:S(2)}) collective-permute-start(f32[16,64,128]{2,1,0:T(8,128)S(1)} %bitcast.26), channel_id=1, source_target_pairs={{0,4},{4,0},{8,12},{12,8},{16,20},{20,16},{24,28},{28,24},{32,36},... | collective-permute-start | bytes 1572872 | tf_op jit(solution)/shard_map/ppermute | solution.py:266
  51.6 13.8 %collective-permute-start.2 = (f32[16,64,128]{2,1,0:T(8,128)S(1)}, f32[16,64,128]{2,1,0:T(8,128)S(1)}, u32[]{:S(2)}, u32[]{:S(2)}) collective-permute-start(f32[16,64,128]{2,1,0:T(8,128)S(1)} %bitcast.27), channel_id=1, source_target_pairs={{0,508},{4,8},{8,4},{12,16},{16,12},{20,24},{24,20},{28,32},{32,28... | collective-permute-start | bytes 1572872 | tf_op jit(solution)/shard_map/ppermute | solution.py:263
  69.8 24.2 %collective-permute-start.4 = (f32[16,64,128]{2,1,0:T(8,128)S(1)}, f32[16,64,128]{2,1,0:T(8,128)S(1)}, u32[]{:S(2)}, u32[]{:S(2)}) collective-permute-start(f32[16,64,128]{2,1,0:T(8,128)S(1)} %get-tuple-element.22), channel_id=1, source_target_pairs={{0,508},{4,8},{8,4},{12,16},{16,12},{20,24},{24,20},{28,32},{32,28... | collective-permute-start | bytes 1572872 | tf_op jit(solution)/shard_map/ppermute | solution.py:263
  78.4 15.6 %collective-permute-start.5 = (f32[16,64,128]{2,1,0:T(8,128)S(1)}, f32[16,64,128]{2,1,0:T(8,128)S(1)}, u32[]{:S(2)}, u32[]{:S(2)}) collective-permute-start(f32[16,64,128]{2,1,0:T(8,128)S(1)} %get-tuple-element.23), channel_id=1, source_target_pairs={{0,4},{4,0},{8,12},{12,8},{16,20},{20,16},{24,28},{28,24},{32,36},... | collective-permute-start | bytes 1572872 | tf_op jit(solution)/shard_map/ppermute | solution.py:266
  94.1 51.1 %copy-start.1 = (bf16[48,256,128]{2,1,0:T(8,128)(2,1)S(1)}, bf16[48,256,128]{2,1,0:T(8,128)(2,1)}, u32[]{:S(2)}) copy-start(bf16[48,256,128]{2,1,0:T(8,128)(2,1)} %copy-done) | copy-start | bytes 9437188
  111.0 14.2 %all-to-all-start.4 = ((f32[4,4,64,128]{3,2,1,0:T(8,128)}), f32[4,4,64,128]{3,2,1,0:T(8,128)}, u32[]{:S(2)}, u32[]{:S(2)}) async-start(f32[4,4,64,128]{3,2,1,0:T(8,128)} %broadcast_in_dim.32), calls=%async_computation.4 | async-start | bytes 1048576 | tf_op jit(solution)/shard_map/all_to_all | solution.py:212
  125.2 19.9 %collective-permute-start.7 = (f32[16,64,128]{2,1,0:T(8,128)}, f32[16,64,128]{2,1,0:T(8,128)S(1)}, u32[]{:S(2)}, u32[]{:S(2)}) collective-permute-start(f32[16,64,128]{2,1,0:T(8,128)} %bitcast.8.s_own), channel_id=1, source_target_pairs={{0,4},{4,0},{8,12},{12,8},{16,20},{20,16},{24,28},{28,24},{32,36},... | collective-permute-start | bytes 1572872 | tf_op jit(solution)/shard_map/ppermute | solution.py:266
  127.1 18.0 %collective-permute-start.6 = (f32[16,64,128]{2,1,0:T(8,128)}, f32[16,64,128]{2,1,0:T(8,128)S(1)}, u32[]{:S(2)}, u32[]{:S(2)}) collective-permute-start(f32[16,64,128]{2,1,0:T(8,128)} %bitcast.8.s_own), channel_id=1, source_target_pairs={{0,508},{4,8},{8,4},{12,16},{16,12},{20,24},{24,20},{28,32},{32,28... | collective-permute-start | bytes 1572872 | tf_op jit(solution)/shard_map/ppermute | solution.py:263

commit v4 on v3

v4 whole, which is shorter than its diff:
```python
import functools

import jax
import jax.numpy as jnp
from jax import lax
from jax.experimental import pallas as pl
from jax.experimental.pallas import tpu as pltpu
from jax.sharding import Mesh
from jax.sharding import PartitionSpec as P


ROWS = ("y", "z", "c")
ROWS_GRP = ("y", "z", "c", "grp")
HIGHEST = lax.Precision.HIGHEST
F32 = jnp.float32
BF16 = jnp.bfloat16
T = 128
CHUNK = 8
VMEM_LIMIT = 50 * 1024 * 1024


def dot(a, b, contract, precision=None):
    return lax.dot_general(
        a, b, ((contract[:1], contract[1:]), ((), ())), precision=precision, preferred_element_type=F32
    )


def halves(x):
    hi = x.astype(BF16)
    return hi, (x - hi.astype(F32)).astype(BF16)


def fold(q, k):
    return (q[:k, :T] + q[k:, T:]) + (q[k:, :T] + q[:k, T:])


def tile_copy(c, tiles, tbuf, sems):
    at = pl.ds(c * CHUNK, CHUNK)
    return pltpu.make_async_copy(tiles.at[at], tbuf.at[at], sems.at[c])


def start_tiles(live, tiles, tbuf, sems):
    for c in range(tiles.shape[0] // CHUNK):

        @pl.when(c * CHUNK < live)
        def _():
            tile_copy(c, tiles, tbuf, sems).start()


def each_chunk(live, cap, work, ready=None):
    for c in range(cap // CHUNK):

        @pl.when(c * CHUNK < live)
        def _():
            if ready is not None:
                ready(c)
            for s in range(c * CHUNK, (c + 1) * CHUNK):
                work(s)


def keep_panel(panel, k, phl):
    for t in range(phl.shape[0]):
        hi, lo = halves(panel(t))
        phl[t, :k, :] = hi
        phl[t, k:, :] = lo


def spread_slot(entry, hi, lo, phl, acc):
    k = phl.shape[1] // 2
    at = entry & 255
    q = dot(phl[entry >> 8], jnp.concatenate([hi, lo], axis=1), (1, 0))
    acc[at] += fold(q, k)


def put_spread(acc, outs):
    each = outs[0].shape[0]
    for n, out in enumerate(outs):
        out[...] = acc[n * each : (n + 1) * each]


def slot_code(s, coords, live, block, mine, rows):
    odd = lax.axis_index("c")
    row = (lax.axis_index("y") * lax.axis_size("z") + lax.axis_index("z")) * 2 + odd
    column = coords[1, s]
    step = lax.rem(lax.div(column, block) - row + 1 + rows, rows)
    step = jnp.where(odd == 1, 2 - step, step)
    place = jnp.where(s < live, step * block + lax.rem(column, block), 3 * block)
    return place + 256 * lax.rem(coords[0, s], mine)


def first_kernel(
    coords, live, tiles, sketch, outer, own, partner, code, tbuf, panel, phl, acc, sems, panel_sem, *, rows
):
    cap = tiles.shape[0]
    k = sketch.shape[0]
    panel_copy = pltpu.make_async_copy(sketch, panel, panel_sem)
    panel_copy.start()
    start_tiles(live[0], tiles, tbuf, sems)
    acc[...] = jnp.zeros_like(acc)
    for s in range(cap):
        code[s] = slot_code(s, coords, live[0], outer.shape[0], phl.shape[0], rows)
    panel_copy.wait()
    keep_panel(lambda t: panel[:, t * T : (t + 1) * T], k, phl)
    each_chunk(
        live[0],
        cap,
        lambda s: spread_slot(code[s], *halves(tbuf[s]), phl, acc),
        lambda c: tile_copy(c, tiles, tbuf, sems).wait(),
    )
    put_spread(acc, (outer, own, partner))


def keep_spread(parts, shl):
    k = parts[0].shape[1]
    each = parts[0].shape[0]
    for n, part in enumerate(parts):

        def one(i, carry, part=part, n=n):
            hi, lo = halves(part[i])
            shl[n * each + i, :k, :] = hi
            shl[n * each + i, k:, :] = lo
            return carry

        lax.fori_loop(0, each, one, 0, unroll=4)
    shl[3 * each] = jnp.zeros_like(shl[3 * each])


def image_slot(entry, hi, lo, shl, img):
    k = shl.shape[1] // 2
    q = dot(shl[entry & 255], jnp.concatenate([hi, lo], axis=0), (1, 1))
    img[entry >> 8] += fold(q, k)


def whole_image(img):
    return jnp.concatenate([img[t] for t in range(img.shape[0])], axis=1)


def put_gram(image, out):
    g = dot(image, image, (1, 1), HIGHEST)
    h = g.shape[0] // 2
    quarters = (g[:h, :h], g[:h, h:], g[h:, h:])
    packed = jnp.concatenate(
        [jnp.concatenate([q[8 * r : 8 * r + 8] for r in range(h // 8)], axis=1) for q in quarters], axis=0
    )
    for n in range(out.shape[0]):
        out[n] = packed


def middle_kernel(
    code, live, tiles, s_outer, s_own, s_partner, outer, own, partner, gram,
    tbuf, thl, shl, img, phl, acc, sems,
):
    cap = tiles.shape[0]
    k = s_own.shape[1]
    start_tiles(live[0], tiles, tbuf, sems)
    keep_spread((s_outer, s_own, s_partner), shl)
    img[...] = jnp.zeros_like(img)
    acc[...] = jnp.zeros_like(acc)

    def forth(s):
        hi, lo = halves(tbuf[s])
        thl[s, :T, :] = hi
        thl[s, T:, :] = lo
        image_slot(code[s], hi, lo, shl, img)

    each_chunk(live[0], cap, forth, lambda c: tile_copy(c, tiles, tbuf, sems).wait())
    put_gram(whole_image(img), gram)
    keep_panel(lambda t: img[t], k, phl)
    each_chunk(live[0], cap, lambda s: spread_slot(code[s], thl[s, :T, :], thl[s, T:, :], phl, acc))
    put_spread(acc, (outer, own, partner))


def share_kernel(pieces, whole, gram):
    rows = whole.shape[1]
    total = pieces[0]
    for n in range(1, pieces.shape[0]):
        total = total + pieces[n]
    for n in range(whole.shape[0]):
        whole[n] = total[:rows]
    for n in range(gram.shape[0]):
        gram[n] = total[rows:]


def inverse_factor(g):
    k = g.shape[0]
    row_id = lax.broadcasted_iota(jnp.int32, (8, 2 * k), 0)
    eye = (lax.broadcasted_iota(jnp.int32, (k, k), 0) == lax.broadcasted_iota(jnp.int32, (k, k), 1)).astype(F32)
    full = jnp.concatenate([g, eye], axis=1)
    m = [full[8 * j : 8 * j + 8] for j in range(k // 8)]

    def row_of(x, r):
        return jnp.broadcast_to(x[r : r + 1, :], x.shape)

    for j in range(k // 8):
        rows = [row_of(m[j], t) for t in range(8)]
        cols = [
            {i: jnp.broadcast_to(m[i][:, 8 * j + t : 8 * j + t + 1], (8, 2 * k)) for i in range(j, k // 8)}
            for t in range(8)
        ]
        scale = jnp.zeros((8, 2 * k), F32)
        for t in range(8):
            pivot = row_of(cols[t][j], t)
            scale = jnp.where(row_id == t, lax.rsqrt(pivot), scale)
            inv = 1.0 / pivot
            q = rows[t] * inv
            cols[t][j] = jnp.where(row_id > t, cols[t][j], 0.0)
            for u in range(t + 1, 8):
                part = row_of(cols[t][j], u)
                f = part * inv
                rows[u] = rows[u] - part * q
                for i in range(j, k // 8):
                    cols[u][i] = cols[u][i] - cols[t][i] * f
            for i in range(j, k // 8):
                m[i] = m[i] - cols[t][i] * q
        m[j] = m[j] * scale
    return jnp.concatenate([x[:, k:] for x in m], axis=0)


def summed_gram(parts, k):
    packed = parts[0]
    for n in range(1, parts.shape[0]):
        packed = packed + parts[n]
    h = k // 2
    ul, ur, lr = (
        jnp.concatenate([packed[8 * q : 8 * q + 8, h * r : h * r + h] for r in range(h // 8)], axis=0) for q in range(3)
    )
    return jnp.concatenate([jnp.concatenate([ul, ur], axis=1), jnp.concatenate([ur.T, lr], axis=1)], axis=0)


def factor_kernel(parts, linv):
    linv[...] = inverse_factor(summed_gram(parts, linv.shape[0]))


def last_kernel(code, live, tiles, s_outer, s_own, s_partner, linv, image, gram, tbuf, shl, img, sems):
    start_tiles(live[0], tiles, tbuf, sems)
    keep_spread((s_outer, s_own, s_partner), shl)
    img[...] = jnp.zeros_like(img)
    each_chunk(
        live[0],
        tiles.shape[0],
        lambda s: image_slot(code[s], *halves(tbuf[s]), shl, img),
        lambda c: tile_copy(c, tiles, tbuf, sems).wait(),
    )
    x = dot(linv[...], whole_image(img), (1, 0), HIGHEST)
    image[...] = x
    put_gram(x, gram)


def basis_kernel(parts, image, basis, *, scale):
    linv = inverse_factor(summed_gram(parts, image.shape[0]))
    basis[...] = dot(linv, image[...], (1, 0), HIGHEST) * scale


def swapped(copies, axes):
    return lax.all_to_all(copies, axes, split_axis=0, concat_axis=0, tiled=True)


def to_everyone(x, axes):
    return swapped(jnp.broadcast_to(x, (lax.axis_size(axes), *x.shape)), axes)


VMEM = pl.BlockSpec(memory_space=pltpu.VMEM)
SMEM = pl.BlockSpec(memory_space=pltpu.SMEM)
HBM = pl.BlockSpec(memory_space=pltpu.HBM)


def call(kernel, ins, outs, scratch=(), prefetch=0, out_specs=None, limit=VMEM_LIMIT):
    return pl.pallas_call(
        kernel,
        grid_spec=pltpu.PrefetchScalarGridSpec(
            num_scalar_prefetch=prefetch,
            grid=(),
            in_specs=ins,
            out_specs=out_specs or [VMEM] * len(outs),
            scratch_shapes=scratch,
        ),
        out_shape=[jax.ShapeDtypeStruct(shape, dtype) for shape, dtype in outs],
        compiler_params=pltpu.CompilerParams(vmem_limit_bytes=limit),
    )


def local(tiles, coords, live, sketch):
    rows = lax.axis_size(ROWS)
    groups = lax.axis_size("grp")
    cap = tiles.shape[0]
    k = sketch.shape[1]
    mine = sketch.shape[0] // T
    block = groups * mine
    packed = (3 * 8, T)

    outer = [(r, (r - 1) % rows if r % 2 == 0 else (r + 1) % rows) for r in range(rows)]
    partner = [(r, r ^ 1) for r in range(rows)]

    tbuf = pltpu.VMEM((cap, T, T), F32)
    thl = pltpu.VMEM((cap, 2 * T, T), BF16)
    panel = pltpu.VMEM((k, mine * T), F32)
    phl = pltpu.VMEM((mine, 2 * k, T), BF16)
    shl = pltpu.VMEM((3 * block + 1, 2 * k, T), BF16)
    acc = pltpu.VMEM((3 * block + 1, k, T), F32)
    img = pltpu.VMEM((mine, k, T), F32)
    sems = pltpu.SemaphoreType.DMA((cap // CHUNK,))
    block_out = ((block, k, T), F32)

    def over_pairs(to_outer, to_partner):
        got_outer = lax.ppermute(to_outer, ROWS, outer)
        got_partner = lax.ppermute(to_partner, ROWS, partner)
        return got_outer, got_partner

    def pieces(x):
        return x.reshape(groups, mine * k, T)

    def exchange(parts):
        p_outer, p_own, p_partner = parts
        got_outer, got = over_pairs(p_outer, p_partner)
        total = p_own + got_outer + got
        own = to_everyone(swapped(pieces(total), "grp").sum(axis=0), "grp").reshape(block, k, T)
        at_outer, at_partner = over_pairs(own, own)
        return at_outer, own, at_partner

    def exchange_with_gram(parts, gram):
        p_outer, p_own, p_partner = parts
        gram = swapped(gram, ("z", "c"))
        got_outer, got = over_pairs(p_outer, p_partner)
        total = pieces(p_own + got_outer + got)
        sides = jnp.broadcast_to(gram.sum(axis=0), (groups, *packed))
        arrived = swapped(jnp.concatenate([total, sides], axis=1), "grp")
        copies, gram = call(
            share_kernel, [VMEM], [((groups, mine * k, T), F32), ((lax.axis_size("y"), *packed), F32)]
        )(arrived)
        own = swapped(copies, "grp").reshape(block, k, T)
        own, gram = lax.optimization_barrier((own, gram))
        gram = swapped(gram, "y")
        at_outer, at_partner = over_pairs(own, own)
        return (at_outer, own, at_partner), gram

    *parts, code = call(
        functools.partial(first_kernel, rows=rows),
        [HBM, HBM],
        [block_out] * 3 + [((cap,), jnp.int32)],
        [tbuf, panel, phl, acc, sems, pltpu.SemaphoreType.DMA],
        2,
        [VMEM] * 3 + [SMEM],
    )(coords.T, live, tiles, sketch.T)
    whole = exchange(parts)
    *parts, gram = call(
        middle_kernel,
        [HBM] + [VMEM] * 3,
        [block_out] * 3 + [((2 * lax.axis_size("z"), *packed), F32)],
        [tbuf, thl, shl, img, phl, acc, sems],
        2,
    )(code, live, tiles, *whole)
    whole, gram = exchange_with_gram(parts, gram)
    linv = call(factor_kernel, [VMEM], [((k, k), F32)])(gram)[0]
    image, gram = call(
        last_kernel, [HBM] + [VMEM] * 4, [((k, mine * T), F32), ((2 * groups, *packed), F32)], [tbuf, shl, img, sems], 2
    )(code, live, tiles, *whole, linv)
    gram = to_everyone(swapped(gram, ("c", "grp")).sum(axis=0), "z").sum(axis=0)
    scale = float(rows * groups * sketch.shape[0]) ** 0.5
    return call(
        functools.partial(basis_kernel, scale=scale), [VMEM] * 2, [(sketch.shape[::-1], F32)]
    )(to_everyone(gram, "y"), image)[0].T


def solution(mesh):
    finer = Mesh(mesh.devices.reshape(8, 8, 2, mesh.shape["grp"]), ROWS_GRP)
    placed = (P(ROWS_GRP, None, None), P(ROWS_GRP, None), P(ROWS_GRP), P(ROWS_GRP, None))
    return jax.shard_map(local, mesh=finer, in_specs=placed, out_specs=P(ROWS_GRP, None), check_vma=False)
```

time: 185 us -> 175 us (0.946)
  waiting for transfers between devices: 20.6 us -> 11.9 us
  blocking collectives: 96.9 us -> 105 us
  starting transfers between devices: 45.5 us -> 40.2 us
  local copies, waits for them, and re-layouts: 3.55 us -> 1.63 us
  other arithmetic: 2.19 us -> 0.32 us
    all_to_all x1 -> x0, waiting for transfers between devices: 8.69 us -> none  [to_everyone(): return lax.all_to_all(copies, axes, split_axis=0, concat_axis=0, tiled=True)]
    all_to_all x8 -> x9, blocking collectives: 96.9 us -> 105 us  [swapped(): return lax.all_to_all(copies, axes, split_axis=0, concat_axis=0, tiled=True)]
    all_to_all x1 -> x0, starting transfers between devices: 5.55 us -> none  [to_everyone(): return lax.all_to_all(copies, axes, split_axis=0, concat_axis=0, tiled=True)]
    pallas_call x5 -> x6, Pallas kernels: 14.7 us -> 14.2 us  [the longest x1 3.3 us: local(): call(middle_kernel, [HBM] + [VMEM] * 3, [block_out] * 3 + [((2 * lax.axis...]
  transfers between devices with their start and end apart: 9 -> 8, of which waited for: 3 -> 2; matrix products, arithmetic and copies ran while one was open for 0% -> 0% of each run, Pallas kernels for 1% -> 1%
where the time goes in v4:
time: 175 us; the launch traced here: 174 us
  blocking collectives  105 us (60%)
  starting transfers between devices  40.2 us (23%)
  Pallas kernels  14.2 us (8%)
  waiting for transfers between devices  11.9 us (7%)
    all_to_all x9, blocking collectives, swapped(): return lax.all_to_all(copies, axes, split_axis=0, concat_axis=0, tiled=True)  105 us
    ppermute x4, starting transfers between devices, over_pairs(): got_outer = lax.ppermute(to_outer, ROWS, outer)  32.5 us
    ppermute x4, waiting for transfers between devices, over_pairs(): got_outer = lax.ppermute(to_outer, ROWS, outer)  11.9 us
    ppermute x4, starting transfers between devices, over_pairs(): got_partner = lax.ppermute(to_partner, ROWS, partner)  7.66 us
  transfers between devices with their start and end apart: 8, of which 2 were waited for; matrix products, arithmetic and copies ran while one was open for 0% of the time, Pallas kernels for 1%

profile of v4, /device:TPU:2, one launch (start us, length us, event | category | flops | bytes accessed | tf_op | source)
XLA Modules:
  0.0 174.1 jit_solution(12490804937256324369)
XLA Ops:
  0.7 0.0 copy-start
  0.7 0.9 copy-done
  1.6 0.0 copy-start.1
  1.6 0.7 copy-done.1
  2.2 3.0 %shard_map.46 = (f32[16,64,128]{2,1,0:T(8,128)S(1)}, f32[16,64,128]{2,1,0:T(8,128)S(1)}, f32[16,64,128]{2,1,0:T(8,128)S(1)}, s32[48]{0:T(128)S(1)}) custom-call(s32[2,48]{1,0:T(2,128)S(1)} %bitcast.14, s32[1]{0:T(128)S(6)} %copy.5.live, f32[48,128,128]{2,1,0:T(8,128)} %tiles.5, f32[64,512]{1,0:T(8,128)S(1)} %bitcast.13), custom_call_target="tpu_custom_call" | custom-call | tf_op jit(solution)/shard_map/pallas_call | solution.py:336
  5.3 14.2 %collective-permute-start = (f32[16,64,128]{2,1,0:T(8,128)S(1)}, f32[16,64,128]{2,1,0:T(8,128)S(1)}, u32[]{:S(2)}, u32[]{:S(2)}) collective-permute-start(f32[16,64,128]{2,1,0:T(8,128)S(1)} %get-tuple-element.21), channel_id=1, source_target_pairs={{0,508},{4,8},{8,4},{12,16},{16,12},{20,24},{24,20},{28,32},{32,28... | collective-permute-start | bytes 1572872 | tf_op jit(solution)/shard_map/ppermute | solution.py:305
  19.4 1.9 %collective-permute-start.1 = (f32[16,64,128]{2,1,0:T(8,128)S(1)}, f32[16,64,128]{2,1,0:T(8,128)S(1)}, u32[]{:S(2)}, u32[]{:S(2)}) collective-permute-start(f32[16,64,128]{2,1,0:T(8,128)S(1)} %get-tuple-element.22), channel_id=1, source_target_pairs={{0,4},{4,0},{8,12},{12,8},{16,20},{20,16},{24,28},{28,24},{32,36},... | collective-permute-start | bytes 1572872 | tf_op jit(solution)/shard_map/ppermute | solution.py:306
  21.4 4.9 %collective-permute-done = f32[16,64,128]{2,1,0:T(8,128)S(1)} collective-permute-done((f32[16,64,128]{2,1,0:T(8,128)S(1)}, f32[16,64,128]{2,1,0:T(8,128)S(1)}, u32[]{:S(2)}, u32[]{:S(2)}) %collective-permute-start) | collective-permute-done | bytes 524320 | tf_op jit(solution)/shard_map/ppermute | solution.py:305
  26.3 0.0 collective-permute-done.1
  26.3 0.1 add_add_fusion.1
  26.4 11.3 %all_to_all.45 = f32[4,256,128]{2,1,0:T(8,128)S(1)} all-to-all(f32[4,256,128]{2,1,0:T(8,128)S(1)} %bitcast.16), channel_id=1, replica_groups=mesh['y'=8,'z'=8,'c'=2,'grp'=4] {'grp'}, dimensions={0} | all-to-all | bytes 1048576 | tf_op jit(solution)/shard_map/all_to_all | solution.py:255
  37.7 10.5 %all_to_all.46 = f32[4,256,128]{2,1,0:T(8,128)S(1)} all-to-all(f32[4,256,128]{2,1,0:T(8,128)S(1)} %broadcast_in_dim.12), channel_id=1, replica_groups=mesh['y'=8,'z'=8,'c'=2,'grp'=4] {'grp'}, dimensions={0} | all-to-all | bytes 1048576 | tf_op jit(solution)/shard_map/all_to_all | solution.py:255
  48.2 1.9 %collective-permute-start.3 = (f32[16,64,128]{2,1,0:T(8,128)S(1)}, f32[16,64,128]{2,1,0:T(8,128)S(1)}, u32[]{:S(2)}, u32[]{:S(2)}) collective-permute-start(f32[16,64,128]{2,1,0:T(8,128)S(1)} %bitcast.7), channel_id=1, source_target_pairs={{0,4},{4,0},{8,12},{12,8},{16,20},{20,16},{24,28},{28,24},{32,36},... | collective-permute-start | bytes 1572872 | tf_op jit(solution)/shard_map/ppermute | solution.py:306
  50.1 6.8 %collective-permute-start.2 = (f32[16,64,128]{2,1,0:T(8,128)S(1)}, f32[16,64,128]{2,1,0:T(8,128)S(1)}, u32[]{:S(2)}, u32[]{:S(2)}) collective-permute-start(f32[16,64,128]{2,1,0:T(8,128)S(1)} %bitcast.8), channel_id=1, source_target_pairs={{0,508},{4,8},{8,4},{12,16},{16,12},{20,24},{24,20},{28,32},{32,28... | collective-permute-start | bytes 1572872 | tf_op jit(solution)/shard_map/ppermute | solution.py:305
  56.9 0.0 collective-permute-done.3.s_partner
  57.0 7.0 %collective-permute-done.2.s_outer = f32[16,64,128]{2,1,0:T(8,128)S(1)} collective-permute-done((f32[16,64,128]{2,1,0:T(8,128)S(1)}, f32[16,64,128]{2,1,0:T(8,128)S(1)}, u32[]{:S(2)}, u32[]{:S(2)}) %collective-permute-start.2) | collective-permute-done | bytes 524320 | tf_op jit(solution)/shard_map/ppermute | solution.py:305
  63.9 3.3 %shard_map.47 = (f32[16,64,128]{2,1,0:T(8,128)S(1)}, f32[16,64,128]{2,1,0:T(8,128)S(1)}, f32[16,64,128]{2,1,0:T(8,128)S(1)}, f32[16,24,128]{2,1,0:T(8,128)S(1)}) custom-call(s32[48]{0:T(128)S(1)} %get-tuple-element.19.code, s32[1]{0:T(128)S(6)} %copy.5.live, f32[48,128,128]{2,1,0:T(8,128)} %tiles.5, f32[16,64,128]{2,1,0:T(8,128)S(1)} %collective-permute-done.2.s_outer, ...), custom_call_target="tpu_custom_call" | custom-call | tf_op jit(solution)/shard_map/pallas_call | solution.py:345
  67.3 8.6 %collective-permute-start.4 = (f32[16,64,128]{2,1,0:T(8,128)S(1)}, f32[16,64,128]{2,1,0:T(8,128)S(1)}, u32[]{:S(2)}, u32[]{:S(2)}) collective-permute-start(f32[16,64,128]{2,1,0:T(8,128)S(1)} %get-tuple-element.24), channel_id=1, source_target_pairs={{0,508},{4,8},{8,4},{12,16},{16,12},{20,24},{24,20},{28,32},{32,28... | collective-permute-start | bytes 1572872 | tf_op jit(solution)/shard_map/ppermute | solution.py:305
  75.9 1.9 %collective-permute-start.5 = (f32[16,64,128]{2,1,0:T(8,128)S(1)}, f32[16,64,128]{2,1,0:T(8,128)S(1)}, u32[]{:S(2)}, u32[]{:S(2)}) collective-permute-start(f32[16,64,128]{2,1,0:T(8,128)S(1)} %get-tuple-element.25), channel_id=1, source_target_pairs={{0,4},{4,0},{8,12},{12,8},{16,20},{20,16},{24,28},{28,24},{32,36},... | collective-permute-start | bytes 1572872 | tf_op jit(solution)/shard_map/ppermute | solution.py:306
  77.8 12.4 %all_to_all.47 = f32[16,24,128]{2,1,0:T(8,128)S(1)} all-to-all(f32[16,24,128]{2,1,0:T(8,128)S(1)} %get-tuple-element.26), channel_id=1, replica_groups=mesh['y'=8,'z'=8,'c'=2,'grp'=4] {'z','c'}, dimensions={0} | all-to-all | bytes 393216 | tf_op jit(solution)/shard_map/all_to_all | solution.py:255
  90.2 0.0 collective-permute-done.4
  90.2 0.0 collective-permute-done.5
  90.2 0.1 add_add_fusion
  90.4 13.6 %all_to_all.48.pieces = f32[4,280,128]{2,1,0:T(8,128)S(1)} all-to-all(f32[4,280,128]{2,1,0:T(8,128)S(1)} %pad_maximum_fusion), channel_id=1, replica_groups=mesh['y'=8,'z'=8,'c'=2,'grp'=4] {'grp'}, dimensions={0} | all-to-all | bytes 1146880 | tf_op jit(solution)/shard_map/all_to_all | solution.py:255
  104.1 12.1 %all_to_all.49 = f32[4,256,128]{2,1,0:T(8,128)S(1)} all-to-all(f32[4,256,128]{2,1,0:T(8,128)S(1)} %get-tuple-element.27), channel_id=1, replica_groups=mesh['y'=8,'z'=8,'c'=2,'grp'=4] {'grp'}, dimensions={0} | all-to-all | bytes 1048576 | tf_op jit(solution)/shard_map/all_to_all | solution.py:255
  116.2 1.9 %collective-permute-start.7 = (f32[16,64,128]{2,1,0:T(8,128)S(1)}, f32[16,64,128]{2,1,0:T(8,128)S(1)}, u32[]{:S(2)}, u32[]{:S(2)}) collective-permute-start(f32[16,64,128]{2,1,0:T(8,128)S(1)} %bitcast.10), channel_id=1, source_target_pairs={{0,4},{4,0},{8,12},{12,8},{16,20},{20,16},{24,28},{28,24},{32,36},... | collective-permute-start | bytes 1572872 | tf_op jit(solution)/shard_map/ppermute | solution.py:306
  118.1 2.9 %collective-permute-start.6 = (f32[16,64,128]{2,1,0:T(8,128)S(1)}, f32[16,64,128]{2,1,0:T(8,128)S(1)}, u32[]{:S(2)}, u32[]{:S(2)}) collective-permute-start(f32[16,64,128]{2,1,0:T(8,128)S(1)} %bitcast.11), channel_id=1, source_target_pairs={{0,508},{4,8},{8,4},{12,16},{16,12},{20,24},{24,20},{28,32},{32,28... | collective-permute-start | bytes 1572872 | tf_op jit(solution)/shard_map/ppermute | solution.py:305
  121.0 13.1 %all_to_all.50.parts = f32[8,24,128]{2,1,0:T(8,128)S(1)} all-to-all(f32[8,24,128]{2,1,0:T(8,128)S(1)} %get-tuple-element.30), channel_id=1, replica_groups=mesh['y'=8,'z'=8,'c'=2,'grp'=4] {'y'}, dimensions={0} | all-to-all | bytes 196608 | tf_op jit(solution)/shard_map/all_to_all | solution.py:255
  134.2 2.0 %shard_map.49.linv = f32[64,64]{1,0:T(8,128)S(1)} custom-call(f32[8,24,128]{2,1,0:T(8,128)S(1)} %all_to_all.50.parts), custom_call_target="tpu_custom_call" | custom-call | tf_op jit(solution)/shard_map/pallas_call | solution.py:353
  136.2 0.0 collective-permute-done.7.s_partner
  136.2 0.0 collective-permute-done.6.s_outer
  136.2 2.9 %shard_map.50 = (f32[64,512]{1,0:T(8,128)S(1)}, f32[8,24,128]{2,1,0:T(8,128)S(1)}) custom-call(s32[48]{0:T(128)S(1)} %get-tuple-element.19.code, s32[1]{0:T(128)S(6)} %copy.5.live, f32[48,128,128]{2,1,0:T(8,128)} %tiles.5, f32[16,64,128]{2,1,0:T(8,128)S(1)} %collective-permute-done.6.s_outer, f32[16,64,128]{2,1,0:T(8,128)S(1)} %bitcast.12, ...), custom_call_target="tpu_custom_call" | custom-call | tf_op jit(solution)/shard_map/pallas_call | solution.py:354
  139.1 9.0 %all_to_all.51 = f32[8,24,128]{2,1,0:T(8,128)S(1)} all-to-all(f32[8,24,128]{2,1,0:T(8,128)S(1)} %get-tuple-element.31), channel_id=1, replica_groups=mesh['y'=8,'z'=8,'c'=2,'grp'=4] {'c','grp'}, dimensions={0} | all-to-all | bytes 196608 | tf_op jit(solution)/shard_map/all_to_all | solution.py:255
  148.1 11.9 %all_to_all.52 = f32[8,24,128]{2,1,0:T(8,128)S(1)} all-to-all(f32[8,24,128]{2,1,0:T(8,128)S(1)} %broadcast_in_dim.14), channel_id=1, replica_groups=mesh['y'=8,'z'=8,'c'=2,'grp'=4] {'z'}, dimensions={0} | all-to-all | bytes 196608 | tf_op jit(solution)/shard_map/all_to_all | solution.py:255
  160.0 11.1 %all_to_all.53.parts = f32[8,24,128]{2,1,0:T(8,128)S(1)} all-to-all(f32[8,24,128]{2,1,0:T(8,128)S(1)} %broadcast_in_dim.15), channel_id=1, replica_groups=mesh['y'=8,'z'=8,'c'=2,'grp'=4] {'y'}, dimensions={0} | all-to-all | bytes 196608 | tf_op jit(solution)/shard_map/all_to_all | solution.py:255
  171.1 2.9 %shard_map.51 = f32[64,512]{1,0:T(8,128)} custom-call(f32[8,24,128]{2,1,0:T(8,128)S(1)} %all_to_all.53.parts, f32[64,512]{1,0:T(8,128)S(1)} %get-tuple-element.32.image), custom_call_target="tpu_custom_call" | custom-call | tf_op jit(solution)/shard_map/pallas_call | solution.py:359
  (10 shorter events, 0.2 us)
Async XLA Ops:
  0.7 0.9 copy-start
  1.6 0.7 copy-start.1
  5.3 21.0 %collective-permute-start = (f32[16,64,128]{2,1,0:T(8,128)S(1)}, f32[16,64,128]{2,1,0:T(8,128)S(1)}, u32[]{:S(2)}, u32[]{:S(2)}) collective-permute-start(f32[16,64,128]{2,1,0:T(8,128)S(1)} %get-tuple-element.21), channel_id=1, source_target_pairs={{0,508},{4,8},{8,4},{12,16},{16,12},{20,24},{24,20},{28,32},{32,28... | collective-permute-start | bytes 1572872 | tf_op jit(solution)/shard_map/ppermute | solution.py:305
  19.4 6.9 %collective-permute-start.1 = (f32[16,64,128]{2,1,0:T(8,128)S(1)}, f32[16,64,128]{2,1,0:T(8,128)S(1)}, u32[]{:S(2)}, u32[]{:S(2)}) collective-permute-start(f32[16,64,128]{2,1,0:T(8,128)S(1)} %get-tuple-element.22), channel_id=1, source_target_pairs={{0,4},{4,0},{8,12},{12,8},{16,20},{20,16},{24,28},{28,24},{32,36},... | collective-permute-start | bytes 1572872 | tf_op jit(solution)/shard_map/ppermute | solution.py:306
  48.2 8.7 %collective-permute-start.3 = (f32[16,64,128]{2,1,0:T(8,128)S(1)}, f32[16,64,128]{2,1,0:T(8,128)S(1)}, u32[]{:S(2)}, u32[]{:S(2)}) collective-permute-start(f32[16,64,128]{2,1,0:T(8,128)S(1)} %bitcast.7), channel_id=1, source_target_pairs={{0,4},{4,0},{8,12},{12,8},{16,20},{20,16},{24,28},{28,24},{32,36},... | collective-permute-start | bytes 1572872 | tf_op jit(solution)/shard_map/ppermute | solution.py:306
  50.1 13.8 %collective-permute-start.2 = (f32[16,64,128]{2,1,0:T(8,128)S(1)}, f32[16,64,128]{2,1,0:T(8,128)S(1)}, u32[]{:S(2)}, u32[]{:S(2)}) collective-permute-start(f32[16,64,128]{2,1,0:T(8,128)S(1)} %bitcast.8), channel_id=1, source_target_pairs={{0,508},{4,8},{8,4},{12,16},{16,12},{20,24},{24,20},{28,32},{32,28... | collective-permute-start | bytes 1572872 | tf_op jit(solution)/shard_map/ppermute | solution.py:305
  67.3 23.0 %collective-permute-start.4 = (f32[16,64,128]{2,1,0:T(8,128)S(1)}, f32[16,64,128]{2,1,0:T(8,128)S(1)}, u32[]{:S(2)}, u32[]{:S(2)}) collective-permute-start(f32[16,64,128]{2,1,0:T(8,128)S(1)} %get-tuple-element.24), channel_id=1, source_target_pairs={{0,508},{4,8},{8,4},{12,16},{16,12},{20,24},{24,20},{28,32},{32,28... | collective-permute-start | bytes 1572872 | tf_op jit(solution)/shard_map/ppermute | solution.py:305
  75.9 14.4 %collective-permute-start.5 = (f32[16,64,128]{2,1,0:T(8,128)S(1)}, f32[16,64,128]{2,1,0:T(8,128)S(1)}, u32[]{:S(2)}, u32[]{:S(2)}) collective-permute-start(f32[16,64,128]{2,1,0:T(8,128)S(1)} %get-tuple-element.25), channel_id=1, source_target_pairs={{0,4},{4,0},{8,12},{12,8},{16,20},{20,16},{24,28},{28,24},{32,36},... | collective-permute-start | bytes 1572872 | tf_op jit(solution)/shard_map/ppermute | solution.py:306
  116.2 20.0 %collective-permute-start.7 = (f32[16,64,128]{2,1,0:T(8,128)S(1)}, f32[16,64,128]{2,1,0:T(8,128)S(1)}, u32[]{:S(2)}, u32[]{:S(2)}) collective-permute-start(f32[16,64,128]{2,1,0:T(8,128)S(1)} %bitcast.10), channel_id=1, source_target_pairs={{0,4},{4,0},{8,12},{12,8},{16,20},{20,16},{24,28},{28,24},{32,36},... | collective-permute-start | bytes 1572872 | tf_op jit(solution)/shard_map/ppermute | solution.py:306
  118.1 18.1 %collective-permute-start.6 = (f32[16,64,128]{2,1,0:T(8,128)S(1)}, f32[16,64,128]{2,1,0:T(8,128)S(1)}, u32[]{:S(2)}, u32[]{:S(2)}) collective-permute-start(f32[16,64,128]{2,1,0:T(8,128)S(1)} %bitcast.11), channel_id=1, source_target_pairs={{0,508},{4,8},{8,4},{12,16},{16,12},{20,24},{24,20},{28,32},{32,28... | collective-permute-start | bytes 1572872 | tf_op jit(solution)/shard_map/ppermute | solution.py:305

commit v5 on v4

--- a/solution.py
+++ b/solution.py
@@ -255,6 +255,9 @@
     return lax.all_to_all(copies, axes, split_axis=0, concat_axis=0, tiled=True)
 
 
+in_space = pltpu.with_memory_space_constraint
+
+
 def to_everyone(x, axes):
     return swapped(jnp.broadcast_to(x, (lax.axis_size(axes), *x.shape)), axes)
 
@@ -319,17 +322,17 @@
 
     def exchange_with_gram(parts, gram):
         p_outer, p_own, p_partner = parts
-        gram = swapped(gram, ("z", "c"))
+        gram = swapped(gram, ("y", "c"))
         got_outer, got = over_pairs(p_outer, p_partner)
         total = pieces(p_own + got_outer + got)
         sides = jnp.broadcast_to(gram.sum(axis=0), (groups, *packed))
         arrived = swapped(jnp.concatenate([total, sides], axis=1), "grp")
         copies, gram = call(
-            share_kernel, [VMEM], [((groups, mine * k, T), F32), ((lax.axis_size("y"), *packed), F32)]
+            share_kernel, [VMEM], [((groups, mine * k, T), F32), ((lax.axis_size("z"), *packed), F32)]
         )(arrived)
         own = swapped(copies, "grp").reshape(block, k, T)
         own, gram = lax.optimization_barrier((own, gram))
-        gram = swapped(gram, "y")
+        gram = swapped(gram, "z")
         at_outer, at_partner = over_pairs(own, own)
         return (at_outer, own, at_partner), gram
 
@@ -340,12 +343,12 @@
         [tbuf, panel, phl, acc, sems, pltpu.SemaphoreType.DMA],
         2,
         [VMEM] * 3 + [SMEM],
-    )(coords.T, live, tiles, sketch.T)
+    )(in_space(coords.T, pltpu.HBM), live, tiles, in_space(sketch.T, pltpu.HBM))
     whole = exchange(parts)
     *parts, gram = call(
         middle_kernel,
         [HBM] + [VMEM] * 3,
-        [block_out] * 3 + [((2 * lax.axis_size("z"), *packed), F32)],
+        [block_out] * 3 + [((2 * lax.axis_size("y"), *packed), F32)],
         [tbuf, thl, shl, img, phl, acc, sems],
         2,
     )(code, live, tiles, *whole)

time: 175 us -> 176 us (level)
  blocking collectives: 105 us -> 108 us
    all_to_all x9, blocking collectives: 105 us -> 108 us  [swapped(): return lax.all_to_all(copies, axes, split_axis=0, concat_axis=0, tiled=True)]
where the time goes in v5:
time: 176 us; the launch traced here: 175 us
  blocking collectives  108 us (61%)
  starting transfers between devices  39.6 us (22%)
  Pallas kernels  14.4 us (8%)
  waiting for transfers between devices  11.9 us (7%)
    all_to_all x9, blocking collectives, swapped(): return lax.all_to_all(copies, axes, split_axis=0, concat_axis=0, tiled=True)  108 us
    ppermute x4, starting transfers between devices, over_pairs(): got_outer = lax.ppermute(to_outer, ROWS, outer)  31.9 us
    ppermute x4, waiting for transfers between devices, over_pairs(): got_outer = lax.ppermute(to_outer, ROWS, outer)  11.9 us
    ppermute x4, starting transfers between devices, over_pairs(): got_partner = lax.ppermute(to_partner, ROWS, partner)  7.66 us
  transfers between devices with their start and end apart: 8, of which 2 were waited for; matrix products, arithmetic and copies ran while one was open for 0% of the time, Pallas kernels for 1%

profile of v5, /device:TPU:2, one launch (start us, length us, event | category | flops | bytes accessed | tf_op | source)
XLA Modules:
  0.0 174.9 jit_solution(15079112085309339307)
XLA Ops:
  0.7 3.2 %shard_map.46 = (f32[16,64,128]{2,1,0:T(8,128)S(1)}, f32[16,64,128]{2,1,0:T(8,128)S(1)}, f32[16,64,128]{2,1,0:T(8,128)S(1)}, s32[48]{0:T(128)S(1)}) custom-call(s32[2,48]{1,0:T(2,128)} %bitcast.16, s32[1]{0:T(128)S(6)} %copy.5.live, f32[48,128,128]{2,1,0:T(8,128)} %tiles.5, f32[64,512]{1,0:T(8,128)} %bitcast.15), custom_call_target="tpu_custom_call" | custom-call | tf_op jit(solution)/shard_map/pallas_call | solution.py:339
  3.8 14.6 %collective-permute-start = (f32[16,64,128]{2,1,0:T(8,128)S(1)}, f32[16,64,128]{2,1,0:T(8,128)S(1)}, u32[]{:S(2)}, u32[]{:S(2)}) collective-permute-start(f32[16,64,128]{2,1,0:T(8,128)S(1)} %get-tuple-element.21), channel_id=1, source_target_pairs={{0,508},{4,8},{8,4},{12,16},{16,12},{20,24},{24,20},{28,32},{32,28... | collective-permute-start | bytes 1572872 | tf_op jit(solution)/shard_map/ppermute | solution.py:308
  18.5 1.9 %collective-permute-start.1 = (f32[16,64,128]{2,1,0:T(8,128)S(1)}, f32[16,64,128]{2,1,0:T(8,128)S(1)}, u32[]{:S(2)}, u32[]{:S(2)}) collective-permute-start(f32[16,64,128]{2,1,0:T(8,128)S(1)} %get-tuple-element.22), channel_id=1, source_target_pairs={{0,4},{4,0},{8,12},{12,8},{16,20},{20,16},{24,28},{28,24},{32,36},... | collective-permute-start | bytes 1572872 | tf_op jit(solution)/shard_map/ppermute | solution.py:309
  20.4 4.9 %collective-permute-done = f32[16,64,128]{2,1,0:T(8,128)S(1)} collective-permute-done((f32[16,64,128]{2,1,0:T(8,128)S(1)}, f32[16,64,128]{2,1,0:T(8,128)S(1)}, u32[]{:S(2)}, u32[]{:S(2)}) %collective-permute-start) | collective-permute-done | bytes 524320 | tf_op jit(solution)/shard_map/ppermute | solution.py:308
  25.3 0.0 collective-permute-done.1
  25.3 0.1 add_add_fusion.1
  25.5 11.3 %all_to_all.45 = f32[4,256,128]{2,1,0:T(8,128)S(1)} all-to-all(f32[4,256,128]{2,1,0:T(8,128)S(1)} %bitcast.14), channel_id=1, replica_groups=mesh['y'=8,'z'=8,'c'=2,'grp'=4] {'grp'}, dimensions={0} | all-to-all | bytes 1048576 | tf_op jit(solution)/shard_map/all_to_all | solution.py:255
  36.8 10.5 %all_to_all.46 = f32[4,256,128]{2,1,0:T(8,128)S(1)} all-to-all(f32[4,256,128]{2,1,0:T(8,128)S(1)} %broadcast_in_dim.12), channel_id=1, replica_groups=mesh['y'=8,'z'=8,'c'=2,'grp'=4] {'grp'}, dimensions={0} | all-to-all | bytes 1048576 | tf_op jit(solution)/shard_map/all_to_all | solution.py:255
  47.3 1.9 %collective-permute-start.3 = (f32[16,64,128]{2,1,0:T(8,128)S(1)}, f32[16,64,128]{2,1,0:T(8,128)S(1)}, u32[]{:S(2)}, u32[]{:S(2)}) collective-permute-start(f32[16,64,128]{2,1,0:T(8,128)S(1)} %bitcast.7), channel_id=1, source_target_pairs={{0,4},{4,0},{8,12},{12,8},{16,20},{20,16},{24,28},{28,24},{32,36},... | collective-permute-start | bytes 1572872 | tf_op jit(solution)/shard_map/ppermute | solution.py:309
  49.2 6.8 %collective-permute-start.2 = (f32[16,64,128]{2,1,0:T(8,128)S(1)}, f32[16,64,128]{2,1,0:T(8,128)S(1)}, u32[]{:S(2)}, u32[]{:S(2)}) collective-permute-start(f32[16,64,128]{2,1,0:T(8,128)S(1)} %bitcast.8), channel_id=1, source_target_pairs={{0,508},{4,8},{8,4},{12,16},{16,12},{20,24},{24,20},{28,32},{32,28... | collective-permute-start | bytes 1572872 | tf_op jit(solution)/shard_map/ppermute | solution.py:308
  56.0 0.0 collective-permute-done.3.s_partner
  56.0 7.0 %collective-permute-done.2.s_outer = f32[16,64,128]{2,1,0:T(8,128)S(1)} collective-permute-done((f32[16,64,128]{2,1,0:T(8,128)S(1)}, f32[16,64,128]{2,1,0:T(8,128)S(1)}, u32[]{:S(2)}, u32[]{:S(2)}) %collective-permute-start.2) | collective-permute-done | bytes 524320 | tf_op jit(solution)/shard_map/ppermute | solution.py:308
  63.0 3.3 %shard_map.47 = (f32[16,64,128]{2,1,0:T(8,128)S(1)}, f32[16,64,128]{2,1,0:T(8,128)S(1)}, f32[16,64,128]{2,1,0:T(8,128)S(1)}, f32[16,24,128]{2,1,0:T(8,128)S(1)}) custom-call(s32[48]{0:T(128)S(1)} %get-tuple-element.19.code, s32[1]{0:T(128)S(6)} %copy.5.live, f32[48,128,128]{2,1,0:T(8,128)} %tiles.5, f32[16,64,128]{2,1,0:T(8,128)S(1)} %collective-permute-done.2.s_outer, ...), custom_call_target="tpu_custom_call" | custom-call | tf_op jit(solution)/shard_map/pallas_call | solution.py:348
  66.3 8.6 %collective-permute-start.4 = (f32[16,64,128]{2,1,0:T(8,128)S(1)}, f32[16,64,128]{2,1,0:T(8,128)S(1)}, u32[]{:S(2)}, u32[]{:S(2)}) collective-permute-start(f32[16,64,128]{2,1,0:T(8,128)S(1)} %get-tuple-element.24), channel_id=1, source_target_pairs={{0,508},{4,8},{8,4},{12,16},{16,12},{20,24},{24,20},{28,32},{32,28... | collective-permute-start | bytes 1572872 | tf_op jit(solution)/shard_map/ppermute | solution.py:308
  74.9 1.9 %collective-permute-start.5 = (f32[16,64,128]{2,1,0:T(8,128)S(1)}, f32[16,64,128]{2,1,0:T(8,128)S(1)}, u32[]{:S(2)}, u32[]{:S(2)}) collective-permute-start(f32[16,64,128]{2,1,0:T(8,128)S(1)} %get-tuple-element.25), channel_id=1, source_target_pairs={{0,4},{4,0},{8,12},{12,8},{16,20},{20,16},{24,28},{28,24},{32,36},... | collective-permute-start | bytes 1572872 | tf_op jit(solution)/shard_map/ppermute | solution.py:309
  76.8 13.3 %all_to_all.47 = f32[16,24,128]{2,1,0:T(8,128)S(1)} all-to-all(f32[16,24,128]{2,1,0:T(8,128)S(1)} %get-tuple-element.26), channel_id=1, replica_groups=mesh['y'=8,'z'=8,'c'=2,'grp'=4] {'y','c'}, dimensions={0} | all-to-all | bytes 393216 | tf_op jit(solution)/shard_map/all_to_all | solution.py:255
  90.2 0.0 collective-permute-done.4
  90.2 0.0 collective-permute-done.5
  90.2 0.1 add_add_fusion
  90.4 14.7 %all_to_all.48.pieces = f32[4,280,128]{2,1,0:T(8,128)S(1)} all-to-all(f32[4,280,128]{2,1,0:T(8,128)S(1)} %pad_maximum_fusion), channel_id=1, replica_groups=mesh['y'=8,'z'=8,'c'=2,'grp'=4] {'grp'}, dimensions={0} | all-to-all | bytes 1146880 | tf_op jit(solution)/shard_map/all_to_all | solution.py:255
  105.2 12.1 %all_to_all.49 = f32[4,256,128]{2,1,0:T(8,128)S(1)} all-to-all(f32[4,256,128]{2,1,0:T(8,128)S(1)} %get-tuple-element.27), channel_id=1, replica_groups=mesh['y'=8,'z'=8,'c'=2,'grp'=4] {'grp'}, dimensions={0} | all-to-all | bytes 1048576 | tf_op jit(solution)/shard_map/all_to_all | solution.py:255
  117.3 1.9 %collective-permute-start.7 = (f32[16,64,128]{2,1,0:T(8,128)S(1)}, f32[16,64,128]{2,1,0:T(8,128)S(1)}, u32[]{:S(2)}, u32[]{:S(2)}) collective-permute-start(f32[16,64,128]{2,1,0:T(8,128)S(1)} %bitcast.10), channel_id=1, source_target_pairs={{0,4},{4,0},{8,12},{12,8},{16,20},{20,16},{24,28},{28,24},{32,36},... | collective-permute-start | bytes 1572872 | tf_op jit(solution)/shard_map/ppermute | solution.py:309
  119.2 1.9 %collective-permute-start.6 = (f32[16,64,128]{2,1,0:T(8,128)S(1)}, f32[16,64,128]{2,1,0:T(8,128)S(1)}, u32[]{:S(2)}, u32[]{:S(2)}) collective-permute-start(f32[16,64,128]{2,1,0:T(8,128)S(1)} %bitcast.11), channel_id=1, source_target_pairs={{0,508},{4,8},{8,4},{12,16},{16,12},{20,24},{24,20},{28,32},{32,28... | collective-permute-start | bytes 1572872 | tf_op jit(solution)/shard_map/ppermute | solution.py:308
  121.1 14.0 %all_to_all.50.parts = f32[8,24,128]{2,1,0:T(8,128)S(1)} all-to-all(f32[8,24,128]{2,1,0:T(8,128)S(1)} %get-tuple-element.30), channel_id=1, replica_groups=mesh['y'=8,'z'=8,'c'=2,'grp'=4] {'z'}, dimensions={0} | all-to-all | bytes 196608 | tf_op jit(solution)/shard_map/all_to_all | solution.py:255
  135.1 2.0 %shard_map.49.linv = f32[64,64]{1,0:T(8,128)S(1)} custom-call(f32[8,24,128]{2,1,0:T(8,128)S(1)} %all_to_all.50.parts), custom_call_target="tpu_custom_call" | custom-call | tf_op jit(solution)/shard_map/pallas_call | solution.py:356
  137.2 0.0 collective-permute-done.7.s_partner
  137.2 0.0 collective-permute-done.6.s_outer
  137.2 2.9 %shard_map.50 = (f32[64,512]{1,0:T(8,128)S(1)}, f32[8,24,128]{2,1,0:T(8,128)S(1)}) custom-call(s32[48]{0:T(128)S(1)} %get-tuple-element.19.code, s32[1]{0:T(128)S(6)} %copy.5.live, f32[48,128,128]{2,1,0:T(8,128)} %tiles.5, f32[16,64,128]{2,1,0:T(8,128)S(1)} %collective-permute-done.6.s_outer, f32[16,64,128]{2,1,0:T(8,128)S(1)} %bitcast.12, ...), custom_call_target="tpu_custom_call" | custom-call | tf_op jit(solution)/shard_map/pallas_call | solution.py:357
  140.1 9.0 %all_to_all.51 = f32[8,24,128]{2,1,0:T(8,128)S(1)} all-to-all(f32[8,24,128]{2,1,0:T(8,128)S(1)} %get-tuple-element.31), channel_id=1, replica_groups=mesh['y'=8,'z'=8,'c'=2,'grp'=4] {'c','grp'}, dimensions={0} | all-to-all | bytes 196608 | tf_op jit(solution)/shard_map/all_to_all | solution.py:255
  149.1 11.7 %all_to_all.52 = f32[8,24,128]{2,1,0:T(8,128)S(1)} all-to-all(f32[8,24,128]{2,1,0:T(8,128)S(1)} %broadcast_in_dim.14), channel_id=1, replica_groups=mesh['y'=8,'z'=8,'c'=2,'grp'=4] {'z'}, dimensions={0} | all-to-all | bytes 196608 | tf_op jit(solution)/shard_map/all_to_all | solution.py:255
  160.9 11.1 %all_to_all.53.parts = f32[8,24,128]{2,1,0:T(8,128)S(1)} all-to-all(f32[8,24,128]{2,1,0:T(8,128)S(1)} %broadcast_in_dim.15), channel_id=1, replica_groups=mesh['y'=8,'z'=8,'c'=2,'grp'=4] {'y'}, dimensions={0} | all-to-all | bytes 196608 | tf_op jit(solution)/shard_map/all_to_all | solution.py:255
  172.0 2.9 %shard_map.51 = f32[64,512]{1,0:T(8,128)} custom-call(f32[8,24,128]{2,1,0:T(8,128)S(1)} %all_to_all.53.parts, f32[64,512]{1,0:T(8,128)S(1)} %get-tuple-element.32.image), custom_call_target="tpu_custom_call" | custom-call | tf_op jit(solution)/shard_map/pallas_call | solution.py:362
  (10 shorter events, 0.2 us)
Async XLA Ops:
  3.8 21.5 %collective-permute-start = (f32[16,64,128]{2,1,0:T(8,128)S(1)}, f32[16,64,128]{2,1,0:T(8,128)S(1)}, u32[]{:S(2)}, u32[]{:S(2)}) collective-permute-start(f32[16,64,128]{2,1,0:T(8,128)S(1)} %get-tuple-element.21), channel_id=1, source_target_pairs={{0,508},{4,8},{8,4},{12,16},{16,12},{20,24},{24,20},{28,32},{32,28... | collective-permute-start | bytes 1572872 | tf_op jit(solution)/shard_map/ppermute | solution.py:308
  18.5 6.9 %collective-permute-start.1 = (f32[16,64,128]{2,1,0:T(8,128)S(1)}, f32[16,64,128]{2,1,0:T(8,128)S(1)}, u32[]{:S(2)}, u32[]{:S(2)}) collective-permute-start(f32[16,64,128]{2,1,0:T(8,128)S(1)} %get-tuple-element.22), channel_id=1, source_target_pairs={{0,4},{4,0},{8,12},{12,8},{16,20},{20,16},{24,28},{28,24},{32,36},... | collective-permute-start | bytes 1572872 | tf_op jit(solution)/shard_map/ppermute | solution.py:309
  47.3 8.7 %collective-permute-start.3 = (f32[16,64,128]{2,1,0:T(8,128)S(1)}, f32[16,64,128]{2,1,0:T(8,128)S(1)}, u32[]{:S(2)}, u32[]{:S(2)}) collective-permute-start(f32[16,64,128]{2,1,0:T(8,128)S(1)} %bitcast.7), channel_id=1, source_target_pairs={{0,4},{4,0},{8,12},{12,8},{16,20},{20,16},{24,28},{28,24},{32,36},... | collective-permute-start | bytes 1572872 | tf_op jit(solution)/shard_map/ppermute | solution.py:309
  49.2 13.8 %collective-permute-start.2 = (f32[16,64,128]{2,1,0:T(8,128)S(1)}, f32[16,64,128]{2,1,0:T(8,128)S(1)}, u32[]{:S(2)}, u32[]{:S(2)}) collective-permute-start(f32[16,64,128]{2,1,0:T(8,128)S(1)} %bitcast.8), channel_id=1, source_target_pairs={{0,508},{4,8},{8,4},{12,16},{16,12},{20,24},{24,20},{28,32},{32,28... | collective-permute-start | bytes 1572872 | tf_op jit(solution)/shard_map/ppermute | solution.py:308
  66.3 23.9 %collective-permute-start.4 = (f32[16,64,128]{2,1,0:T(8,128)S(1)}, f32[16,64,128]{2,1,0:T(8,128)S(1)}, u32[]{:S(2)}, u32[]{:S(2)}) collective-permute-start(f32[16,64,128]{2,1,0:T(8,128)S(1)} %get-tuple-element.24), channel_id=1, source_target_pairs={{0,508},{4,8},{8,4},{12,16},{16,12},{20,24},{24,20},{28,32},{32,28... | collective-permute-start | bytes 1572872 | tf_op jit(solution)/shard_map/ppermute | solution.py:308
  74.9 15.3 %collective-permute-start.5 = (f32[16,64,128]{2,1,0:T(8,128)S(1)}, f32[16,64,128]{2,1,0:T(8,128)S(1)}, u32[]{:S(2)}, u32[]{:S(2)}) collective-permute-start(f32[16,64,128]{2,1,0:T(8,128)S(1)} %get-tuple-element.25), channel_id=1, source_target_pairs={{0,4},{4,0},{8,12},{12,8},{16,20},{20,16},{24,28},{28,24},{32,36},... | collective-permute-start | bytes 1572872 | tf_op jit(solution)/shard_map/ppermute | solution.py:309
  117.3 19.9 %collective-permute-start.7 = (f32[16,64,128]{2,1,0:T(8,128)S(1)}, f32[16,64,128]{2,1,0:T(8,128)S(1)}, u32[]{:S(2)}, u32[]{:S(2)}) collective-permute-start(f32[16,64,128]{2,1,0:T(8,128)S(1)} %bitcast.10), channel_id=1, source_target_pairs={{0,4},{4,0},{8,12},{12,8},{16,20},{20,16},{24,28},{28,24},{32,36},... | collective-permute-start | bytes 1572872 | tf_op jit(solution)/shard_map/ppermute | solution.py:309
  119.2 18.0 %collective-permute-start.6 = (f32[16,64,128]{2,1,0:T(8,128)S(1)}, f32[16,64,128]{2,1,0:T(8,128)S(1)}, u32[]{:S(2)}, u32[]{:S(2)}) collective-permute-start(f32[16,64,128]{2,1,0:T(8,128)S(1)} %bitcast.11), channel_id=1, source_target_pairs={{0,508},{4,8},{8,4},{12,16},{16,12},{20,24},{24,20},{28,32},{32,28... | collective-permute-start | bytes 1572872 | tf_op jit(solution)/shard_map/ppermute | solution.py:308

commit v6 on v5

--- a/solution.py
+++ b/solution.py
@@ -177,8 +177,7 @@
         total = total + pieces[n]
     for n in range(whole.shape[0]):
         whole[n] = total[:rows]
-    for n in range(gram.shape[0]):
-        gram[n] = total[rows:]
+    gram[...] = total[rows:]
 
 
 def inverse_factor(g):
@@ -322,17 +321,16 @@
 
     def exchange_with_gram(parts, gram):
         p_outer, p_own, p_partner = parts
-        gram = swapped(gram, ("y", "c"))
+        gram = swapped(gram, "y")
         got_outer, got = over_pairs(p_outer, p_partner)
         total = pieces(p_own + got_outer + got)
         sides = jnp.broadcast_to(gram.sum(axis=0), (groups, *packed))
         arrived = swapped(jnp.concatenate([total, sides], axis=1), "grp")
-        copies, gram = call(
-            share_kernel, [VMEM], [((groups, mine * k, T), F32), ((lax.axis_size("z"), *packed), F32)]
-        )(arrived)
+        copies, gram = call(share_kernel, [VMEM], [((groups, mine * k, T), F32), (packed, F32)])(arrived)
         own = swapped(copies, "grp").reshape(block, k, T)
-        own, gram = lax.optimization_barrier((own, gram))
-        gram = swapped(gram, "z")
+        beside = lax.ppermute(gram, ROWS, partner)
+        own, gram = lax.optimization_barrier((own, gram + beside))
+        gram = to_everyone(gram, "z")
         at_outer, at_partner = over_pairs(own, own)
         return (at_outer, own, at_partner), gram
 
@@ -348,7 +346,7 @@
     *parts, gram = call(
         middle_kernel,
         [HBM] + [VMEM] * 3,
-        [block_out] * 3 + [((2 * lax.axis_size("y"), *packed), F32)],
+        [block_out] * 3 + [((lax.axis_size("y"), *packed), F32)],
         [tbuf, thl, shl, img, phl, acc, sems],
         2,
     )(code, live, tiles, *whole)

time: 176 us -> 173 us (0.983)
  blocking collectives: 108 us -> 92.8 us
  starting transfers between devices: 39.6 us -> 46.4 us
  waiting for transfers between devices: 11.9 us -> 16.6 us
    all_to_all x9 -> x8, blocking collectives: 108 us -> 92.8 us  [swapped(): return lax.all_to_all(copies, axes, split_axis=0, concat_axis=0, tiled=True)]
    all_to_all x0 -> x1, starting transfers between devices: none -> 4.89 us  [swapped(): return lax.all_to_all(copies, axes, split_axis=0, concat_axis=0, tiled=True)]
    all_to_all x0 -> x1, waiting for transfers between devices: none -> 3.56 us  [swapped(): return lax.all_to_all(copies, axes, split_axis=0, concat_axis=0, tiled=True)]
    ppermute x0 -> x1, starting transfers between devices: none -> 1.91 us  [exchange_with_gram(): beside = lax.ppermute(gram, ROWS, partner)]
  transfers between devices with their start and end apart: 8 -> 10, of which waited for: 2 -> 4; matrix products, arithmetic and copies ran while one was open for 0% -> 0% of each run, Pallas kernels for 1% -> 1%
where the time goes in v6:
time: 173 us; the launch traced here: 172 us
  blocking collectives  92.8 us (54%)
  starting transfers between devices  46.4 us (27%)
  waiting for transfers between devices  16.6 us (10%)
  Pallas kernels  15.2 us (9%)
    all_to_all x8, blocking collectives, swapped(): return lax.all_to_all(copies, axes, split_axis=0, concat_axis=0, tiled=True)  92.8 us
    ppermute x4, starting transfers between devices, over_pairs(): got_outer = lax.ppermute(to_outer, ROWS, outer)  31.9 us
    ppermute x4, waiting for transfers between devices, over_pairs(): got_outer = lax.ppermute(to_outer, ROWS, outer)  11.9 us
    ppermute x4, starting transfers between devices, over_pairs(): got_partner = lax.ppermute(to_partner, ROWS, partner)  7.66 us
    all_to_all x1, starting transfers between devices, swapped(): return lax.all_to_all(copies, axes, split_axis=0, concat_axis=0, tiled=True)  4.89 us
    all_to_all x1, waiting for transfers between devices, swapped(): return lax.all_to_all(copies, axes, split_axis=0, concat_axis=0, tiled=True)  3.56 us
  transfers between devices with their start and end apart: 10, of which 4 were waited for; matrix products, arithmetic and copies ran while one was open for 0% of the time, Pallas kernels for 1%

profile of v6, /device:TPU:2, one launch (start us, length us, event | category | flops | bytes accessed | tf_op | source)
XLA Modules:
  0.0 172.3 jit_solution(146318457406278815)
XLA Ops:
  0.7 3.2 %shard_map.46 = (f32[16,64,128]{2,1,0:T(8,128)S(1)}, f32[16,64,128]{2,1,0:T(8,128)S(1)}, f32[16,64,128]{2,1,0:T(8,128)S(1)}, s32[48]{0:T(128)S(1)}) custom-call(s32[2,48]{1,0:T(2,128)} %bitcast.16, s32[1]{0:T(128)S(6)} %copy.5.live, f32[48,128,128]{2,1,0:T(8,128)} %tiles.5, f32[64,512]{1,0:T(8,128)} %bitcast.15), custom_call_target="tpu_custom_call" | custom-call | tf_op jit(solution)/shard_map/pallas_call | solution.py:337
  3.8 14.6 %collective-permute-start = (f32[16,64,128]{2,1,0:T(8,128)S(1)}, f32[16,64,128]{2,1,0:T(8,128)S(1)}, u32[]{:S(2)}, u32[]{:S(2)}) collective-permute-start(f32[16,64,128]{2,1,0:T(8,128)S(1)} %get-tuple-element.21), channel_id=1, source_target_pairs={{0,508},{4,8},{8,4},{12,16},{16,12},{20,24},{24,20},{28,32},{32,28... | collective-permute-start | bytes 1572872 | tf_op jit(solution)/shard_map/ppermute | solution.py:307
  18.5 1.9 %collective-permute-start.1 = (f32[16,64,128]{2,1,0:T(8,128)S(1)}, f32[16,64,128]{2,1,0:T(8,128)S(1)}, u32[]{:S(2)}, u32[]{:S(2)}) collective-permute-start(f32[16,64,128]{2,1,0:T(8,128)S(1)} %get-tuple-element.22), channel_id=1, source_target_pairs={{0,4},{4,0},{8,12},{12,8},{16,20},{20,16},{24,28},{28,24},{32,36},... | collective-permute-start | bytes 1572872 | tf_op jit(solution)/shard_map/ppermute | solution.py:308
  20.4 4.9 %collective-permute-done = f32[16,64,128]{2,1,0:T(8,128)S(1)} collective-permute-done((f32[16,64,128]{2,1,0:T(8,128)S(1)}, f32[16,64,128]{2,1,0:T(8,128)S(1)}, u32[]{:S(2)}, u32[]{:S(2)}) %collective-permute-start) | collective-permute-done | bytes 524320 | tf_op jit(solution)/shard_map/ppermute | solution.py:307
  25.3 0.0 collective-permute-done.1
  25.3 0.1 add_add_fusion.1
  25.5 11.3 %all_to_all.45 = f32[4,256,128]{2,1,0:T(8,128)S(1)} all-to-all(f32[4,256,128]{2,1,0:T(8,128)S(1)} %bitcast.14), channel_id=1, replica_groups=mesh['y'=8,'z'=8,'c'=2,'grp'=4] {'grp'}, dimensions={0} | all-to-all | bytes 1048576 | tf_op jit(solution)/shard_map/all_to_all | solution.py:254
  36.8 10.5 %all_to_all.46 = f32[4,256,128]{2,1,0:T(8,128)S(1)} all-to-all(f32[4,256,128]{2,1,0:T(8,128)S(1)} %broadcast_in_dim.15), channel_id=1, replica_groups=mesh['y'=8,'z'=8,'c'=2,'grp'=4] {'grp'}, dimensions={0} | all-to-all | bytes 1048576 | tf_op jit(solution)/shard_map/all_to_all | solution.py:254
  47.3 1.9 %collective-permute-start.3 = (f32[16,64,128]{2,1,0:T(8,128)S(1)}, f32[16,64,128]{2,1,0:T(8,128)S(1)}, u32[]{:S(2)}, u32[]{:S(2)}) collective-permute-start(f32[16,64,128]{2,1,0:T(8,128)S(1)} %bitcast.7), channel_id=1, source_target_pairs={{0,4},{4,0},{8,12},{12,8},{16,20},{20,16},{24,28},{28,24},{32,36},... | collective-permute-start | bytes 1572872 | tf_op jit(solution)/shard_map/ppermute | solution.py:308
  49.2 6.8 %collective-permute-start.2 = (f32[16,64,128]{2,1,0:T(8,128)S(1)}, f32[16,64,128]{2,1,0:T(8,128)S(1)}, u32[]{:S(2)}, u32[]{:S(2)}) collective-permute-start(f32[16,64,128]{2,1,0:T(8,128)S(1)} %bitcast.8), channel_id=1, source_target_pairs={{0,508},{4,8},{8,4},{12,16},{16,12},{20,24},{24,20},{28,32},{32,28... | collective-permute-start | bytes 1572872 | tf_op jit(solution)/shard_map/ppermute | solution.py:307
  56.0 0.0 collective-permute-done.3.s_partner
  56.0 7.0 %collective-permute-done.2.s_outer = f32[16,64,128]{2,1,0:T(8,128)S(1)} collective-permute-done((f32[16,64,128]{2,1,0:T(8,128)S(1)}, f32[16,64,128]{2,1,0:T(8,128)S(1)}, u32[]{:S(2)}, u32[]{:S(2)}) %collective-permute-start.2) | collective-permute-done | bytes 524320 | tf_op jit(solution)/shard_map/ppermute | solution.py:307
  63.0 3.3 %shard_map.47 = (f32[16,64,128]{2,1,0:T(8,128)S(1)}, f32[16,64,128]{2,1,0:T(8,128)S(1)}, f32[16,64,128]{2,1,0:T(8,128)S(1)}, f32[8,24,128]{2,1,0:T(8,128)S(1)}) custom-call(s32[48]{0:T(128)S(1)} %get-tuple-element.19.code, s32[1]{0:T(128)S(6)} %copy.5.live, f32[48,128,128]{2,1,0:T(8,128)} %tiles.5, f32[16,64,128]{2,1,0:T(8,128)S(1)} %collective-permute-done.2.s_outer, ...), custom_call_target="tpu_custom_call" | custom-call | tf_op jit(solution)/shard_map/pallas_call | solution.py:346
  66.3 8.6 %collective-permute-start.4 = (f32[16,64,128]{2,1,0:T(8,128)S(1)}, f32[16,64,128]{2,1,0:T(8,128)S(1)}, u32[]{:S(2)}, u32[]{:S(2)}) collective-permute-start(f32[16,64,128]{2,1,0:T(8,128)S(1)} %get-tuple-element.24), channel_id=1, source_target_pairs={{0,508},{4,8},{8,4},{12,16},{16,12},{20,24},{24,20},{28,32},{32,28... | collective-permute-start | bytes 1572872 | tf_op jit(solution)/shard_map/ppermute | solution.py:307
  74.9 1.9 %collective-permute-start.5 = (f32[16,64,128]{2,1,0:T(8,128)S(1)}, f32[16,64,128]{2,1,0:T(8,128)S(1)}, u32[]{:S(2)}, u32[]{:S(2)}) collective-permute-start(f32[16,64,128]{2,1,0:T(8,128)S(1)} %get-tuple-element.25), channel_id=1, source_target_pairs={{0,4},{4,0},{8,12},{12,8},{16,20},{20,16},{24,28},{28,24},{32,36},... | collective-permute-start | bytes 1572872 | tf_op jit(solution)/shard_map/ppermute | solution.py:308
  76.8 12.3 %all_to_all.47 = f32[8,24,128]{2,1,0:T(8,128)S(1)} all-to-all(f32[8,24,128]{2,1,0:T(8,128)S(1)} %get-tuple-element.26), channel_id=1, replica_groups=mesh['y'=8,'z'=8,'c'=2,'grp'=4] {'y'}, dimensions={0} | all-to-all | bytes 196608 | tf_op jit(solution)/shard_map/all_to_all | solution.py:254
  89.1 0.0 collective-permute-done.4
  89.1 0.0 collective-permute-done.5
  89.1 0.1 add_add_fusion
  89.3 13.0 %all_to_all.48.pieces = f32[4,280,128]{2,1,0:T(8,128)S(1)} all-to-all(f32[4,280,128]{2,1,0:T(8,128)S(1)} %pad_maximum_fusion), channel_id=1, replica_groups=mesh['y'=8,'z'=8,'c'=2,'grp'=4] {'grp'}, dimensions={0} | all-to-all | bytes 1146880 | tf_op jit(solution)/shard_map/all_to_all | solution.py:254
  102.3 0.8 shard_map.48
  103.1 4.9 %all-to-all-start.4 = ((f32[4,256,128]{2,1,0:T(8,128)}), f32[4,256,128]{2,1,0:T(8,128)S(1)}, u32[]{:S(2)}, u32[]{:S(2)}) async-start(f32[4,256,128]{2,1,0:T(8,128)} %get-tuple-element.27), calls=%async_computation.4 | async-start | bytes 1048576 | tf_op jit(solution)/shard_map/all_to_all | solution.py:254
  108.0 1.9 %collective-permute-start.6 = (f32[24,128]{1,0:T(8,128)S(1)}, f32[24,128]{1,0:T(8,128)S(1)}, u32[]{:S(2)}, u32[]{:S(2)}) collective-permute-start(f32[24,128]{1,0:T(8,128)S(1)} %get-tuple-element.28), channel_id=1, source_target_pairs={{0,4},{4,0},{8,12},{12,8},{16,20},{20,16},{24,28},{28,24},{32,36},... | collective-permute-start | bytes 36872 | tf_op jit(solution)/shard_map/ppermute | solution.py:331
  109.9 1.1 collective-permute-done.6
  111.0 3.6 %all-to-all-done.4 = f32[4,256,128]{2,1,0:T(8,128)S(1)} async-done(((f32[4,256,128]{2,1,0:T(8,128)}), f32[4,256,128]{2,1,0:T(8,128)S(1)}, u32[]{:S(2)}, u32[]{:S(2)}) %all-to-all-start.4) | async-done | bytes 524320 | tf_op jit(solution)/shard_map/all_to_all | solution.py:254
  114.6 1.9 %collective-permute-start.8 = (f32[16,64,128]{2,1,0:T(8,128)S(1)}, f32[16,64,128]{2,1,0:T(8,128)S(1)}, u32[]{:S(2)}, u32[]{:S(2)}) collective-permute-start(f32[16,64,128]{2,1,0:T(8,128)S(1)} %bitcast.10), channel_id=1, source_target_pairs={{0,4},{4,0},{8,12},{12,8},{16,20},{20,16},{24,28},{28,24},{32,36},... | collective-permute-start | bytes 1572872 | tf_op jit(solution)/shard_map/ppermute | solution.py:308
  116.5 1.9 %collective-permute-start.7 = (f32[16,64,128]{2,1,0:T(8,128)S(1)}, f32[16,64,128]{2,1,0:T(8,128)S(1)}, u32[]{:S(2)}, u32[]{:S(2)}) collective-permute-start(f32[16,64,128]{2,1,0:T(8,128)S(1)} %bitcast.11), channel_id=1, source_target_pairs={{0,508},{4,8},{8,4},{12,16},{16,12},{20,24},{24,20},{28,32},{32,28... | collective-permute-start | bytes 1572872 | tf_op jit(solution)/shard_map/ppermute | solution.py:307
  118.5 14.0 %all_to_all.49.parts = f32[8,24,128]{2,1,0:T(8,128)S(1)} all-to-all(f32[8,24,128]{2,1,0:T(8,128)S(1)} %broadcast_in_dim.17), channel_id=1, replica_groups=mesh['y'=8,'z'=8,'c'=2,'grp'=4] {'z'}, dimensions={0} | all-to-all | bytes 196608 | tf_op jit(solution)/shard_map/all_to_all | solution.py:254
  132.5 2.0 %shard_map.49.linv = f32[64,64]{1,0:T(8,128)S(1)} custom-call(f32[8,24,128]{2,1,0:T(8,128)S(1)} %all_to_all.49.parts), custom_call_target="tpu_custom_call" | custom-call | tf_op jit(solution)/shard_map/pallas_call | solution.py:354
  134.5 0.0 collective-permute-done.8.s_partner
  134.5 0.0 collective-permute-done.7.s_outer
  134.5 2.9 %shard_map.50 = (f32[64,512]{1,0:T(8,128)S(1)}, f32[8,24,128]{2,1,0:T(8,128)S(1)}) custom-call(s32[48]{0:T(128)S(1)} %get-tuple-element.19.code, s32[1]{0:T(128)S(6)} %copy.5.live, f32[48,128,128]{2,1,0:T(8,128)} %tiles.5, f32[16,64,128]{2,1,0:T(8,128)S(1)} %collective-permute-done.7.s_outer, f32[16,64,128]{2,1,0:T(8,128)S(1)} %bitcast.12, ...), custom_call_target="tpu_custom_call" | custom-call | tf_op jit(solution)/shard_map/pallas_call | solution.py:355
  137.4 9.0 %all_to_all.50 = f32[8,24,128]{2,1,0:T(8,128)S(1)} all-to-all(f32[8,24,128]{2,1,0:T(8,128)S(1)} %get-tuple-element.31), channel_id=1, replica_groups=mesh['y'=8,'z'=8,'c'=2,'grp'=4] {'c','grp'}, dimensions={0} | all-to-all | bytes 196608 | tf_op jit(solution)/shard_map/all_to_all | solution.py:254
  146.4 11.7 %all_to_all.51 = f32[8,24,128]{2,1,0:T(8,128)S(1)} all-to-all(f32[8,24,128]{2,1,0:T(8,128)S(1)} %broadcast_in_dim.18), channel_id=1, replica_groups=mesh['y'=8,'z'=8,'c'=2,'grp'=4] {'z'}, dimensions={0} | all-to-all | bytes 196608 | tf_op jit(solution)/shard_map/all_to_all | solution.py:254
  158.2 11.1 %all_to_all.52.parts = f32[8,24,128]{2,1,0:T(8,128)S(1)} all-to-all(f32[8,24,128]{2,1,0:T(8,128)S(1)} %broadcast_in_dim.19), channel_id=1, replica_groups=mesh['y'=8,'z'=8,'c'=2,'grp'=4] {'y'}, dimensions={0} | all-to-all | bytes 196608 | tf_op jit(solution)/shard_map/all_to_all | solution.py:254
  169.3 2.9 %shard_map.51 = f32[64,512]{1,0:T(8,128)} custom-call(f32[8,24,128]{2,1,0:T(8,128)S(1)} %all_to_all.52.parts, f32[64,512]{1,0:T(8,128)S(1)} %get-tuple-element.32.image), custom_call_target="tpu_custom_call" | custom-call | tf_op jit(solution)/shard_map/pallas_call | solution.py:360
  (11 shorter events, 0.2 us)
Async XLA Ops:
  3.8 21.5 %collective-permute-start = (f32[16,64,128]{2,1,0:T(8,128)S(1)}, f32[16,64,128]{2,1,0:T(8,128)S(1)}, u32[]{:S(2)}, u32[]{:S(2)}) collective-permute-start(f32[16,64,128]{2,1,0:T(8,128)S(1)} %get-tuple-element.21), channel_id=1, source_target_pairs={{0,508},{4,8},{8,4},{12,16},{16,12},{20,24},{24,20},{28,32},{32,28... | collective-permute-start | bytes 1572872 | tf_op jit(solution)/shard_map/ppermute | solution.py:307
  18.5 6.9 %collective-permute-start.1 = (f32[16,64,128]{2,1,0:T(8,128)S(1)}, f32[16,64,128]{2,1,0:T(8,128)S(1)}, u32[]{:S(2)}, u32[]{:S(2)}) collective-permute-start(f32[16,64,128]{2,1,0:T(8,128)S(1)} %get-tuple-element.22), channel_id=1, source_target_pairs={{0,4},{4,0},{8,12},{12,8},{16,20},{20,16},{24,28},{28,24},{32,36},... | collective-permute-start | bytes 1572872 | tf_op jit(solution)/shard_map/ppermute | solution.py:308
  47.3 8.7 %collective-permute-start.3 = (f32[16,64,128]{2,1,0:T(8,128)S(1)}, f32[16,64,128]{2,1,0:T(8,128)S(1)}, u32[]{:S(2)}, u32[]{:S(2)}) collective-permute-start(f32[16,64,128]{2,1,0:T(8,128)S(1)} %bitcast.7), channel_id=1, source_target_pairs={{0,4},{4,0},{8,12},{12,8},{16,20},{20,16},{24,28},{28,24},{32,36},... | collective-permute-start | bytes 1572872 | tf_op jit(solution)/shard_map/ppermute | solution.py:308
  49.2 13.8 %collective-permute-start.2 = (f32[16,64,128]{2,1,0:T(8,128)S(1)}, f32[16,64,128]{2,1,0:T(8,128)S(1)}, u32[]{:S(2)}, u32[]{:S(2)}) collective-permute-start(f32[16,64,128]{2,1,0:T(8,128)S(1)} %bitcast.8), channel_id=1, source_target_pairs={{0,508},{4,8},{8,4},{12,16},{16,12},{20,24},{24,20},{28,32},{32,28... | collective-permute-start | bytes 1572872 | tf_op jit(solution)/shard_map/ppermute | solution.py:307
  66.3 22.8 %collective-permute-start.4 = (f32[16,64,128]{2,1,0:T(8,128)S(1)}, f32[16,64,128]{2,1,0:T(8,128)S(1)}, u32[]{:S(2)}, u32[]{:S(2)}) collective-permute-start(f32[16,64,128]{2,1,0:T(8,128)S(1)} %get-tuple-element.24), channel_id=1, source_target_pairs={{0,508},{4,8},{8,4},{12,16},{16,12},{20,24},{24,20},{28,32},{32,28... | collective-permute-start | bytes 1572872 | tf_op jit(solution)/shard_map/ppermute | solution.py:307
  74.9 14.2 %collective-permute-start.5 = (f32[16,64,128]{2,1,0:T(8,128)S(1)}, f32[16,64,128]{2,1,0:T(8,128)S(1)}, u32[]{:S(2)}, u32[]{:S(2)}) collective-permute-start(f32[16,64,128]{2,1,0:T(8,128)S(1)} %get-tuple-element.25), channel_id=1, source_target_pairs={{0,4},{4,0},{8,12},{12,8},{16,20},{20,16},{24,28},{28,24},{32,36},... | collective-permute-start | bytes 1572872 | tf_op jit(solution)/shard_map/ppermute | solution.py:308
  103.1 11.5 %all-to-all-start.4 = ((f32[4,256,128]{2,1,0:T(8,128)}), f32[4,256,128]{2,1,0:T(8,128)S(1)}, u32[]{:S(2)}, u32[]{:S(2)}) async-start(f32[4,256,128]{2,1,0:T(8,128)} %get-tuple-element.27), calls=%async_computation.4 | async-start | bytes 1048576 | tf_op jit(solution)/shard_map/all_to_all | solution.py:254
  108.0 3.1 %collective-permute-start.6 = (f32[24,128]{1,0:T(8,128)S(1)}, f32[24,128]{1,0:T(8,128)S(1)}, u32[]{:S(2)}, u32[]{:S(2)}) collective-permute-start(f32[24,128]{1,0:T(8,128)S(1)} %get-tuple-element.28), channel_id=1, source_target_pairs={{0,4},{4,0},{8,12},{12,8},{16,20},{20,16},{24,28},{28,24},{32,36},... | collective-permute-start | bytes 36872 | tf_op jit(solution)/shard_map/ppermute | solution.py:331
  114.6 19.9 %collective-permute-start.8 = (f32[16,64,128]{2,1,0:T(8,128)S(1)}, f32[16,64,128]{2,1,0:T(8,128)S(1)}, u32[]{:S(2)}, u32[]{:S(2)}) collective-permute-start(f32[16,64,128]{2,1,0:T(8,128)S(1)} %bitcast.10), channel_id=1, source_target_pairs={{0,4},{4,0},{8,12},{12,8},{16,20},{20,16},{24,28},{28,24},{32,36},... | collective-permute-start | bytes 1572872 | tf_op jit(solution)/shard_map/ppermute | solution.py:308
  116.5 18.0 %collective-permute-start.7 = (f32[16,64,128]{2,1,0:T(8,128)S(1)}, f32[16,64,128]{2,1,0:T(8,128)S(1)}, u32[]{:S(2)}, u32[]{:S(2)}) collective-permute-start(f32[16,64,128]{2,1,0:T(8,128)S(1)} %bitcast.11), channel_id=1, source_target_pairs={{0,508},{4,8},{8,4},{12,16},{16,12},{20,24},{24,20},{28,32},{32,28... | collective-permute-start | bytes 1572872 | tf_op jit(solution)/shard_map/ppermute | solution.py:307

commit v7 on v6

--- a/solution.py
+++ b/solution.py
@@ -329,8 +329,9 @@
         copies, gram = call(share_kernel, [VMEM], [((groups, mine * k, T), F32), (packed, F32)])(arrived)
         own = swapped(copies, "grp").reshape(block, k, T)
         beside = lax.ppermute(gram, ROWS, partner)
-        own, gram = lax.optimization_barrier((own, gram + beside))
-        gram = to_everyone(gram, "z")
+        copies = jnp.broadcast_to(gram + beside, (lax.axis_size("z"), *packed))
+        own, copies = lax.optimization_barrier((own, copies))
+        gram = swapped(copies, "z")
         at_outer, at_partner = over_pairs(own, own)
         return (at_outer, own, at_partner), gram
 

time: 173 us -> 173 us (level)
  no operation moved by 1% of the time
where the time goes in v7:
time: 173 us; the launch traced here: 172 us
  blocking collectives  92.8 us (54%)
  starting transfers between devices  46.4 us (27%)
  waiting for transfers between devices  16.6 us (10%)
  Pallas kernels  15.2 us (9%)
    all_to_all x8, blocking collectives, swapped(): return lax.all_to_all(copies, axes, split_axis=0, concat_axis=0, tiled=True)  92.8 us
    ppermute x4, starting transfers between devices, over_pairs(): got_outer = lax.ppermute(to_outer, ROWS, outer)  31.9 us
    ppermute x4, waiting for transfers between devices, over_pairs(): got_outer = lax.ppermute(to_outer, ROWS, outer)  11.9 us
    ppermute x4, starting transfers between devices, over_pairs(): got_partner = lax.ppermute(to_partner, ROWS, partner)  7.67 us
    all_to_all x1, starting transfers between devices, swapped(): return lax.all_to_all(copies, axes, split_axis=0, concat_axis=0, tiled=True)  4.89 us
    all_to_all x1, waiting for transfers between devices, swapped(): return lax.all_to_all(copies, axes, split_axis=0, concat_axis=0, tiled=True)  3.56 us
  transfers between devices with their start and end apart: 10, of which 4 were waited for; matrix products, arithmetic and copies ran while one was open for 0% of the time, Pallas kernels for 1%

profile of v7, /device:TPU:2, one launch (start us, length us, event | category | flops | bytes accessed | tf_op | source)
XLA Modules:
  0.0 172.3 jit_solution(14924205116730582076)
XLA Ops:
  0.7 3.2 %shard_map.46 = (f32[16,64,128]{2,1,0:T(8,128)S(1)}, f32[16,64,128]{2,1,0:T(8,128)S(1)}, f32[16,64,128]{2,1,0:T(8,128)S(1)}, s32[48]{0:T(128)S(1)}) custom-call(s32[2,48]{1,0:T(2,128)} %bitcast.16, s32[1]{0:T(128)S(6)} %copy.5.live, f32[48,128,128]{2,1,0:T(8,128)} %tiles.5, f32[64,512]{1,0:T(8,128)} %bitcast.15), custom_call_target="tpu_custom_call" | custom-call | tf_op jit(solution)/shard_map/pallas_call | solution.py:338
  3.8 14.6 %collective-permute-start = (f32[16,64,128]{2,1,0:T(8,128)S(1)}, f32[16,64,128]{2,1,0:T(8,128)S(1)}, u32[]{:S(2)}, u32[]{:S(2)}) collective-permute-start(f32[16,64,128]{2,1,0:T(8,128)S(1)} %get-tuple-element.21), channel_id=1, source_target_pairs={{0,508},{4,8},{8,4},{12,16},{16,12},{20,24},{24,20},{28,32},{32,28... | collective-permute-start | bytes 1572872 | tf_op jit(solution)/shard_map/ppermute | solution.py:307
  18.5 1.9 %collective-permute-start.1 = (f32[16,64,128]{2,1,0:T(8,128)S(1)}, f32[16,64,128]{2,1,0:T(8,128)S(1)}, u32[]{:S(2)}, u32[]{:S(2)}) collective-permute-start(f32[16,64,128]{2,1,0:T(8,128)S(1)} %get-tuple-element.22), channel_id=1, source_target_pairs={{0,4},{4,0},{8,12},{12,8},{16,20},{20,16},{24,28},{28,24},{32,36},... | collective-permute-start | bytes 1572872 | tf_op jit(solution)/shard_map/ppermute | solution.py:308
  20.4 4.9 %collective-permute-done = f32[16,64,128]{2,1,0:T(8,128)S(1)} collective-permute-done((f32[16,64,128]{2,1,0:T(8,128)S(1)}, f32[16,64,128]{2,1,0:T(8,128)S(1)}, u32[]{:S(2)}, u32[]{:S(2)}) %collective-permute-start) | collective-permute-done | bytes 524320 | tf_op jit(solution)/shard_map/ppermute | solution.py:307
  25.3 0.0 collective-permute-done.1
  25.3 0.1 add_add_fusion.1
  25.5 11.3 %all_to_all.45 = f32[4,256,128]{2,1,0:T(8,128)S(1)} all-to-all(f32[4,256,128]{2,1,0:T(8,128)S(1)} %bitcast.14), channel_id=1, replica_groups=mesh['y'=8,'z'=8,'c'=2,'grp'=4] {'grp'}, dimensions={0} | all-to-all | bytes 1048576 | tf_op jit(solution)/shard_map/all_to_all | solution.py:254
  36.8 10.5 %all_to_all.46 = f32[4,256,128]{2,1,0:T(8,128)S(1)} all-to-all(f32[4,256,128]{2,1,0:T(8,128)S(1)} %broadcast_in_dim.15), channel_id=1, replica_groups=mesh['y'=8,'z'=8,'c'=2,'grp'=4] {'grp'}, dimensions={0} | all-to-all | bytes 1048576 | tf_op jit(solution)/shard_map/all_to_all | solution.py:254
  47.3 1.9 %collective-permute-start.3 = (f32[16,64,128]{2,1,0:T(8,128)S(1)}, f32[16,64,128]{2,1,0:T(8,128)S(1)}, u32[]{:S(2)}, u32[]{:S(2)}) collective-permute-start(f32[16,64,128]{2,1,0:T(8,128)S(1)} %bitcast.7), channel_id=1, source_target_pairs={{0,4},{4,0},{8,12},{12,8},{16,20},{20,16},{24,28},{28,24},{32,36},... | collective-permute-start | bytes 1572872 | tf_op jit(solution)/shard_map/ppermute | solution.py:308
  49.2 6.8 %collective-permute-start.2 = (f32[16,64,128]{2,1,0:T(8,128)S(1)}, f32[16,64,128]{2,1,0:T(8,128)S(1)}, u32[]{:S(2)}, u32[]{:S(2)}) collective-permute-start(f32[16,64,128]{2,1,0:T(8,128)S(1)} %bitcast.8), channel_id=1, source_target_pairs={{0,508},{4,8},{8,4},{12,16},{16,12},{20,24},{24,20},{28,32},{32,28... | collective-permute-start | bytes 1572872 | tf_op jit(solution)/shard_map/ppermute | solution.py:307
  56.0 0.0 collective-permute-done.3.s_partner
  56.0 7.0 %collective-permute-done.2.s_outer = f32[16,64,128]{2,1,0:T(8,128)S(1)} collective-permute-done((f32[16,64,128]{2,1,0:T(8,128)S(1)}, f32[16,64,128]{2,1,0:T(8,128)S(1)}, u32[]{:S(2)}, u32[]{:S(2)}) %collective-permute-start.2) | collective-permute-done | bytes 524320 | tf_op jit(solution)/shard_map/ppermute | solution.py:307
  63.0 3.3 %shard_map.47 = (f32[16,64,128]{2,1,0:T(8,128)S(1)}, f32[16,64,128]{2,1,0:T(8,128)S(1)}, f32[16,64,128]{2,1,0:T(8,128)S(1)}, f32[8,24,128]{2,1,0:T(8,128)S(1)}) custom-call(s32[48]{0:T(128)S(1)} %get-tuple-element.19.code, s32[1]{0:T(128)S(6)} %copy.5.live, f32[48,128,128]{2,1,0:T(8,128)} %tiles.5, f32[16,64,128]{2,1,0:T(8,128)S(1)} %collective-permute-done.2.s_outer, ...), custom_call_target="tpu_custom_call" | custom-call | tf_op jit(solution)/shard_map/pallas_call | solution.py:347
  66.3 8.6 %collective-permute-start.4 = (f32[16,64,128]{2,1,0:T(8,128)S(1)}, f32[16,64,128]{2,1,0:T(8,128)S(1)}, u32[]{:S(2)}, u32[]{:S(2)}) collective-permute-start(f32[16,64,128]{2,1,0:T(8,128)S(1)} %get-tuple-element.24), channel_id=1, source_target_pairs={{0,508},{4,8},{8,4},{12,16},{16,12},{20,24},{24,20},{28,32},{32,28... | collective-permute-start | bytes 1572872 | tf_op jit(solution)/shard_map/ppermute | solution.py:307
  74.9 1.9 %collective-permute-start.5 = (f32[16,64,128]{2,1,0:T(8,128)S(1)}, f32[16,64,128]{2,1,0:T(8,128)S(1)}, u32[]{:S(2)}, u32[]{:S(2)}) collective-permute-start(f32[16,64,128]{2,1,0:T(8,128)S(1)} %get-tuple-element.25), channel_id=1, source_target_pairs={{0,4},{4,0},{8,12},{12,8},{16,20},{20,16},{24,28},{28,24},{32,36},... | collective-permute-start | bytes 1572872 | tf_op jit(solution)/shard_map/ppermute | solution.py:308
  76.8 12.3 %all_to_all.47 = f32[8,24,128]{2,1,0:T(8,128)S(1)} all-to-all(f32[8,24,128]{2,1,0:T(8,128)S(1)} %get-tuple-element.26), channel_id=1, replica_groups=mesh['y'=8,'z'=8,'c'=2,'grp'=4] {'y'}, dimensions={0} | all-to-all | bytes 196608 | tf_op jit(solution)/shard_map/all_to_all | solution.py:254
  89.1 0.0 collective-permute-done.4
  89.1 0.0 collective-permute-done.5
  89.1 0.1 add_add_fusion
  89.3 13.0 %all_to_all.48.pieces = f32[4,280,128]{2,1,0:T(8,128)S(1)} all-to-all(f32[4,280,128]{2,1,0:T(8,128)S(1)} %pad_maximum_fusion), channel_id=1, replica_groups=mesh['y'=8,'z'=8,'c'=2,'grp'=4] {'grp'}, dimensions={0} | all-to-all | bytes 1146880 | tf_op jit(solution)/shard_map/all_to_all | solution.py:254
  102.3 0.8 shard_map.48
  103.1 4.9 %all-to-all-start.4 = ((f32[4,256,128]{2,1,0:T(8,128)}), f32[4,256,128]{2,1,0:T(8,128)S(1)}, u32[]{:S(2)}, u32[]{:S(2)}) async-start(f32[4,256,128]{2,1,0:T(8,128)} %get-tuple-element.27), calls=%async_computation.4 | async-start | bytes 1048576 | tf_op jit(solution)/shard_map/all_to_all | solution.py:254
  108.0 1.9 %collective-permute-start.6 = (f32[24,128]{1,0:T(8,128)S(1)}, f32[24,128]{1,0:T(8,128)S(1)}, u32[]{:S(2)}, u32[]{:S(2)}) collective-permute-start(f32[24,128]{1,0:T(8,128)S(1)} %get-tuple-element.28), channel_id=1, source_target_pairs={{0,4},{4,0},{8,12},{12,8},{16,20},{20,16},{24,28},{28,24},{32,36},... | collective-permute-start | bytes 36872 | tf_op jit(solution)/shard_map/ppermute | solution.py:331
  109.9 1.1 collective-permute-done.6
  111.0 3.6 %all-to-all-done.4 = f32[4,256,128]{2,1,0:T(8,128)S(1)} async-done(((f32[4,256,128]{2,1,0:T(8,128)}), f32[4,256,128]{2,1,0:T(8,128)S(1)}, u32[]{:S(2)}, u32[]{:S(2)}) %all-to-all-start.4) | async-done | bytes 524320 | tf_op jit(solution)/shard_map/all_to_all | solution.py:254
  114.6 1.9 %collective-permute-start.8 = (f32[16,64,128]{2,1,0:T(8,128)S(1)}, f32[16,64,128]{2,1,0:T(8,128)S(1)}, u32[]{:S(2)}, u32[]{:S(2)}) collective-permute-start(f32[16,64,128]{2,1,0:T(8,128)S(1)} %bitcast.10), channel_id=1, source_target_pairs={{0,4},{4,0},{8,12},{12,8},{16,20},{20,16},{24,28},{28,24},{32,36},... | collective-permute-start | bytes 1572872 | tf_op jit(solution)/shard_map/ppermute | solution.py:308
  116.5 1.9 %collective-permute-start.7 = (f32[16,64,128]{2,1,0:T(8,128)S(1)}, f32[16,64,128]{2,1,0:T(8,128)S(1)}, u32[]{:S(2)}, u32[]{:S(2)}) collective-permute-start(f32[16,64,128]{2,1,0:T(8,128)S(1)} %bitcast.11), channel_id=1, source_target_pairs={{0,508},{4,8},{8,4},{12,16},{16,12},{20,24},{24,20},{28,32},{32,28... | collective-permute-start | bytes 1572872 | tf_op jit(solution)/shard_map/ppermute | solution.py:307
  118.5 14.0 %all_to_all.49.parts = f32[8,24,128]{2,1,0:T(8,128)S(1)} all-to-all(f32[8,24,128]{2,1,0:T(8,128)S(1)} %broadcast_in_dim.17), channel_id=1, replica_groups=mesh['y'=8,'z'=8,'c'=2,'grp'=4] {'z'}, dimensions={0} | all-to-all | bytes 196608 | tf_op jit(solution)/shard_map/all_to_all | solution.py:254
  132.5 2.0 %shard_map.49.linv = f32[64,64]{1,0:T(8,128)S(1)} custom-call(f32[8,24,128]{2,1,0:T(8,128)S(1)} %all_to_all.49.parts), custom_call_target="tpu_custom_call" | custom-call | tf_op jit(solution)/shard_map/pallas_call | solution.py:355
  134.5 0.0 collective-permute-done.8.s_partner
  134.5 0.0 collective-permute-done.7.s_outer
  134.5 2.9 %shard_map.50 = (f32[64,512]{1,0:T(8,128)S(1)}, f32[8,24,128]{2,1,0:T(8,128)S(1)}) custom-call(s32[48]{0:T(128)S(1)} %get-tuple-element.19.code, s32[1]{0:T(128)S(6)} %copy.5.live, f32[48,128,128]{2,1,0:T(8,128)} %tiles.5, f32[16,64,128]{2,1,0:T(8,128)S(1)} %collective-permute-done.7.s_outer, f32[16,64,128]{2,1,0:T(8,128)S(1)} %bitcast.12, ...), custom_call_target="tpu_custom_call" | custom-call | tf_op jit(solution)/shard_map/pallas_call | solution.py:356
  137.4 9.0 %all_to_all.50 = f32[8,24,128]{2,1,0:T(8,128)S(1)} all-to-all(f32[8,24,128]{2,1,0:T(8,128)S(1)} %get-tuple-element.31), channel_id=1, replica_groups=mesh['y'=8,'z'=8,'c'=2,'grp'=4] {'c','grp'}, dimensions={0} | all-to-all | bytes 196608 | tf_op jit(solution)/shard_map/all_to_all | solution.py:254
  146.4 11.7 %all_to_all.51 = f32[8,24,128]{2,1,0:T(8,128)S(1)} all-to-all(f32[8,24,128]{2,1,0:T(8,128)S(1)} %broadcast_in_dim.18), channel_id=1, replica_groups=mesh['y'=8,'z'=8,'c'=2,'grp'=4] {'z'}, dimensions={0} | all-to-all | bytes 196608 | tf_op jit(solution)/shard_map/all_to_all | solution.py:254
  158.2 11.2 %all_to_all.52.parts = f32[8,24,128]{2,1,0:T(8,128)S(1)} all-to-all(f32[8,24,128]{2,1,0:T(8,128)S(1)} %broadcast_in_dim.19), channel_id=1, replica_groups=mesh['y'=8,'z'=8,'c'=2,'grp'=4] {'y'}, dimensions={0} | all-to-all | bytes 196608 | tf_op jit(solution)/shard_map/all_to_all | solution.py:254
  169.3 2.9 %shard_map.51 = f32[64,512]{1,0:T(8,128)} custom-call(f32[8,24,128]{2,1,0:T(8,128)S(1)} %all_to_all.52.parts, f32[64,512]{1,0:T(8,128)S(1)} %get-tuple-element.32.image), custom_call_target="tpu_custom_call" | custom-call | tf_op jit(solution)/shard_map/pallas_call | solution.py:361
  (11 shorter events, 0.2 us)
Async XLA Ops:
  3.8 21.5 %collective-permute-start = (f32[16,64,128]{2,1,0:T(8,128)S(1)}, f32[16,64,128]{2,1,0:T(8,128)S(1)}, u32[]{:S(2)}, u32[]{:S(2)}) collective-permute-start(f32[16,64,128]{2,1,0:T(8,128)S(1)} %get-tuple-element.21), channel_id=1, source_target_pairs={{0,508},{4,8},{8,4},{12,16},{16,12},{20,24},{24,20},{28,32},{32,28... | collective-permute-start | bytes 1572872 | tf_op jit(solution)/shard_map/ppermute | solution.py:307
  18.5 6.9 %collective-permute-start.1 = (f32[16,64,128]{2,1,0:T(8,128)S(1)}, f32[16,64,128]{2,1,0:T(8,128)S(1)}, u32[]{:S(2)}, u32[]{:S(2)}) collective-permute-start(f32[16,64,128]{2,1,0:T(8,128)S(1)} %get-tuple-element.22), channel_id=1, source_target_pairs={{0,4},{4,0},{8,12},{12,8},{16,20},{20,16},{24,28},{28,24},{32,36},... | collective-permute-start | bytes 1572872 | tf_op jit(solution)/shard_map/ppermute | solution.py:308
  47.3 8.7 %collective-permute-start.3 = (f32[16,64,128]{2,1,0:T(8,128)S(1)}, f32[16,64,128]{2,1,0:T(8,128)S(1)}, u32[]{:S(2)}, u32[]{:S(2)}) collective-permute-start(f32[16,64,128]{2,1,0:T(8,128)S(1)} %bitcast.7), channel_id=1, source_target_pairs={{0,4},{4,0},{8,12},{12,8},{16,20},{20,16},{24,28},{28,24},{32,36},... | collective-permute-start | bytes 1572872 | tf_op jit(solution)/shard_map/ppermute | solution.py:308
  49.2 13.8 %collective-permute-start.2 = (f32[16,64,128]{2,1,0:T(8,128)S(1)}, f32[16,64,128]{2,1,0:T(8,128)S(1)}, u32[]{:S(2)}, u32[]{:S(2)}) collective-permute-start(f32[16,64,128]{2,1,0:T(8,128)S(1)} %bitcast.8), channel_id=1, source_target_pairs={{0,508},{4,8},{8,4},{12,16},{16,12},{20,24},{24,20},{28,32},{32,28... | collective-permute-start | bytes 1572872 | tf_op jit(solution)/shard_map/ppermute | solution.py:307
  66.3 22.8 %collective-permute-start.4 = (f32[16,64,128]{2,1,0:T(8,128)S(1)}, f32[16,64,128]{2,1,0:T(8,128)S(1)}, u32[]{:S(2)}, u32[]{:S(2)}) collective-permute-start(f32[16,64,128]{2,1,0:T(8,128)S(1)} %get-tuple-element.24), channel_id=1, source_target_pairs={{0,508},{4,8},{8,4},{12,16},{16,12},{20,24},{24,20},{28,32},{32,28... | collective-permute-start | bytes 1572872 | tf_op jit(solution)/shard_map/ppermute | solution.py:307
  74.9 14.2 %collective-permute-start.5 = (f32[16,64,128]{2,1,0:T(8,128)S(1)}, f32[16,64,128]{2,1,0:T(8,128)S(1)}, u32[]{:S(2)}, u32[]{:S(2)}) collective-permute-start(f32[16,64,128]{2,1,0:T(8,128)S(1)} %get-tuple-element.25), channel_id=1, source_target_pairs={{0,4},{4,0},{8,12},{12,8},{16,20},{20,16},{24,28},{28,24},{32,36},... | collective-permute-start | bytes 1572872 | tf_op jit(solution)/shard_map/ppermute | solution.py:308
  103.1 11.5 %all-to-all-start.4 = ((f32[4,256,128]{2,1,0:T(8,128)}), f32[4,256,128]{2,1,0:T(8,128)S(1)}, u32[]{:S(2)}, u32[]{:S(2)}) async-start(f32[4,256,128]{2,1,0:T(8,128)} %get-tuple-element.27), calls=%async_computation.4 | async-start | bytes 1048576 | tf_op jit(solution)/shard_map/all_to_all | solution.py:254
  108.0 3.1 %collective-permute-start.6 = (f32[24,128]{1,0:T(8,128)S(1)}, f32[24,128]{1,0:T(8,128)S(1)}, u32[]{:S(2)}, u32[]{:S(2)}) collective-permute-start(f32[24,128]{1,0:T(8,128)S(1)} %get-tuple-element.28), channel_id=1, source_target_pairs={{0,4},{4,0},{8,12},{12,8},{16,20},{20,16},{24,28},{28,24},{32,36},... | collective-permute-start | bytes 36872 | tf_op jit(solution)/shard_map/ppermute | solution.py:331
  114.6 19.9 %collective-permute-start.8 = (f32[16,64,128]{2,1,0:T(8,128)S(1)}, f32[16,64,128]{2,1,0:T(8,128)S(1)}, u32[]{:S(2)}, u32[]{:S(2)}) collective-permute-start(f32[16,64,128]{2,1,0:T(8,128)S(1)} %bitcast.10), channel_id=1, source_target_pairs={{0,4},{4,0},{8,12},{12,8},{16,20},{20,16},{24,28},{28,24},{32,36},... | collective-permute-start | bytes 1572872 | tf_op jit(solution)/shard_map/ppermute | solution.py:308
  116.5 18.0 %collective-permute-start.7 = (f32[16,64,128]{2,1,0:T(8,128)S(1)}, f32[16,64,128]{2,1,0:T(8,128)S(1)}, u32[]{:S(2)}, u32[]{:S(2)}) collective-permute-start(f32[16,64,128]{2,1,0:T(8,128)S(1)} %bitcast.11), channel_id=1, source_target_pairs={{0,508},{4,8},{8,4},{12,16},{16,12},{20,24},{24,20},{28,32},{32,28... | collective-permute-start | bytes 1572872 | tf_op jit(solution)/shard_map/ppermute | solution.py:307

commit v8 on v6

--- a/solution.py
+++ b/solution.py
@@ -16,7 +16,9 @@
 BF16 = jnp.bfloat16
 T = 128
 CHUNK = 8
+L1, L2, L3 = 16 << 20, 16 << 20, 50 << 20
 VMEM_LIMIT = 50 * 1024 * 1024
+SMALL_LIMIT = 8 * 1024 * 1024
 
 
 def dot(a, b, contract, precision=None):
@@ -89,7 +91,7 @@
 
 
 def first_kernel(
-    coords, live, tiles, sketch, outer, own, partner, code, tbuf, panel, phl, acc, sems, panel_sem, *, rows
+    coords, live, tiles, sketch, outer, own, partner, code, thl, tbuf, panel, phl, acc, sems, panel_sem, *, rows
 ):
     cap = tiles.shape[0]
     k = sketch.shape[0]
@@ -101,12 +103,14 @@
         code[s] = slot_code(s, coords, live[0], outer.shape[0], phl.shape[0], rows)
     panel_copy.wait()
     keep_panel(lambda t: panel[:, t * T : (t + 1) * T], k, phl)
-    each_chunk(
-        live[0],
-        cap,
-        lambda s: spread_slot(code[s], *halves(tbuf[s]), phl, acc),
-        lambda c: tile_copy(c, tiles, tbuf, sems).wait(),
-    )
+
+    def work(s):
+        hi, lo = halves(tbuf[s])
+        thl[s, :T, :] = hi
+        thl[s, T:, :] = lo
+        spread_slot(code[s], hi, lo, phl, acc)
+
+    each_chunk(live[0], cap, work, lambda c: tile_copy(c, tiles, tbuf, sems).wait())
     put_spread(acc, (outer, own, partner))
 
 
@@ -125,10 +129,9 @@
     shl[3 * each] = jnp.zeros_like(shl[3 * each])
 
 
-def image_slot(entry, hi, lo, shl, img):
+def image_slot(entry, hl, shl, img):
     k = shl.shape[1] // 2
-    q = dot(shl[entry & 255], jnp.concatenate([hi, lo], axis=0), (1, 1))
-    img[entry >> 8] += fold(q, k)
+    img[entry >> 8] += fold(dot(shl[entry & 255], hl, (1, 1)), k)
 
 
 def whole_image(img):
@@ -147,27 +150,40 @@
 
 
 def middle_kernel(
-    code, live, tiles, s_outer, s_own, s_partner, outer, own, partner, gram,
-    tbuf, thl, shl, img, phl, acc, sems,
+    code, live, thl, s_outer, s_own, s_partner, outer, own, partner, gram, shl, img, phl, acc
 ):
-    cap = tiles.shape[0]
+    cap = thl.shape[0]
     k = s_own.shape[1]
-    start_tiles(live[0], tiles, tbuf, sems)
     keep_spread((s_outer, s_own, s_partner), shl)
     img[...] = jnp.zeros_like(img)
     acc[...] = jnp.zeros_like(acc)
-
-    def forth(s):
-        hi, lo = halves(tbuf[s])
-        thl[s, :T, :] = hi
-        thl[s, T:, :] = lo
-        image_slot(code[s], hi, lo, shl, img)
-
-    each_chunk(live[0], cap, forth, lambda c: tile_copy(c, tiles, tbuf, sems).wait())
+    each_chunk(live[0], cap, lambda s: image_slot(code[s], thl[s], shl, img))
     put_gram(whole_image(img), gram)
     keep_panel(lambda t: img[t], k, phl)
     each_chunk(live[0], cap, lambda s: spread_slot(code[s], thl[s, :T, :], thl[s, T:, :], phl, acc))
     put_spread(acc, (outer, own, partner))
+
+
+def join_kernel(own, outer, partner, out):
+    groups = out.shape[0]
+    mine = own.shape[0] // groups
+    k = own.shape[1]
+    for t in range(own.shape[0]):
+        at = (t % mine) * k
+        out[t // mine, at : at + k, :] = own[t] + outer[t] + partner[t]
+
+
+def sum_of(parts):
+    total = parts[0]
+    for n in range(1, parts.shape[0]):
+        total = total + parts[n]
+    return total
+
+
+def fan_kernel(parts, copies):
+    total = sum_of(parts)
+    for n in range(copies.shape[0]):
+        copies[n] = total
 
 
 def share_kernel(pieces, whole, gram):
@@ -237,7 +253,7 @@
     each_chunk(
         live[0],
         tiles.shape[0],
-        lambda s: image_slot(code[s], *halves(tbuf[s]), shl, img),
+        lambda s: image_slot(code[s], jnp.concatenate(halves(tbuf[s]), axis=0), shl, img),
         lambda c: tile_copy(c, tiles, tbuf, sems).wait(),
     )
     x = dot(linv[...], whole_image(img), (1, 0), HIGHEST)
@@ -294,7 +310,6 @@
     partner = [(r, r ^ 1) for r in range(rows)]
 
     tbuf = pltpu.VMEM((cap, T, T), F32)
-    thl = pltpu.VMEM((cap, 2 * T, T), BF16)
     panel = pltpu.VMEM((k, mine * T), F32)
     phl = pltpu.VMEM((mine, 2 * k, T), BF16)
     shl = pltpu.VMEM((3 * block + 1, 2 * k, T), BF16)
@@ -308,14 +323,17 @@
         got_partner = lax.ppermute(to_partner, ROWS, partner)
         return got_outer, got_partner
 
-    def pieces(x):
-        return x.reshape(groups, mine * k, T)
+    def small(kernel, outs, *args):
+        return call(kernel, [VMEM] * len(args), outs, limit=SMALL_LIMIT)(*args)
+
+    whole_out = ((groups, mine * k, T), F32)
 
     def exchange(parts):
         p_outer, p_own, p_partner = parts
         got_outer, got = over_pairs(p_outer, p_partner)
-        total = p_own + got_outer + got
-        own = to_everyone(swapped(pieces(total), "grp").sum(axis=0), "grp").reshape(block, k, T)
+        (total,) = small(join_kernel, [whole_out], p_own, got_outer, got)
+        (copies,) = small(fan_kernel, [whole_out], swapped(total, "grp"))
+        own = swapped(copies, "grp").reshape(block, k, T)
         at_outer, at_partner = over_pairs(own, own)
         return at_outer, own, at_partner
 
@@ -323,7 +341,7 @@
         p_outer, p_own, p_partner = parts
         gram = swapped(gram, "y")
         got_outer, got = over_pairs(p_outer, p_partner)
-        total = pieces(p_own + got_outer + got)
+        total = (p_own + got_outer + got).reshape(groups, mine * k, T)
         sides = jnp.broadcast_to(gram.sum(axis=0), (groups, *packed))
         arrived = swapped(jnp.concatenate([total, sides], axis=1), "grp")
         copies, gram = call(share_kernel, [VMEM], [((groups, mine * k, T), F32), (packed, F32)])(arrived)
@@ -334,31 +352,38 @@
         at_outer, at_partner = over_pairs(own, own)
         return (at_outer, own, at_partner), gram
 
-    *parts, code = call(
+    *parts, code, thl = call(
         functools.partial(first_kernel, rows=rows),
         [HBM, HBM],
-        [block_out] * 3 + [((cap,), jnp.int32)],
+        [block_out] * 3 + [((cap,), jnp.int32), ((cap, 2 * T, T), BF16)],
         [tbuf, panel, phl, acc, sems, pltpu.SemaphoreType.DMA],
         2,
-        [VMEM] * 3 + [SMEM],
-    )(in_space(coords.T, pltpu.HBM), live, tiles, in_space(sketch.T, pltpu.HBM))
+        [VMEM] * 3 + [SMEM, VMEM],
+        L1,
+    )(in_space(coords.T, pltpu.HBM), live, in_space(tiles, pltpu.HBM), in_space(sketch.T, pltpu.HBM))
     whole = exchange(parts)
     *parts, gram = call(
         middle_kernel,
-        [HBM] + [VMEM] * 3,
+        [VMEM] * 4,
         [block_out] * 3 + [((lax.axis_size("y"), *packed), F32)],
-        [tbuf, thl, shl, img, phl, acc, sems],
+        [shl, img, phl, acc],
         2,
-    )(code, live, tiles, *whole)
+        limit=L2,
+    )(code, live, thl, *whole)
     whole, gram = exchange_with_gram(parts, gram)
-    linv = call(factor_kernel, [VMEM], [((k, k), F32)])(gram)[0]
+    linv = call(factor_kernel, [VMEM], [((k, k), F32)], limit=SMALL_LIMIT)(gram)[0]
     image, gram = call(
-        last_kernel, [HBM] + [VMEM] * 4, [((k, mine * T), F32), ((2 * groups, *packed), F32)], [tbuf, shl, img, sems], 2
+        last_kernel,
+        [HBM] + [VMEM] * 4,
+        [((k, mine * T), F32), ((2 * groups, *packed), F32)],
+        [tbuf, shl, img, sems],
+        2,
+        limit=L3,
     )(code, live, tiles, *whole, linv)
     gram = to_everyone(swapped(gram, ("c", "grp")).sum(axis=0), "z").sum(axis=0)
     scale = float(rows * groups * sketch.shape[0]) ** 0.5
     return call(
-        functools.partial(basis_kernel, scale=scale), [VMEM] * 2, [(sketch.shape[::-1], F32)]
+        functools.partial(basis_kernel, scale=scale), [VMEM] * 2, [(sketch.shape[::-1], F32)], limit=SMALL_LIMIT
     )(to_everyone(gram, "y"), image)[0].T
 
 

time: 173 us -> 172 us (level)
    pallas_call x2 -> x4, Pallas kernels: 5.31 us -> 4.61 us  [the longest x1 2.48 us: local(): call(middle_kernel, [VMEM] * 4, [block_out] * 3 + [((lax.axis_size('y'),...]
where the time goes in v8:
time: 172 us; the launch traced here: 171 us
  blocking collectives  92.8 us (54%)
  starting transfers between devices  46.4 us (27%)
  waiting for transfers between devices  16.6 us (10%)
  Pallas kernels  14.5 us (8%)
    all_to_all x8, blocking collectives, swapped(): return lax.all_to_all(copies, axes, split_axis=0, concat_axis=0, tiled=True)  92.8 us
    ppermute x4, starting transfers between devices, over_pairs(): got_outer = lax.ppermute(to_outer, ROWS, outer)  32 us
    ppermute x4, waiting for transfers between devices, over_pairs(): got_outer = lax.ppermute(to_outer, ROWS, outer)  11.9 us
    ppermute x4, starting transfers between devices, over_pairs(): got_partner = lax.ppermute(to_partner, ROWS, partner)  7.66 us
    all_to_all x1, starting transfers between devices, swapped(): return lax.all_to_all(copies, axes, split_axis=0, concat_axis=0, tiled=True)  4.89 us
    all_to_all x1, waiting for transfers between devices, swapped(): return lax.all_to_all(copies, axes, split_axis=0, concat_axis=0, tiled=True)  3.56 us
  transfers between devices with their start and end apart: 10, of which 4 were waited for; matrix products, arithmetic and copies ran while one was open for 0% of the time, Pallas kernels for 1%

profile of v8, /device:TPU:2, one launch (start us, length us, event | category | flops | bytes accessed | tf_op | source)
XLA Modules:
  0.0 171.4 jit_solution(7445061331198282908)
XLA Ops:
  0.7 3.2 %shard_map.46 = (f32[16,64,128]{2,1,0:T(8,128)S(1)}, f32[16,64,128]{2,1,0:T(8,128)S(1)}, f32[16,64,128]{2,1,0:T(8,128)S(1)}, s32[48]{0:T(128)S(1)}, bf16[48,256,128]{2,1,0:T(8,128)(2,1)S(1)}) custom-call(s32[2,48]{1,0:T(2,128)} %bitcast.14, s32[1]{0:T(128)S(6)} %copy.5.live, f32[48,128,128]{2,1,0:T(8,128)} %tiles.3, f32[64,512]{1,0:T(8,128)} %bitcast.13), custom_call_target="tpu_custom_call" | custom-call | tf_op jit(solution)/shard_map/pallas_call | solution.py:355
  3.9 14.7 %collective-permute-start = (f32[16,64,128]{2,1,0:T(8,128)S(1)}, f32[16,64,128]{2,1,0:T(8,128)S(1)}, u32[]{:S(2)}, u32[]{:S(2)}) collective-permute-start(f32[16,64,128]{2,1,0:T(8,128)S(1)} %get-tuple-element.23), channel_id=1, source_target_pairs={{0,508},{4,8},{8,4},{12,16},{16,12},{20,24},{24,20},{28,32},{32,28... | collective-permute-start | bytes 1572872 | tf_op jit(solution)/shard_map/ppermute | solution.py:322
  18.5 1.9 %collective-permute-start.1 = (f32[16,64,128]{2,1,0:T(8,128)S(1)}, f32[16,64,128]{2,1,0:T(8,128)S(1)}, u32[]{:S(2)}, u32[]{:S(2)}) collective-permute-start(f32[16,64,128]{2,1,0:T(8,128)S(1)} %get-tuple-element.24), channel_id=1, source_target_pairs={{0,4},{4,0},{8,12},{12,8},{16,20},{20,16},{24,28},{28,24},{32,36},... | collective-permute-start | bytes 1572872 | tf_op jit(solution)/shard_map/ppermute | solution.py:323
  20.5 4.9 %collective-permute-done.outer = f32[16,64,128]{2,1,0:T(8,128)S(1)} collective-permute-done((f32[16,64,128]{2,1,0:T(8,128)S(1)}, f32[16,64,128]{2,1,0:T(8,128)S(1)}, u32[]{:S(2)}, u32[]{:S(2)}) %collective-permute-start) | collective-permute-done | bytes 524320 | tf_op jit(solution)/shard_map/ppermute | solution.py:322
  25.4 0.0 collective-permute-done.1.partner
  25.4 0.1 shard_map.47
  25.5 11.3 %all_to_all.45.parts = f32[4,256,128]{2,1,0:T(8,128)S(1)} all-to-all(f32[4,256,128]{2,1,0:T(8,128)S(1)} %shard_map.47), channel_id=1, replica_groups=mesh['y'=8,'z'=8,'c'=2,'grp'=4] {'grp'}, dimensions={0} | all-to-all | bytes 1048576 | tf_op jit(solution)/shard_map/all_to_all | solution.py:270
  36.8 10.5 %all_to_all.46 = f32[4,256,128]{2,1,0:T(8,128)S(1)} all-to-all(f32[4,256,128]{2,1,0:T(8,128)S(1)} %shard_map.48), channel_id=1, replica_groups=mesh['y'=8,'z'=8,'c'=2,'grp'=4] {'grp'}, dimensions={0} | all-to-all | bytes 1048576 | tf_op jit(solution)/shard_map/all_to_all | solution.py:270
  47.3 1.9 %collective-permute-start.3 = (f32[16,64,128]{2,1,0:T(8,128)S(1)}, f32[16,64,128]{2,1,0:T(8,128)S(1)}, u32[]{:S(2)}, u32[]{:S(2)}) collective-permute-start(f32[16,64,128]{2,1,0:T(8,128)S(1)} %bitcast.6), channel_id=1, source_target_pairs={{0,4},{4,0},{8,12},{12,8},{16,20},{20,16},{24,28},{28,24},{32,36},... | collective-permute-start | bytes 1572872 | tf_op jit(solution)/shard_map/ppermute | solution.py:323
  49.2 6.8 %collective-permute-start.2 = (f32[16,64,128]{2,1,0:T(8,128)S(1)}, f32[16,64,128]{2,1,0:T(8,128)S(1)}, u32[]{:S(2)}, u32[]{:S(2)}) collective-permute-start(f32[16,64,128]{2,1,0:T(8,128)S(1)} %bitcast.7), channel_id=1, source_target_pairs={{0,508},{4,8},{8,4},{12,16},{16,12},{20,24},{24,20},{28,32},{32,28... | collective-permute-start | bytes 1572872 | tf_op jit(solution)/shard_map/ppermute | solution.py:322
  56.0 0.0 collective-permute-done.3.s_partner
  56.0 7.0 %collective-permute-done.2.s_outer = f32[16,64,128]{2,1,0:T(8,128)S(1)} collective-permute-done((f32[16,64,128]{2,1,0:T(8,128)S(1)}, f32[16,64,128]{2,1,0:T(8,128)S(1)}, u32[]{:S(2)}, u32[]{:S(2)}) %collective-permute-start.2) | collective-permute-done | bytes 524320 | tf_op jit(solution)/shard_map/ppermute | solution.py:322
  63.0 2.5 %shard_map.49 = (f32[16,64,128]{2,1,0:T(8,128)S(1)}, f32[16,64,128]{2,1,0:T(8,128)S(1)}, f32[16,64,128]{2,1,0:T(8,128)S(1)}, f32[8,24,128]{2,1,0:T(8,128)S(1)}) custom-call(s32[48]{0:T(128)S(1)} %get-tuple-element.20.code, s32[1]{0:T(128)S(6)} %copy.5.live, bf16[48,256,128]{2,1,0:T(8,128)(2,1)S(1)} %get-tuple-element.21.thl, ...), custom_call_target="tpu_custom_call" | custom-call | tf_op jit(solution)/shard_map/pallas_call | solution.py:365
  65.5 8.6 %collective-permute-start.4 = (f32[16,64,128]{2,1,0:T(8,128)S(1)}, f32[16,64,128]{2,1,0:T(8,128)S(1)}, u32[]{:S(2)}, u32[]{:S(2)}) collective-permute-start(f32[16,64,128]{2,1,0:T(8,128)S(1)} %get-tuple-element.26), channel_id=1, source_target_pairs={{0,508},{4,8},{8,4},{12,16},{16,12},{20,24},{24,20},{28,32},{32,28... | collective-permute-start | bytes 1572872 | tf_op jit(solution)/shard_map/ppermute | solution.py:322
  74.1 1.9 %collective-permute-start.5 = (f32[16,64,128]{2,1,0:T(8,128)S(1)}, f32[16,64,128]{2,1,0:T(8,128)S(1)}, u32[]{:S(2)}, u32[]{:S(2)}) collective-permute-start(f32[16,64,128]{2,1,0:T(8,128)S(1)} %get-tuple-element.27), channel_id=1, source_target_pairs={{0,4},{4,0},{8,12},{12,8},{16,20},{20,16},{24,28},{28,24},{32,36},... | collective-permute-start | bytes 1572872 | tf_op jit(solution)/shard_map/ppermute | solution.py:323
  76.0 12.2 %all_to_all.47 = f32[8,24,128]{2,1,0:T(8,128)S(1)} all-to-all(f32[8,24,128]{2,1,0:T(8,128)S(1)} %get-tuple-element.28), channel_id=1, replica_groups=mesh['y'=8,'z'=8,'c'=2,'grp'=4] {'y'}, dimensions={0} | all-to-all | bytes 196608 | tf_op jit(solution)/shard_map/all_to_all | solution.py:270
  88.3 0.0 collective-permute-done.4
  88.3 0.0 collective-permute-done.5
  88.3 0.1 add_add_fusion
  88.5 12.9 %all_to_all.48.pieces = f32[4,280,128]{2,1,0:T(8,128)S(1)} all-to-all(f32[4,280,128]{2,1,0:T(8,128)S(1)} %pad_maximum_fusion), channel_id=1, replica_groups=mesh['y'=8,'z'=8,'c'=2,'grp'=4] {'grp'}, dimensions={0} | all-to-all | bytes 1146880 | tf_op jit(solution)/shard_map/all_to_all | solution.py:270
  101.4 0.8 shard_map.50
  102.3 4.9 %all-to-all-start.4 = ((f32[4,256,128]{2,1,0:T(8,128)}), f32[4,256,128]{2,1,0:T(8,128)S(1)}, u32[]{:S(2)}, u32[]{:S(2)}) async-start(f32[4,256,128]{2,1,0:T(8,128)} %get-tuple-element.29), calls=%async_computation.4 | async-start | bytes 1048576 | tf_op jit(solution)/shard_map/all_to_all | solution.py:270
  107.1 1.9 %collective-permute-start.6 = (f32[24,128]{1,0:T(8,128)S(1)}, f32[24,128]{1,0:T(8,128)S(1)}, u32[]{:S(2)}, u32[]{:S(2)}) collective-permute-start(f32[24,128]{1,0:T(8,128)S(1)} %get-tuple-element.30), channel_id=1, source_target_pairs={{0,4},{4,0},{8,12},{12,8},{16,20},{20,16},{24,28},{28,24},{32,36},... | collective-permute-start | bytes 36872 | tf_op jit(solution)/shard_map/ppermute | solution.py:349
  109.1 1.1 collective-permute-done.6
  110.2 3.6 %all-to-all-done.4 = f32[4,256,128]{2,1,0:T(8,128)S(1)} async-done(((f32[4,256,128]{2,1,0:T(8,128)}), f32[4,256,128]{2,1,0:T(8,128)S(1)}, u32[]{:S(2)}, u32[]{:S(2)}) %all-to-all-start.4) | async-done | bytes 524320 | tf_op jit(solution)/shard_map/all_to_all | solution.py:270
  113.8 1.9 %collective-permute-start.8 = (f32[16,64,128]{2,1,0:T(8,128)S(1)}, f32[16,64,128]{2,1,0:T(8,128)S(1)}, u32[]{:S(2)}, u32[]{:S(2)}) collective-permute-start(f32[16,64,128]{2,1,0:T(8,128)S(1)} %bitcast.9), channel_id=1, source_target_pairs={{0,4},{4,0},{8,12},{12,8},{16,20},{20,16},{24,28},{28,24},{32,36},... | collective-permute-start | bytes 1572872 | tf_op jit(solution)/shard_map/ppermute | solution.py:323
  115.7 1.9 %collective-permute-start.7 = (f32[16,64,128]{2,1,0:T(8,128)S(1)}, f32[16,64,128]{2,1,0:T(8,128)S(1)}, u32[]{:S(2)}, u32[]{:S(2)}) collective-permute-start(f32[16,64,128]{2,1,0:T(8,128)S(1)} %bitcast.10), channel_id=1, source_target_pairs={{0,508},{4,8},{8,4},{12,16},{16,12},{20,24},{24,20},{28,32},{32,28... | collective-permute-start | bytes 1572872 | tf_op jit(solution)/shard_map/ppermute | solution.py:322
  117.6 14.0 %all_to_all.49.parts = f32[8,24,128]{2,1,0:T(8,128)S(1)} all-to-all(f32[8,24,128]{2,1,0:T(8,128)S(1)} %broadcast_in_dim.13), channel_id=1, replica_groups=mesh['y'=8,'z'=8,'c'=2,'grp'=4] {'z'}, dimensions={0} | all-to-all | bytes 196608 | tf_op jit(solution)/shard_map/all_to_all | solution.py:270
  131.6 2.0 %shard_map.51.linv = f32[64,64]{1,0:T(8,128)S(1)} custom-call(f32[8,24,128]{2,1,0:T(8,128)S(1)} %all_to_all.49.parts), custom_call_target="tpu_custom_call" | custom-call | tf_op jit(solution)/shard_map/pallas_call | solution.py:374
  133.6 0.0 collective-permute-done.8.s_partner
  133.6 0.0 collective-permute-done.7.s_outer
  133.6 2.9 %shard_map.52 = (f32[64,512]{1,0:T(8,128)S(1)}, f32[8,24,128]{2,1,0:T(8,128)S(1)}) custom-call(s32[48]{0:T(128)S(1)} %get-tuple-element.20.code, s32[1]{0:T(128)S(6)} %copy.5.live, f32[48,128,128]{2,1,0:T(8,128)} %tiles.3, f32[16,64,128]{2,1,0:T(8,128)S(1)} %collective-permute-done.7.s_outer, f32[16,64,128]{2,1,0:T(8,128)S(1)} %bitcast.11, ...), custom_call_target="tpu_custom_call" | custom-call | tf_op jit(solution)/shard_map/pallas_call | solution.py:375
  136.6 9.0 %all_to_all.50 = f32[8,24,128]{2,1,0:T(8,128)S(1)} all-to-all(f32[8,24,128]{2,1,0:T(8,128)S(1)} %get-tuple-element.33), channel_id=1, replica_groups=mesh['y'=8,'z'=8,'c'=2,'grp'=4] {'c','grp'}, dimensions={0} | all-to-all | bytes 196608 | tf_op jit(solution)/shard_map/all_to_all | solution.py:270
  145.6 11.7 %all_to_all.51 = f32[8,24,128]{2,1,0:T(8,128)S(1)} all-to-all(f32[8,24,128]{2,1,0:T(8,128)S(1)} %broadcast_in_dim.14), channel_id=1, replica_groups=mesh['y'=8,'z'=8,'c'=2,'grp'=4] {'z'}, dimensions={0} | all-to-all | bytes 196608 | tf_op jit(solution)/shard_map/all_to_all | solution.py:270
  157.3 11.2 %all_to_all.52.parts = f32[8,24,128]{2,1,0:T(8,128)S(1)} all-to-all(f32[8,24,128]{2,1,0:T(8,128)S(1)} %broadcast_in_dim.15), channel_id=1, replica_groups=mesh['y'=8,'z'=8,'c'=2,'grp'=4] {'y'}, dimensions={0} | all-to-all | bytes 196608 | tf_op jit(solution)/shard_map/all_to_all | solution.py:270
  168.5 2.9 %shard_map.53 = f32[64,512]{1,0:T(8,128)} custom-call(f32[8,24,128]{2,1,0:T(8,128)S(1)} %all_to_all.52.parts, f32[64,512]{1,0:T(8,128)S(1)} %get-tuple-element.34.image), custom_call_target="tpu_custom_call" | custom-call | tf_op jit(solution)/shard_map/pallas_call | solution.py:385
  (10 shorter events, 0.1 us)
Async XLA Ops:
  3.9 21.5 %collective-permute-start = (f32[16,64,128]{2,1,0:T(8,128)S(1)}, f32[16,64,128]{2,1,0:T(8,128)S(1)}, u32[]{:S(2)}, u32[]{:S(2)}) collective-permute-start(f32[16,64,128]{2,1,0:T(8,128)S(1)} %get-tuple-element.23), channel_id=1, source_target_pairs={{0,508},{4,8},{8,4},{12,16},{16,12},{20,24},{24,20},{28,32},{32,28... | collective-permute-start | bytes 1572872 | tf_op jit(solution)/shard_map/ppermute | solution.py:322
  18.5 6.9 %collective-permute-start.1 = (f32[16,64,128]{2,1,0:T(8,128)S(1)}, f32[16,64,128]{2,1,0:T(8,128)S(1)}, u32[]{:S(2)}, u32[]{:S(2)}) collective-permute-start(f32[16,64,128]{2,1,0:T(8,128)S(1)} %get-tuple-element.24), channel_id=1, source_target_pairs={{0,4},{4,0},{8,12},{12,8},{16,20},{20,16},{24,28},{28,24},{32,36},... | collective-permute-start | bytes 1572872 | tf_op jit(solution)/shard_map/ppermute | solution.py:323
  47.3 8.7 %collective-permute-start.3 = (f32[16,64,128]{2,1,0:T(8,128)S(1)}, f32[16,64,128]{2,1,0:T(8,128)S(1)}, u32[]{:S(2)}, u32[]{:S(2)}) collective-permute-start(f32[16,64,128]{2,1,0:T(8,128)S(1)} %bitcast.6), channel_id=1, source_target_pairs={{0,4},{4,0},{8,12},{12,8},{16,20},{20,16},{24,28},{28,24},{32,36},... | collective-permute-start | bytes 1572872 | tf_op jit(solution)/shard_map/ppermute | solution.py:323
  49.2 13.8 %collective-permute-start.2 = (f32[16,64,128]{2,1,0:T(8,128)S(1)}, f32[16,64,128]{2,1,0:T(8,128)S(1)}, u32[]{:S(2)}, u32[]{:S(2)}) collective-permute-start(f32[16,64,128]{2,1,0:T(8,128)S(1)} %bitcast.7), channel_id=1, source_target_pairs={{0,508},{4,8},{8,4},{12,16},{16,12},{20,24},{24,20},{28,32},{32,28... | collective-permute-start | bytes 1572872 | tf_op jit(solution)/shard_map/ppermute | solution.py:322
  65.5 22.8 %collective-permute-start.4 = (f32[16,64,128]{2,1,0:T(8,128)S(1)}, f32[16,64,128]{2,1,0:T(8,128)S(1)}, u32[]{:S(2)}, u32[]{:S(2)}) collective-permute-start(f32[16,64,128]{2,1,0:T(8,128)S(1)} %get-tuple-element.26), channel_id=1, source_target_pairs={{0,508},{4,8},{8,4},{12,16},{16,12},{20,24},{24,20},{28,32},{32,28... | collective-permute-start | bytes 1572872 | tf_op jit(solution)/shard_map/ppermute | solution.py:322
  74.1 14.2 %collective-permute-start.5 = (f32[16,64,128]{2,1,0:T(8,128)S(1)}, f32[16,64,128]{2,1,0:T(8,128)S(1)}, u32[]{:S(2)}, u32[]{:S(2)}) collective-permute-start(f32[16,64,128]{2,1,0:T(8,128)S(1)} %get-tuple-element.27), channel_id=1, source_target_pairs={{0,4},{4,0},{8,12},{12,8},{16,20},{20,16},{24,28},{28,24},{32,36},... | collective-permute-start | bytes 1572872 | tf_op jit(solution)/shard_map/ppermute | solution.py:323
  102.3 11.5 %all-to-all-start.4 = ((f32[4,256,128]{2,1,0:T(8,128)}), f32[4,256,128]{2,1,0:T(8,128)S(1)}, u32[]{:S(2)}, u32[]{:S(2)}) async-start(f32[4,256,128]{2,1,0:T(8,128)} %get-tuple-element.29), calls=%async_computation.4 | async-start | bytes 1048576 | tf_op jit(solution)/shard_map/all_to_all | solution.py:270
  107.1 3.1 %collective-permute-start.6 = (f32[24,128]{1,0:T(8,128)S(1)}, f32[24,128]{1,0:T(8,128)S(1)}, u32[]{:S(2)}, u32[]{:S(2)}) collective-permute-start(f32[24,128]{1,0:T(8,128)S(1)} %get-tuple-element.30), channel_id=1, source_target_pairs={{0,4},{4,0},{8,12},{12,8},{16,20},{20,16},{24,28},{28,24},{32,36},... | collective-permute-start | bytes 36872 | tf_op jit(solution)/shard_map/ppermute | solution.py:349
  113.8 19.9 %collective-permute-start.8 = (f32[16,64,128]{2,1,0:T(8,128)S(1)}, f32[16,64,128]{2,1,0:T(8,128)S(1)}, u32[]{:S(2)}, u32[]{:S(2)}) collective-permute-start(f32[16,64,128]{2,1,0:T(8,128)S(1)} %bitcast.9), channel_id=1, source_target_pairs={{0,4},{4,0},{8,12},{12,8},{16,20},{20,16},{24,28},{28,24},{32,36},... | collective-permute-start | bytes 1572872 | tf_op jit(solution)/shard_map/ppermute | solution.py:323
  115.7 18.0 %collective-permute-start.7 = (f32[16,64,128]{2,1,0:T(8,128)S(1)}, f32[16,64,128]{2,1,0:T(8,128)S(1)}, u32[]{:S(2)}, u32[]{:S(2)}) collective-permute-start(f32[16,64,128]{2,1,0:T(8,128)S(1)} %bitcast.10), channel_id=1, source_target_pairs={{0,508},{4,8},{8,4},{12,16},{16,12},{20,24},{24,20},{28,32},{32,28... | collective-permute-start | bytes 1572872 | tf_op jit(solution)/shard_map/ppermute | solution.py:322

commit v9 on v8

--- a/solution.py
+++ b/solution.py
@@ -91,14 +91,18 @@
 
 
 def first_kernel(
-    coords, live, tiles, sketch, outer, own, partner, code, thl, tbuf, panel, phl, acc, sems, panel_sem, *, rows
+    live, coords_in, tiles, sketch, outer, own, partner, code, thl,
+    coords, tbuf, panel, phl, acc, sems, panel_sem, coords_sem, *, rows
 ):
     cap = tiles.shape[0]
     k = sketch.shape[0]
     panel_copy = pltpu.make_async_copy(sketch, panel, panel_sem)
     panel_copy.start()
+    coords_copy = pltpu.make_async_copy(coords_in, coords, coords_sem)
+    coords_copy.start()
     start_tiles(live[0], tiles, tbuf, sems)
     acc[...] = jnp.zeros_like(acc)
+    coords_copy.wait()
     for s in range(cap):
         code[s] = slot_code(s, coords, live[0], outer.shape[0], phl.shape[0], rows)
     panel_copy.wait()
@@ -182,6 +186,12 @@
 
 def fan_kernel(parts, copies):
     total = sum_of(parts)
+    for n in range(copies.shape[0]):
+        copies[n] = total
+
+
+def pair_kernel(one, other, copies):
+    total = one[...] + other[...]
     for n in range(copies.shape[0]):
         copies[n] = total
 
@@ -347,20 +357,21 @@
         copies, gram = call(share_kernel, [VMEM], [((groups, mine * k, T), F32), (packed, F32)])(arrived)
         own = swapped(copies, "grp").reshape(block, k, T)
         beside = lax.ppermute(gram, ROWS, partner)
-        own, gram = lax.optimization_barrier((own, gram + beside))
-        gram = to_everyone(gram, "z")
+        (copies,) = small(pair_kernel, [((lax.axis_size("z"), *packed), F32)], gram, beside)
+        own, copies = lax.optimization_barrier((own, copies))
+        gram = swapped(copies, "z")
         at_outer, at_partner = over_pairs(own, own)
         return (at_outer, own, at_partner), gram
 
     *parts, code, thl = call(
         functools.partial(first_kernel, rows=rows),
-        [HBM, HBM],
+        [HBM] * 3,
         [block_out] * 3 + [((cap,), jnp.int32), ((cap, 2 * T, T), BF16)],
-        [tbuf, panel, phl, acc, sems, pltpu.SemaphoreType.DMA],
-        2,
+        [pltpu.SMEM((2, cap), jnp.int32), tbuf, panel, phl, acc, sems, pltpu.SemaphoreType.DMA, pltpu.SemaphoreType.DMA],
+        1,
         [VMEM] * 3 + [SMEM, VMEM],
         L1,
-    )(in_space(coords.T, pltpu.HBM), live, in_space(tiles, pltpu.HBM), in_space(sketch.T, pltpu.HBM))
+    )(live, in_space(coords.T, pltpu.HBM), in_space(tiles, pltpu.HBM), in_space(sketch.T, pltpu.HBM))
     whole = exchange(parts)
     *parts, gram = call(
         middle_kernel,

time: 172 us -> 171 us (level)
  no operation moved by 1% of the time
where the time goes in v9:
time: 171 us
  blocking collectives  92.8 us (54%)
  starting transfers between devices  46.3 us (27%)
  waiting for transfers between devices  16.7 us (10%)
  Pallas kernels  13.9 us (8%)
    all_to_all x8, blocking collectives, swapped(): return lax.all_to_all(copies, axes, split_axis=0, concat_axis=0, tiled=True)  92.8 us
    ppermute x4, starting transfers between devices, over_pairs(): got_outer = lax.ppermute(to_outer, ROWS, outer)  31.9 us
    ppermute x4, waiting for transfers between devices, over_pairs(): got_outer = lax.ppermute(to_outer, ROWS, outer)  12 us
    ppermute x4, starting transfers between devices, over_pairs(): got_partner = lax.ppermute(to_partner, ROWS, partner)  7.66 us
    all_to_all x1, starting transfers between devices, swapped(): return lax.all_to_all(copies, axes, split_axis=0, concat_axis=0, tiled=True)  4.89 us
    all_to_all x1, waiting for transfers between devices, swapped(): return lax.all_to_all(copies, axes, split_axis=0, concat_axis=0, tiled=True)  3.56 us
  transfers between devices with their start and end apart: 10, of which 4 were waited for; matrix products, arithmetic and copies ran while one was open for 0% of the time, Pallas kernels for 1%

profile of v9, /device:TPU:2, one launch (start us, length us, event | category | flops | bytes accessed | tf_op | source)
XLA Modules:
  0.0 170.7 jit_solution(4932465690644821841)
XLA Ops:
  0.7 2.6 %shard_map.46 = (f32[16,64,128]{2,1,0:T(8,128)S(1)}, f32[16,64,128]{2,1,0:T(8,128)S(1)}, f32[16,64,128]{2,1,0:T(8,128)S(1)}, s32[48]{0:T(128)S(1)}, bf16[48,256,128]{2,1,0:T(8,128)(2,1)S(1)}) custom-call(s32[1]{0:T(128)S(6)} %copy.5.live, s32[2,48]{1,0:T(2,128)} %bitcast.14, f32[48,128,128]{2,1,0:T(8,128)} %tiles.3, f32[64,512]{1,0:T(8,128)} %bitcast.13), custom_call_target="tpu_custom_call" | custom-call | tf_op jit(solution)/shard_map/pallas_call | solution.py:366
  3.2 14.6 %collective-permute-start = (f32[16,64,128]{2,1,0:T(8,128)S(1)}, f32[16,64,128]{2,1,0:T(8,128)S(1)}, u32[]{:S(2)}, u32[]{:S(2)}) collective-permute-start(f32[16,64,128]{2,1,0:T(8,128)S(1)} %get-tuple-element.23), channel_id=1, source_target_pairs={{0,508},{4,8},{8,4},{12,16},{16,12},{20,24},{24,20},{28,32},{32,28... | collective-permute-start | bytes 1572872 | tf_op jit(solution)/shard_map/ppermute | solution.py:332
  17.9 1.9 %collective-permute-start.1 = (f32[16,64,128]{2,1,0:T(8,128)S(1)}, f32[16,64,128]{2,1,0:T(8,128)S(1)}, u32[]{:S(2)}, u32[]{:S(2)}) collective-permute-start(f32[16,64,128]{2,1,0:T(8,128)S(1)} %get-tuple-element.24), channel_id=1, source_target_pairs={{0,4},{4,0},{8,12},{12,8},{16,20},{20,16},{24,28},{28,24},{32,36},... | collective-permute-start | bytes 1572872 | tf_op jit(solution)/shard_map/ppermute | solution.py:333
  19.8 4.9 %collective-permute-done.outer = f32[16,64,128]{2,1,0:T(8,128)S(1)} collective-permute-done((f32[16,64,128]{2,1,0:T(8,128)S(1)}, f32[16,64,128]{2,1,0:T(8,128)S(1)}, u32[]{:S(2)}, u32[]{:S(2)}) %collective-permute-start) | collective-permute-done | bytes 524320 | tf_op jit(solution)/shard_map/ppermute | solution.py:332
  24.7 0.0 collective-permute-done.1.partner
  24.7 0.1 shard_map.47
  24.8 11.3 %all_to_all.45.parts = f32[4,256,128]{2,1,0:T(8,128)S(1)} all-to-all(f32[4,256,128]{2,1,0:T(8,128)S(1)} %shard_map.47), channel_id=1, replica_groups=mesh['y'=8,'z'=8,'c'=2,'grp'=4] {'grp'}, dimensions={0} | all-to-all | bytes 1048576 | tf_op jit(solution)/shard_map/all_to_all | solution.py:280
  36.1 10.5 %all_to_all.46 = f32[4,256,128]{2,1,0:T(8,128)S(1)} all-to-all(f32[4,256,128]{2,1,0:T(8,128)S(1)} %shard_map.48), channel_id=1, replica_groups=mesh['y'=8,'z'=8,'c'=2,'grp'=4] {'grp'}, dimensions={0} | all-to-all | bytes 1048576 | tf_op jit(solution)/shard_map/all_to_all | solution.py:280
  46.6 1.9 %collective-permute-start.3 = (f32[16,64,128]{2,1,0:T(8,128)S(1)}, f32[16,64,128]{2,1,0:T(8,128)S(1)}, u32[]{:S(2)}, u32[]{:S(2)}) collective-permute-start(f32[16,64,128]{2,1,0:T(8,128)S(1)} %bitcast.6), channel_id=1, source_target_pairs={{0,4},{4,0},{8,12},{12,8},{16,20},{20,16},{24,28},{28,24},{32,36},... | collective-permute-start | bytes 1572872 | tf_op jit(solution)/shard_map/ppermute | solution.py:333
  48.5 6.8 %collective-permute-start.2 = (f32[16,64,128]{2,1,0:T(8,128)S(1)}, f32[16,64,128]{2,1,0:T(8,128)S(1)}, u32[]{:S(2)}, u32[]{:S(2)}) collective-permute-start(f32[16,64,128]{2,1,0:T(8,128)S(1)} %bitcast.7), channel_id=1, source_target_pairs={{0,508},{4,8},{8,4},{12,16},{16,12},{20,24},{24,20},{28,32},{32,28... | collective-permute-start | bytes 1572872 | tf_op jit(solution)/shard_map/ppermute | solution.py:332
  55.3 0.0 collective-permute-done.3.s_partner
  55.3 7.0 %collective-permute-done.2.s_outer = f32[16,64,128]{2,1,0:T(8,128)S(1)} collective-permute-done((f32[16,64,128]{2,1,0:T(8,128)S(1)}, f32[16,64,128]{2,1,0:T(8,128)S(1)}, u32[]{:S(2)}, u32[]{:S(2)}) %collective-permute-start.2) | collective-permute-done | bytes 524320 | tf_op jit(solution)/shard_map/ppermute | solution.py:332
  62.3 2.5 %shard_map.49 = (f32[16,64,128]{2,1,0:T(8,128)S(1)}, f32[16,64,128]{2,1,0:T(8,128)S(1)}, f32[16,64,128]{2,1,0:T(8,128)S(1)}, f32[8,24,128]{2,1,0:T(8,128)S(1)}) custom-call(s32[48]{0:T(128)S(1)} %get-tuple-element.20.code, s32[1]{0:T(128)S(6)} %copy.5.live, bf16[48,256,128]{2,1,0:T(8,128)(2,1)S(1)} %get-tuple-element.21.thl, ...), custom_call_target="tpu_custom_call" | custom-call | tf_op jit(solution)/shard_map/pallas_call | solution.py:376
  64.8 8.6 %collective-permute-start.4 = (f32[16,64,128]{2,1,0:T(8,128)S(1)}, f32[16,64,128]{2,1,0:T(8,128)S(1)}, u32[]{:S(2)}, u32[]{:S(2)}) collective-permute-start(f32[16,64,128]{2,1,0:T(8,128)S(1)} %get-tuple-element.26), channel_id=1, source_target_pairs={{0,508},{4,8},{8,4},{12,16},{16,12},{20,24},{24,20},{28,32},{32,28... | collective-permute-start | bytes 1572872 | tf_op jit(solution)/shard_map/ppermute | solution.py:332
  73.4 1.9 %collective-permute-start.5 = (f32[16,64,128]{2,1,0:T(8,128)S(1)}, f32[16,64,128]{2,1,0:T(8,128)S(1)}, u32[]{:S(2)}, u32[]{:S(2)}) collective-permute-start(f32[16,64,128]{2,1,0:T(8,128)S(1)} %get-tuple-element.27), channel_id=1, source_target_pairs={{0,4},{4,0},{8,12},{12,8},{16,20},{20,16},{24,28},{28,24},{32,36},... | collective-permute-start | bytes 1572872 | tf_op jit(solution)/shard_map/ppermute | solution.py:333
  75.3 12.2 %all_to_all.47 = f32[8,24,128]{2,1,0:T(8,128)S(1)} all-to-all(f32[8,24,128]{2,1,0:T(8,128)S(1)} %get-tuple-element.28), channel_id=1, replica_groups=mesh['y'=8,'z'=8,'c'=2,'grp'=4] {'y'}, dimensions={0} | all-to-all | bytes 196608 | tf_op jit(solution)/shard_map/all_to_all | solution.py:280
  87.6 0.0 collective-permute-done.4
  87.6 0.0 collective-permute-done.5
  87.6 0.1 add_add_fusion
  87.8 13.0 %all_to_all.48.pieces = f32[4,280,128]{2,1,0:T(8,128)S(1)} all-to-all(f32[4,280,128]{2,1,0:T(8,128)S(1)} %pad_maximum_fusion), channel_id=1, replica_groups=mesh['y'=8,'z'=8,'c'=2,'grp'=4] {'grp'}, dimensions={0} | all-to-all | bytes 1146880 | tf_op jit(solution)/shard_map/all_to_all | solution.py:280
  100.7 0.8 shard_map.50
  101.6 4.9 %all-to-all-start.4 = ((f32[4,256,128]{2,1,0:T(8,128)}), f32[4,256,128]{2,1,0:T(8,128)S(1)}, u32[]{:S(2)}, u32[]{:S(2)}) async-start(f32[4,256,128]{2,1,0:T(8,128)} %get-tuple-element.29), calls=%async_computation.4 | async-start | bytes 1048576 | tf_op jit(solution)/shard_map/all_to_all | solution.py:280
  106.5 1.9 %collective-permute-start.6 = (f32[24,128]{1,0:T(8,128)S(1)}, f32[24,128]{1,0:T(8,128)S(1)}, u32[]{:S(2)}, u32[]{:S(2)}) collective-permute-start(f32[24,128]{1,0:T(8,128)S(1)} %get-tuple-element.30.one), channel_id=1, source_target_pairs={{0,4},{4,0},{8,12},{12,8},{16,20},{20,16},{24,28},{28,24},{32,36},... | collective-permute-start | bytes 36872 | tf_op jit(solution)/shard_map/ppermute | solution.py:359
  108.4 1.1 collective-permute-done.6.other
  109.5 3.6 %all-to-all-done.4 = f32[4,256,128]{2,1,0:T(8,128)S(1)} async-done(((f32[4,256,128]{2,1,0:T(8,128)}), f32[4,256,128]{2,1,0:T(8,128)S(1)}, u32[]{:S(2)}, u32[]{:S(2)}) %all-to-all-start.4) | async-done | bytes 524320 | tf_op jit(solution)/shard_map/all_to_all | solution.py:280
  113.1 1.9 %collective-permute-start.8 = (f32[16,64,128]{2,1,0:T(8,128)S(1)}, f32[16,64,128]{2,1,0:T(8,128)S(1)}, u32[]{:S(2)}, u32[]{:S(2)}) collective-permute-start(f32[16,64,128]{2,1,0:T(8,128)S(1)} %bitcast.9), channel_id=1, source_target_pairs={{0,4},{4,0},{8,12},{12,8},{16,20},{20,16},{24,28},{28,24},{32,36},... | collective-permute-start | bytes 1572872 | tf_op jit(solution)/shard_map/ppermute | solution.py:333
  115.0 1.9 %collective-permute-start.7 = (f32[16,64,128]{2,1,0:T(8,128)S(1)}, f32[16,64,128]{2,1,0:T(8,128)S(1)}, u32[]{:S(2)}, u32[]{:S(2)}) collective-permute-start(f32[16,64,128]{2,1,0:T(8,128)S(1)} %bitcast.10), channel_id=1, source_target_pairs={{0,508},{4,8},{8,4},{12,16},{16,12},{20,24},{24,20},{28,32},{32,28... | collective-permute-start | bytes 1572872 | tf_op jit(solution)/shard_map/ppermute | solution.py:332
  116.9 14.0 %all_to_all.49.parts = f32[8,24,128]{2,1,0:T(8,128)S(1)} all-to-all(f32[8,24,128]{2,1,0:T(8,128)S(1)} %shard_map.51), channel_id=1, replica_groups=mesh['y'=8,'z'=8,'c'=2,'grp'=4] {'z'}, dimensions={0} | all-to-all | bytes 196608 | tf_op jit(solution)/shard_map/all_to_all | solution.py:280
  130.9 2.0 %shard_map.52.linv = f32[64,64]{1,0:T(8,128)S(1)} custom-call(f32[8,24,128]{2,1,0:T(8,128)S(1)} %all_to_all.49.parts), custom_call_target="tpu_custom_call" | custom-call | tf_op jit(solution)/shard_map/pallas_call | solution.py:385
  133.0 0.0 collective-permute-done.8.s_partner
  133.0 0.0 collective-permute-done.7.s_outer
  133.0 2.9 %shard_map.53 = (f32[64,512]{1,0:T(8,128)S(1)}, f32[8,24,128]{2,1,0:T(8,128)S(1)}) custom-call(s32[48]{0:T(128)S(1)} %get-tuple-element.20.code, s32[1]{0:T(128)S(6)} %copy.5.live, f32[48,128,128]{2,1,0:T(8,128)} %tiles.3, f32[16,64,128]{2,1,0:T(8,128)S(1)} %collective-permute-done.7.s_outer, f32[16,64,128]{2,1,0:T(8,128)S(1)} %bitcast.11, ...), custom_call_target="tpu_custom_call" | custom-call | tf_op jit(solution)/shard_map/pallas_call | solution.py:386
  135.9 9.0 %all_to_all.50 = f32[8,24,128]{2,1,0:T(8,128)S(1)} all-to-all(f32[8,24,128]{2,1,0:T(8,128)S(1)} %get-tuple-element.33), channel_id=1, replica_groups=mesh['y'=8,'z'=8,'c'=2,'grp'=4] {'c','grp'}, dimensions={0} | all-to-all | bytes 196608 | tf_op jit(solution)/shard_map/all_to_all | solution.py:280
  144.9 11.7 %all_to_all.51 = f32[8,24,128]{2,1,0:T(8,128)S(1)} all-to-all(f32[8,24,128]{2,1,0:T(8,128)S(1)} %broadcast_in_dim.10), channel_id=1, replica_groups=mesh['y'=8,'z'=8,'c'=2,'grp'=4] {'z'}, dimensions={0} | all-to-all | bytes 196608 | tf_op jit(solution)/shard_map/all_to_all | solution.py:280
  156.7 11.2 %all_to_all.52.parts = f32[8,24,128]{2,1,0:T(8,128)S(1)} all-to-all(f32[8,24,128]{2,1,0:T(8,128)S(1)} %broadcast_in_dim.11), channel_id=1, replica_groups=mesh['y'=8,'z'=8,'c'=2,'grp'=4] {'y'}, dimensions={0} | all-to-all | bytes 196608 | tf_op jit(solution)/shard_map/all_to_all | solution.py:280
  167.8 2.9 %shard_map.54 = f32[64,512]{1,0:T(8,128)} custom-call(f32[8,24,128]{2,1,0:T(8,128)S(1)} %all_to_all.52.parts, f32[64,512]{1,0:T(8,128)S(1)} %get-tuple-element.34.image), custom_call_target="tpu_custom_call" | custom-call | tf_op jit(solution)/shard_map/pallas_call | solution.py:396
  (9 shorter events, 0.1 us)
Async XLA Ops:
  3.2 21.5 %collective-permute-start = (f32[16,64,128]{2,1,0:T(8,128)S(1)}, f32[16,64,128]{2,1,0:T(8,128)S(1)}, u32[]{:S(2)}, u32[]{:S(2)}) collective-permute-start(f32[16,64,128]{2,1,0:T(8,128)S(1)} %get-tuple-element.23), channel_id=1, source_target_pairs={{0,508},{4,8},{8,4},{12,16},{16,12},{20,24},{24,20},{28,32},{32,28... | collective-permute-start | bytes 1572872 | tf_op jit(solution)/shard_map/ppermute | solution.py:332
  17.9 6.9 %collective-permute-start.1 = (f32[16,64,128]{2,1,0:T(8,128)S(1)}, f32[16,64,128]{2,1,0:T(8,128)S(1)}, u32[]{:S(2)}, u32[]{:S(2)}) collective-permute-start(f32[16,64,128]{2,1,0:T(8,128)S(1)} %get-tuple-element.24), channel_id=1, source_target_pairs={{0,4},{4,0},{8,12},{12,8},{16,20},{20,16},{24,28},{28,24},{32,36},... | collective-permute-start | bytes 1572872 | tf_op jit(solution)/shard_map/ppermute | solution.py:333
  46.6 8.7 %collective-permute-start.3 = (f32[16,64,128]{2,1,0:T(8,128)S(1)}, f32[16,64,128]{2,1,0:T(8,128)S(1)}, u32[]{:S(2)}, u32[]{:S(2)}) collective-permute-start(f32[16,64,128]{2,1,0:T(8,128)S(1)} %bitcast.6), channel_id=1, source_target_pairs={{0,4},{4,0},{8,12},{12,8},{16,20},{20,16},{24,28},{28,24},{32,36},... | collective-permute-start | bytes 1572872 | tf_op jit(solution)/shard_map/ppermute | solution.py:333
  48.5 13.8 %collective-permute-start.2 = (f32[16,64,128]{2,1,0:T(8,128)S(1)}, f32[16,64,128]{2,1,0:T(8,128)S(1)}, u32[]{:S(2)}, u32[]{:S(2)}) collective-permute-start(f32[16,64,128]{2,1,0:T(8,128)S(1)} %bitcast.7), channel_id=1, source_target_pairs={{0,508},{4,8},{8,4},{12,16},{16,12},{20,24},{24,20},{28,32},{32,28... | collective-permute-start | bytes 1572872 | tf_op jit(solution)/shard_map/ppermute | solution.py:332
  64.8 22.7 %collective-permute-start.4 = (f32[16,64,128]{2,1,0:T(8,128)S(1)}, f32[16,64,128]{2,1,0:T(8,128)S(1)}, u32[]{:S(2)}, u32[]{:S(2)}) collective-permute-start(f32[16,64,128]{2,1,0:T(8,128)S(1)} %get-tuple-element.26), channel_id=1, source_target_pairs={{0,508},{4,8},{8,4},{12,16},{16,12},{20,24},{24,20},{28,32},{32,28... | collective-permute-start | bytes 1572872 | tf_op jit(solution)/shard_map/ppermute | solution.py:332
  73.4 14.2 %collective-permute-start.5 = (f32[16,64,128]{2,1,0:T(8,128)S(1)}, f32[16,64,128]{2,1,0:T(8,128)S(1)}, u32[]{:S(2)}, u32[]{:S(2)}) collective-permute-start(f32[16,64,128]{2,1,0:T(8,128)S(1)} %get-tuple-element.27), channel_id=1, source_target_pairs={{0,4},{4,0},{8,12},{12,8},{16,20},{20,16},{24,28},{28,24},{32,36},... | collective-permute-start | bytes 1572872 | tf_op jit(solution)/shard_map/ppermute | solution.py:333
  101.6 11.5 %all-to-all-start.4 = ((f32[4,256,128]{2,1,0:T(8,128)}), f32[4,256,128]{2,1,0:T(8,128)S(1)}, u32[]{:S(2)}, u32[]{:S(2)}) async-start(f32[4,256,128]{2,1,0:T(8,128)} %get-tuple-element.29), calls=%async_computation.4 | async-start | bytes 1048576 | tf_op jit(solution)/shard_map/all_to_all | solution.py:280
  106.5 3.1 %collective-permute-start.6 = (f32[24,128]{1,0:T(8,128)S(1)}, f32[24,128]{1,0:T(8,128)S(1)}, u32[]{:S(2)}, u32[]{:S(2)}) collective-permute-start(f32[24,128]{1,0:T(8,128)S(1)} %get-tuple-element.30.one), channel_id=1, source_target_pairs={{0,4},{4,0},{8,12},{12,8},{16,20},{20,16},{24,28},{28,24},{32,36},... | collective-permute-start | bytes 36872 | tf_op jit(solution)/shard_map/ppermute | solution.py:359
  113.1 19.9 %collective-permute-start.8 = (f32[16,64,128]{2,1,0:T(8,128)S(1)}, f32[16,64,128]{2,1,0:T(8,128)S(1)}, u32[]{:S(2)}, u32[]{:S(2)}) collective-permute-start(f32[16,64,128]{2,1,0:T(8,128)S(1)} %bitcast.9), channel_id=1, source_target_pairs={{0,4},{4,0},{8,12},{12,8},{16,20},{20,16},{24,28},{28,24},{32,36},... | collective-permute-start | bytes 1572872 | tf_op jit(solution)/shard_map/ppermute | solution.py:333
  115.0 18.0 %collective-permute-start.7 = (f32[16,64,128]{2,1,0:T(8,128)S(1)}, f32[16,64,128]{2,1,0:T(8,128)S(1)}, u32[]{:S(2)}, u32[]{:S(2)}) collective-permute-start(f32[16,64,128]{2,1,0:T(8,128)S(1)} %bitcast.10), channel_id=1, source_target_pairs={{0,508},{4,8},{8,4},{12,16},{16,12},{20,24},{24,20},{28,32},{32,28... | collective-permute-start | bytes 1572872 | tf_op jit(solution)/shard_map/ppermute | solution.py:332

commit v10 on v9

--- a/solution.py
+++ b/solution.py
@@ -16,6 +16,7 @@
 BF16 = jnp.bfloat16
 T = 128
 CHUNK = 8
+KEPT = 8
 L1, L2, L3 = 16 << 20, 16 << 20, 50 << 20
 VMEM_LIMIT = 50 * 1024 * 1024
 SMALL_LIMIT = 8 * 1024 * 1024
@@ -41,8 +42,8 @@
     return pltpu.make_async_copy(tiles.at[at], tbuf.at[at], sems.at[c])
 
 
-def start_tiles(live, tiles, tbuf, sems):
-    for c in range(tiles.shape[0] // CHUNK):
+def start_tiles(live, tiles, tbuf, sems, skip=0):
+    for c in range(skip // CHUNK, tiles.shape[0] // CHUNK):
 
         @pl.when(c * CHUNK < live)
         def _():
@@ -91,7 +92,7 @@
 
 
 def first_kernel(
-    live, coords_in, tiles, sketch, outer, own, partner, code, thl,
+    live, coords_in, tiles, sketch, outer, own, partner, code, kept, thl,
     coords, tbuf, panel, phl, acc, sems, panel_sem, coords_sem, *, rows
 ):
     cap = tiles.shape[0]
@@ -110,8 +111,9 @@
 
     def work(s):
         hi, lo = halves(tbuf[s])
-        thl[s, :T, :] = hi
-        thl[s, T:, :] = lo
+        here, at = (kept, s) if s < KEPT else (thl, s - KEPT)
+        here[at, :T, :] = hi
+        here[at, T:, :] = lo
         spread_slot(code[s], hi, lo, phl, acc)
 
     each_chunk(live[0], cap, work, lambda c: tile_copy(c, tiles, tbuf, sems).wait())
@@ -154,17 +156,25 @@
 
 
 def middle_kernel(
-    code, live, thl, s_outer, s_own, s_partner, outer, own, partner, gram, shl, img, phl, acc
+    code, live, kept, thl, s_outer, s_own, s_partner, outer, own, partner, gram, shl, img, phl, acc
 ):
-    cap = thl.shape[0]
+    cap = kept.shape[0] + thl.shape[0]
     k = s_own.shape[1]
+
+    def split(s):
+        return kept[s] if s < KEPT else thl[s - KEPT]
+
+    def back(s):
+        hl = split(s)
+        spread_slot(code[s], hl[:T], hl[T:], phl, acc)
+
     keep_spread((s_outer, s_own, s_partner), shl)
     img[...] = jnp.zeros_like(img)
     acc[...] = jnp.zeros_like(acc)
-    each_chunk(live[0], cap, lambda s: image_slot(code[s], thl[s], shl, img))
+    each_chunk(live[0], cap, lambda s: image_slot(code[s], split(s), shl, img))
     put_gram(whole_image(img), gram)
     keep_panel(lambda t: img[t], k, phl)
-    each_chunk(live[0], cap, lambda s: spread_slot(code[s], thl[s, :T, :], thl[s, T:, :], phl, acc))
+    each_chunk(live[0], cap, back)
     put_spread(acc, (outer, own, partner))
 
 
@@ -256,16 +266,20 @@
     linv[...] = inverse_factor(summed_gram(parts, linv.shape[0]))
 
 
-def last_kernel(code, live, tiles, s_outer, s_own, s_partner, linv, image, gram, tbuf, shl, img, sems):
-    start_tiles(live[0], tiles, tbuf, sems)
+def last_kernel(code, live, tiles, kept, s_outer, s_own, s_partner, linv, image, gram, tbuf, shl, img, sems):
+    start_tiles(live[0], tiles, tbuf, sems, KEPT)
     keep_spread((s_outer, s_own, s_partner), shl)
     img[...] = jnp.zeros_like(img)
-    each_chunk(
-        live[0],
-        tiles.shape[0],
-        lambda s: image_slot(code[s], jnp.concatenate(halves(tbuf[s]), axis=0), shl, img),
-        lambda c: tile_copy(c, tiles, tbuf, sems).wait(),
-    )
+
+    def ready(c):
+        if c * CHUNK >= KEPT:
+            tile_copy(c, tiles, tbuf, sems).wait()
+
+    def work(s):
+        hl = kept[s] if s < KEPT else jnp.concatenate(halves(tbuf[s]), axis=0)
+        image_slot(code[s], hl, shl, img)
+
+    each_chunk(live[0], tiles.shape[0], work, ready)
     x = dot(linv[...], whole_image(img), (1, 0), HIGHEST)
     image[...] = x
     put_gram(x, gram)
@@ -363,34 +377,34 @@
         at_outer, at_partner = over_pairs(own, own)
         return (at_outer, own, at_partner), gram
 
-    *parts, code, thl = call(
+    *parts, code, kept, thl = call(
         functools.partial(first_kernel, rows=rows),
         [HBM] * 3,
-        [block_out] * 3 + [((cap,), jnp.int32), ((cap, 2 * T, T), BF16)],
+        [block_out] * 3 + [((cap,), jnp.int32), ((KEPT, 2 * T, T), BF16), ((cap - KEPT, 2 * T, T), BF16)],
         [pltpu.SMEM((2, cap), jnp.int32), tbuf, panel, phl, acc, sems, pltpu.SemaphoreType.DMA, pltpu.SemaphoreType.DMA],
         1,
-        [VMEM] * 3 + [SMEM, VMEM],
+        [VMEM] * 3 + [SMEM, VMEM, VMEM],
         L1,
     )(live, in_space(coords.T, pltpu.HBM), in_space(tiles, pltpu.HBM), in_space(sketch.T, pltpu.HBM))
     whole = exchange(parts)
     *parts, gram = call(
         middle_kernel,
-        [VMEM] * 4,
+        [VMEM] * 5,
         [block_out] * 3 + [((lax.axis_size("y"), *packed), F32)],
         [shl, img, phl, acc],
         2,
         limit=L2,
-    )(code, live, thl, *whole)
+    )(code, live, kept, thl, *whole)
     whole, gram = exchange_with_gram(parts, gram)
     linv = call(factor_kernel, [VMEM], [((k, k), F32)], limit=SMALL_LIMIT)(gram)[0]
     image, gram = call(
         last_kernel,
-        [HBM] + [VMEM] * 4,
+        [HBM] + [VMEM] * 5,
         [((k, mine * T), F32), ((2 * groups, *packed), F32)],
         [tbuf, shl, img, sems],
         2,
         limit=L3,
-    )(code, live, tiles, *whole, linv)
+    )(code, live, tiles, kept, *whole, linv)
     gram = to_everyone(swapped(gram, ("c", "grp")).sum(axis=0), "z").sum(axis=0)
     scale = float(rows * groups * sketch.shape[0]) ** 0.5
     return call(

time: 171 us -> 171 us (level)
  no operation moved by 1% of the time
where the time goes in v10:
time: 171 us; the launch traced here: 170 us
  blocking collectives  92.8 us (54%)
  starting transfers between devices  46.4 us (27%)
  waiting for transfers between devices  16.6 us (10%)
  Pallas kernels  13.5 us (8%)
    all_to_all x8, blocking collectives, swapped(): return lax.all_to_all(copies, axes, split_axis=0, concat_axis=0, tiled=True)  92.8 us
    ppermute x4, starting transfers between devices, over_pairs(): got_outer = lax.ppermute(to_outer, ROWS, outer)  31.9 us
    ppermute x4, waiting for transfers between devices, over_pairs(): got_outer = lax.ppermute(to_outer, ROWS, outer)  11.9 us
    ppermute x4, starting transfers between devices, over_pairs(): got_partner = lax.ppermute(to_partner, ROWS, partner)  7.66 us
    all_to_all x1, starting transfers between devices, swapped(): return lax.all_to_all(copies, axes, split_axis=0, concat_axis=0, tiled=True)  4.89 us
    all_to_all x1, waiting for transfers between devices, swapped(): return lax.all_to_all(copies, axes, split_axis=0, concat_axis=0, tiled=True)  3.56 us
  transfers between devices with their start and end apart: 10, of which 4 were waited for; matrix products, arithmetic and copies ran while one was open for 0% of the time, Pallas kernels for 1%

profile of v10, /device:TPU:2, one launch (start us, length us, event | category | flops | bytes accessed | tf_op | source)
XLA Modules:
  0.0 170.4 jit_solution(12593422277659438889)
XLA Ops:
  0.7 2.6 %shard_map.46 = (f32[16,64,128]{2,1,0:T(8,128)S(1)}, f32[16,64,128]{2,1,0:T(8,128)S(1)}, f32[16,64,128]{2,1,0:T(8,128)S(1)}, s32[48]{0:T(128)S(1)}, bf16[8,256,1...) custom-call(s32[1]{0:T(128)S(6)} %copy.5.live, s32[2,48]{1,0:T(2,128)} %bitcast.14, f32[48,128,128]{2,1,0:T(8,128)} %tiles.3, ...), custom_call_target="tpu_custom_call" | custom-call | tf_op jit(solution)/shard_map/pallas_call | solution.py:380
  3.2 14.6 %collective-permute-start = (f32[16,64,128]{2,1,0:T(8,128)S(1)}, f32[16,64,128]{2,1,0:T(8,128)S(1)}, u32[]{:S(2)}, u32[]{:S(2)}) collective-permute-start(f32[16,64,128]{2,1,0:T(8,128)S(1)} %get-tuple-element.25), channel_id=1, source_target_pairs={{0,508},{4,8},{8,4},{12,16},{16,12},{20,24},{24,20},{28,32},{32,28... | collective-permute-start | bytes 1572872 | tf_op jit(solution)/shard_map/ppermute | solution.py:346
  17.9 1.9 %collective-permute-start.1 = (f32[16,64,128]{2,1,0:T(8,128)S(1)}, f32[16,64,128]{2,1,0:T(8,128)S(1)}, u32[]{:S(2)}, u32[]{:S(2)}) collective-permute-start(f32[16,64,128]{2,1,0:T(8,128)S(1)} %get-tuple-element.26), channel_id=1, source_target_pairs={{0,4},{4,0},{8,12},{12,8},{16,20},{20,16},{24,28},{28,24},{32,36},... | collective-permute-start | bytes 1572872 | tf_op jit(solution)/shard_map/ppermute | solution.py:347
  19.8 4.9 %collective-permute-done.outer = f32[16,64,128]{2,1,0:T(8,128)S(1)} collective-permute-done((f32[16,64,128]{2,1,0:T(8,128)S(1)}, f32[16,64,128]{2,1,0:T(8,128)S(1)}, u32[]{:S(2)}, u32[]{:S(2)}) %collective-permute-start) | collective-permute-done | bytes 524320 | tf_op jit(solution)/shard_map/ppermute | solution.py:346
  24.7 0.0 collective-permute-done.1.partner
  24.7 0.1 shard_map.47
  24.8 11.3 %all_to_all.45.parts = f32[4,256,128]{2,1,0:T(8,128)S(1)} all-to-all(f32[4,256,128]{2,1,0:T(8,128)S(1)} %shard_map.47), channel_id=1, replica_groups=mesh['y'=8,'z'=8,'c'=2,'grp'=4] {'grp'}, dimensions={0} | all-to-all | bytes 1048576 | tf_op jit(solution)/shard_map/all_to_all | solution.py:294
  36.1 10.5 %all_to_all.46 = f32[4,256,128]{2,1,0:T(8,128)S(1)} all-to-all(f32[4,256,128]{2,1,0:T(8,128)S(1)} %shard_map.48), channel_id=1, replica_groups=mesh['y'=8,'z'=8,'c'=2,'grp'=4] {'grp'}, dimensions={0} | all-to-all | bytes 1048576 | tf_op jit(solution)/shard_map/all_to_all | solution.py:294
  46.6 1.9 %collective-permute-start.3 = (f32[16,64,128]{2,1,0:T(8,128)S(1)}, f32[16,64,128]{2,1,0:T(8,128)S(1)}, u32[]{:S(2)}, u32[]{:S(2)}) collective-permute-start(f32[16,64,128]{2,1,0:T(8,128)S(1)} %bitcast.9), channel_id=1, source_target_pairs={{0,4},{4,0},{8,12},{12,8},{16,20},{20,16},{24,28},{28,24},{32,36},... | collective-permute-start | bytes 1572872 | tf_op jit(solution)/shard_map/ppermute | solution.py:347
  48.5 6.8 %collective-permute-start.2 = (f32[16,64,128]{2,1,0:T(8,128)S(1)}, f32[16,64,128]{2,1,0:T(8,128)S(1)}, u32[]{:S(2)}, u32[]{:S(2)}) collective-permute-start(f32[16,64,128]{2,1,0:T(8,128)S(1)} %bitcast.10), channel_id=1, source_target_pairs={{0,508},{4,8},{8,4},{12,16},{16,12},{20,24},{24,20},{28,32},{32,28... | collective-permute-start | bytes 1572872 | tf_op jit(solution)/shard_map/ppermute | solution.py:346
  55.3 0.0 collective-permute-done.3.s_partner
  55.3 7.0 %collective-permute-done.2.s_outer = f32[16,64,128]{2,1,0:T(8,128)S(1)} collective-permute-done((f32[16,64,128]{2,1,0:T(8,128)S(1)}, f32[16,64,128]{2,1,0:T(8,128)S(1)}, u32[]{:S(2)}, u32[]{:S(2)}) %collective-permute-start.2) | collective-permute-done | bytes 524320 | tf_op jit(solution)/shard_map/ppermute | solution.py:346
  62.3 2.5 %shard_map.49 = (f32[16,64,128]{2,1,0:T(8,128)S(1)}, f32[16,64,128]{2,1,0:T(8,128)S(1)}, f32[16,64,128]{2,1,0:T(8,128)S(1)}, f32[8,24,128]{2,1,0:T(8,128)S(1)}) custom-call(s32[48]{0:T(128)S(1)} %get-tuple-element.21.code, s32[1]{0:T(128)S(6)} %copy.5.live, bf16[8,256,128]{2,1,0:T(8,128)(2,1)S(1)} %get-tuple-element.22.kept, ...), custom_call_target="tpu_custom_call" | custom-call | tf_op jit(solution)/shard_map/pallas_call | solution.py:390
  64.8 8.6 %collective-permute-start.4 = (f32[16,64,128]{2,1,0:T(8,128)S(1)}, f32[16,64,128]{2,1,0:T(8,128)S(1)}, u32[]{:S(2)}, u32[]{:S(2)}) collective-permute-start(f32[16,64,128]{2,1,0:T(8,128)S(1)} %get-tuple-element.28), channel_id=1, source_target_pairs={{0,508},{4,8},{8,4},{12,16},{16,12},{20,24},{24,20},{28,32},{32,28... | collective-permute-start | bytes 1572872 | tf_op jit(solution)/shard_map/ppermute | solution.py:346
  73.4 1.9 %collective-permute-start.5 = (f32[16,64,128]{2,1,0:T(8,128)S(1)}, f32[16,64,128]{2,1,0:T(8,128)S(1)}, u32[]{:S(2)}, u32[]{:S(2)}) collective-permute-start(f32[16,64,128]{2,1,0:T(8,128)S(1)} %get-tuple-element.29), channel_id=1, source_target_pairs={{0,4},{4,0},{8,12},{12,8},{16,20},{20,16},{24,28},{28,24},{32,36},... | collective-permute-start | bytes 1572872 | tf_op jit(solution)/shard_map/ppermute | solution.py:347
  75.3 12.2 %all_to_all.47 = f32[8,24,128]{2,1,0:T(8,128)S(1)} all-to-all(f32[8,24,128]{2,1,0:T(8,128)S(1)} %get-tuple-element.30), channel_id=1, replica_groups=mesh['y'=8,'z'=8,'c'=2,'grp'=4] {'y'}, dimensions={0} | all-to-all | bytes 196608 | tf_op jit(solution)/shard_map/all_to_all | solution.py:294
  87.6 0.0 collective-permute-done.4
  87.6 0.0 collective-permute-done.5
  87.6 0.1 add_add_fusion
  87.8 13.0 %all_to_all.48.pieces = f32[4,280,128]{2,1,0:T(8,128)S(1)} all-to-all(f32[4,280,128]{2,1,0:T(8,128)S(1)} %pad_maximum_fusion), channel_id=1, replica_groups=mesh['y'=8,'z'=8,'c'=2,'grp'=4] {'grp'}, dimensions={0} | all-to-all | bytes 1146880 | tf_op jit(solution)/shard_map/all_to_all | solution.py:294
  100.7 0.8 shard_map.50
  101.6 4.9 %all-to-all-start.4 = ((f32[4,256,128]{2,1,0:T(8,128)}), f32[4,256,128]{2,1,0:T(8,128)S(1)}, u32[]{:S(2)}, u32[]{:S(2)}) async-start(f32[4,256,128]{2,1,0:T(8,128)} %get-tuple-element.31), calls=%async_computation.4 | async-start | bytes 1048576 | tf_op jit(solution)/shard_map/all_to_all | solution.py:294
  106.5 1.9 %collective-permute-start.6 = (f32[24,128]{1,0:T(8,128)S(1)}, f32[24,128]{1,0:T(8,128)S(1)}, u32[]{:S(2)}, u32[]{:S(2)}) collective-permute-start(f32[24,128]{1,0:T(8,128)S(1)} %get-tuple-element.32.one), channel_id=1, source_target_pairs={{0,4},{4,0},{8,12},{12,8},{16,20},{20,16},{24,28},{28,24},{32,36},... | collective-permute-start | bytes 36872 | tf_op jit(solution)/shard_map/ppermute | solution.py:373
  108.4 1.1 collective-permute-done.6.other
  109.5 3.6 %all-to-all-done.4 = f32[4,256,128]{2,1,0:T(8,128)S(1)} async-done(((f32[4,256,128]{2,1,0:T(8,128)}), f32[4,256,128]{2,1,0:T(8,128)S(1)}, u32[]{:S(2)}, u32[]{:S(2)}) %all-to-all-start.4) | async-done | bytes 524320 | tf_op jit(solution)/shard_map/all_to_all | solution.py:294
  113.1 1.9 %collective-permute-start.8 = (f32[16,64,128]{2,1,0:T(8,128)S(1)}, f32[16,64,128]{2,1,0:T(8,128)S(1)}, u32[]{:S(2)}, u32[]{:S(2)}) collective-permute-start(f32[16,64,128]{2,1,0:T(8,128)S(1)} %bitcast.6), channel_id=1, source_target_pairs={{0,4},{4,0},{8,12},{12,8},{16,20},{20,16},{24,28},{28,24},{32,36},... | collective-permute-start | bytes 1572872 | tf_op jit(solution)/shard_map/ppermute | solution.py:347
  115.0 1.9 %collective-permute-start.7 = (f32[16,64,128]{2,1,0:T(8,128)S(1)}, f32[16,64,128]{2,1,0:T(8,128)S(1)}, u32[]{:S(2)}, u32[]{:S(2)}) collective-permute-start(f32[16,64,128]{2,1,0:T(8,128)S(1)} %bitcast.7), channel_id=1, source_target_pairs={{0,508},{4,8},{8,4},{12,16},{16,12},{20,24},{24,20},{28,32},{32,28... | collective-permute-start | bytes 1572872 | tf_op jit(solution)/shard_map/ppermute | solution.py:346
  116.9 14.0 %all_to_all.49.parts = f32[8,24,128]{2,1,0:T(8,128)S(1)} all-to-all(f32[8,24,128]{2,1,0:T(8,128)S(1)} %shard_map.51), channel_id=1, replica_groups=mesh['y'=8,'z'=8,'c'=2,'grp'=4] {'z'}, dimensions={0} | all-to-all | bytes 196608 | tf_op jit(solution)/shard_map/all_to_all | solution.py:294
  130.9 2.0 %shard_map.52.linv = f32[64,64]{1,0:T(8,128)S(1)} custom-call(f32[8,24,128]{2,1,0:T(8,128)S(1)} %all_to_all.49.parts), custom_call_target="tpu_custom_call" | custom-call | tf_op jit(solution)/shard_map/pallas_call | solution.py:399
  133.0 0.0 collective-permute-done.8.s_partner
  133.0 0.0 collective-permute-done.7.s_outer
  133.0 2.6 %shard_map.53 = (f32[64,512]{1,0:T(8,128)S(1)}, f32[8,24,128]{2,1,0:T(8,128)S(1)}) custom-call(s32[48]{0:T(128)S(1)} %get-tuple-element.21.code, s32[1]{0:T(128)S(6)} %copy.5.live, f32[48,128,128]{2,1,0:T(8,128)} %tiles.3, bf16[8,256,128]{2,1,0:T(8,128)(2,1)S(1)} %get-tuple-element.22.kept, f32[16,64,128]{2,1,0:T(8,128)S(1)} %collective-permute-done.7.s_outer, ...), custom_call_target="tpu_custom_call" | custom-call | tf_op jit(solution)/shard_map/pallas_call | solution.py:400
  135.6 9.0 %all_to_all.50 = f32[8,24,128]{2,1,0:T(8,128)S(1)} all-to-all(f32[8,24,128]{2,1,0:T(8,128)S(1)} %get-tuple-element.35), channel_id=1, replica_groups=mesh['y'=8,'z'=8,'c'=2,'grp'=4] {'c','grp'}, dimensions={0} | all-to-all | bytes 196608 | tf_op jit(solution)/shard_map/all_to_all | solution.py:294
  144.6 11.7 %all_to_all.51 = f32[8,24,128]{2,1,0:T(8,128)S(1)} all-to-all(f32[8,24,128]{2,1,0:T(8,128)S(1)} %broadcast_in_dim.10), channel_id=1, replica_groups=mesh['y'=8,'z'=8,'c'=2,'grp'=4] {'z'}, dimensions={0} | all-to-all | bytes 196608 | tf_op jit(solution)/shard_map/all_to_all | solution.py:294
  156.3 11.1 %all_to_all.52.parts = f32[8,24,128]{2,1,0:T(8,128)S(1)} all-to-all(f32[8,24,128]{2,1,0:T(8,128)S(1)} %broadcast_in_dim.11), channel_id=1, replica_groups=mesh['y'=8,'z'=8,'c'=2,'grp'=4] {'y'}, dimensions={0} | all-to-all | bytes 196608 | tf_op jit(solution)/shard_map/all_to_all | solution.py:294
  167.5 2.9 %shard_map.54 = f32[64,512]{1,0:T(8,128)} custom-call(f32[8,24,128]{2,1,0:T(8,128)S(1)} %all_to_all.52.parts, f32[64,512]{1,0:T(8,128)S(1)} %get-tuple-element.36.image), custom_call_target="tpu_custom_call" | custom-call | tf_op jit(solution)/shard_map/pallas_call | solution.py:410
  (9 shorter events, 0.1 us)
Async XLA Ops:
  3.2 21.5 %collective-permute-start = (f32[16,64,128]{2,1,0:T(8,128)S(1)}, f32[16,64,128]{2,1,0:T(8,128)S(1)}, u32[]{:S(2)}, u32[]{:S(2)}) collective-permute-start(f32[16,64,128]{2,1,0:T(8,128)S(1)} %get-tuple-element.25), channel_id=1, source_target_pairs={{0,508},{4,8},{8,4},{12,16},{16,12},{20,24},{24,20},{28,32},{32,28... | collective-permute-start | bytes 1572872 | tf_op jit(solution)/shard_map/ppermute | solution.py:346
  17.9 6.9 %collective-permute-start.1 = (f32[16,64,128]{2,1,0:T(8,128)S(1)}, f32[16,64,128]{2,1,0:T(8,128)S(1)}, u32[]{:S(2)}, u32[]{:S(2)}) collective-permute-start(f32[16,64,128]{2,1,0:T(8,128)S(1)} %get-tuple-element.26), channel_id=1, source_target_pairs={{0,4},{4,0},{8,12},{12,8},{16,20},{20,16},{24,28},{28,24},{32,36},... | collective-permute-start | bytes 1572872 | tf_op jit(solution)/shard_map/ppermute | solution.py:347
  46.6 8.7 %collective-permute-start.3 = (f32[16,64,128]{2,1,0:T(8,128)S(1)}, f32[16,64,128]{2,1,0:T(8,128)S(1)}, u32[]{:S(2)}, u32[]{:S(2)}) collective-permute-start(f32[16,64,128]{2,1,0:T(8,128)S(1)} %bitcast.9), channel_id=1, source_target_pairs={{0,4},{4,0},{8,12},{12,8},{16,20},{20,16},{24,28},{28,24},{32,36},... | collective-permute-start | bytes 1572872 | tf_op jit(solution)/shard_map/ppermute | solution.py:347
  48.5 13.8 %collective-permute-start.2 = (f32[16,64,128]{2,1,0:T(8,128)S(1)}, f32[16,64,128]{2,1,0:T(8,128)S(1)}, u32[]{:S(2)}, u32[]{:S(2)}) collective-permute-start(f32[16,64,128]{2,1,0:T(8,128)S(1)} %bitcast.10), channel_id=1, source_target_pairs={{0,508},{4,8},{8,4},{12,16},{16,12},{20,24},{24,20},{28,32},{32,28... | collective-permute-start | bytes 1572872 | tf_op jit(solution)/shard_map/ppermute | solution.py:346
  64.8 22.8 %collective-permute-start.4 = (f32[16,64,128]{2,1,0:T(8,128)S(1)}, f32[16,64,128]{2,1,0:T(8,128)S(1)}, u32[]{:S(2)}, u32[]{:S(2)}) collective-permute-start(f32[16,64,128]{2,1,0:T(8,128)S(1)} %get-tuple-element.28), channel_id=1, source_target_pairs={{0,508},{4,8},{8,4},{12,16},{16,12},{20,24},{24,20},{28,32},{32,28... | collective-permute-start | bytes 1572872 | tf_op jit(solution)/shard_map/ppermute | solution.py:346
  73.4 14.2 %collective-permute-start.5 = (f32[16,64,128]{2,1,0:T(8,128)S(1)}, f32[16,64,128]{2,1,0:T(8,128)S(1)}, u32[]{:S(2)}, u32[]{:S(2)}) collective-permute-start(f32[16,64,128]{2,1,0:T(8,128)S(1)} %get-tuple-element.29), channel_id=1, source_target_pairs={{0,4},{4,0},{8,12},{12,8},{16,20},{20,16},{24,28},{28,24},{32,36},... | collective-permute-start | bytes 1572872 | tf_op jit(solution)/shard_map/ppermute | solution.py:347
  101.6 11.5 %all-to-all-start.4 = ((f32[4,256,128]{2,1,0:T(8,128)}), f32[4,256,128]{2,1,0:T(8,128)S(1)}, u32[]{:S(2)}, u32[]{:S(2)}) async-start(f32[4,256,128]{2,1,0:T(8,128)} %get-tuple-element.31), calls=%async_computation.4 | async-start | bytes 1048576 | tf_op jit(solution)/shard_map/all_to_all | solution.py:294
  106.5 3.1 %collective-permute-start.6 = (f32[24,128]{1,0:T(8,128)S(1)}, f32[24,128]{1,0:T(8,128)S(1)}, u32[]{:S(2)}, u32[]{:S(2)}) collective-permute-start(f32[24,128]{1,0:T(8,128)S(1)} %get-tuple-element.32.one), channel_id=1, source_target_pairs={{0,4},{4,0},{8,12},{12,8},{16,20},{20,16},{24,28},{28,24},{32,36},... | collective-permute-start | bytes 36872 | tf_op jit(solution)/shard_map/ppermute | solution.py:373
  113.1 19.9 %collective-permute-start.8 = (f32[16,64,128]{2,1,0:T(8,128)S(1)}, f32[16,64,128]{2,1,0:T(8,128)S(1)}, u32[]{:S(2)}, u32[]{:S(2)}) collective-permute-start(f32[16,64,128]{2,1,0:T(8,128)S(1)} %bitcast.6), channel_id=1, source_target_pairs={{0,4},{4,0},{8,12},{12,8},{16,20},{20,16},{24,28},{28,24},{32,36},... | collective-permute-start | bytes 1572872 | tf_op jit(solution)/shard_map/ppermute | solution.py:347
  115.0 18.0 %collective-permute-start.7 = (f32[16,64,128]{2,1,0:T(8,128)S(1)}, f32[16,64,128]{2,1,0:T(8,128)S(1)}, u32[]{:S(2)}, u32[]{:S(2)}) collective-permute-start(f32[16,64,128]{2,1,0:T(8,128)S(1)} %bitcast.7), channel_id=1, source_target_pairs={{0,508},{4,8},{8,4},{12,16},{16,12},{20,24},{24,20},{28,32},{32,28... | collective-permute-start | bytes 1572872 | tf_op jit(solution)/shard_map/ppermute | solution.py:346
